TPU v7x, 32 devices: a whole 2x2x4 slice. The times are simulated.
32 devices in a mesh: dp: 8 (over z, y), tm: 4 (over x, core).
Axes of the slice: x: 2, y: 2, z: 4, core: 2. Of those that a mesh axis runs over, the one named last changes fastest.
Arguments:
- mel: float32 [16, 1024, 80], P('dp', 'tm'), may hold values from -6 to 6
- cotangent: float32 [16, 1024, 80], P('dp', 'tm'), may hold values from -6 to 6
- lengths: int32 [16], P('dp'), may hold values from 1 to 1024, 9830 in all
- w_first: float32 [5, 80, 512], replicated, may hold values from -0.3125 to 0.3125
- w_mid: float32 [3, 5, 512, 512], replicated, may hold values from -0.125 to 0.125
- w_last: float32 [5, 512, 80], replicated, may hold values from -0.125 to 0.125
- gain_hidden: float32 [4, 512], replicated, may hold values from 0.5 to 1.5
- bias_hidden: float32 [4, 512], replicated, may hold values from -3 to 3
- gain_last: float32 [80], replicated, may hold values from 0.5 to 1.5
- bias_last: float32 [80], replicated, may hold values from -3 to 3
Outputs:
- mel_after: float32 [16, 1024, 80], P('dp', 'tm')
- grad_mel: float32 [16, 1024, 80], P('dp', 'tm')
- grad_w_first: float32 [5, 80, 512], replicated
- grad_w_mid: float32 [3, 5, 512, 512], replicated
- grad_w_last: float32 [5, 512, 80], replicated
- grad_gain_hidden: float32 [4, 512], replicated
- grad_bias_hidden: float32 [4, 512], replicated
- grad_gain_last: float32 [80], replicated
- grad_bias_last: float32 [80], replicated
Inputs may be any that keep to these rules, and one draw needn't show every extreme that they name: `lengths`: each utterance has at least one frame; in every draw some utterance fills all 1024 frame slots.
All inputs are finite; a program needn't handle non-finite values. No bound on the sum of `lengths` on one device may be relied on, other than what follows from the above.
Results may differ from a plain program's by a relative error of at most 0.00029.
Values sent between devices are 32-bit elements; how exact they have to be, the bound alone decides.
No kernel may reach another device: no remote copies, remote signals or barrier semaphores. Data moves between devices by JAX's collectives and lax.ppermute only.
A program may use at most 192 MiB of HBM per device.

v0:
```python
import jax
import jax.numpy as jnp
from jax import lax
from jax.sharding import PartitionSpec as P


def with_halo(block, sides, width):
    for axis, dim in sides:
        count = lax.axis_size(axis)
        forward = [(i, i + 1) for i in range(count - 1)]
        backward = [(target, source) for source, target in forward]
        low = lax.ppermute(
            lax.slice_in_dim(block, block.shape[dim] - width, None, axis=dim), axis, forward
        )
        high = lax.ppermute(lax.slice_in_dim(block, 0, width, axis=dim), axis, backward)
        block = jnp.concatenate([low, block, high], axis=dim)
    return block


def shards(
    mel, cotangent, lengths, w_first, w_mid, w_last, gain_hidden, bias_hidden, gain_last, bias_last
):
    frames = mel.shape[1]
    position = lax.axis_index("tm") * frames + jnp.arange(frames, dtype=jnp.int32)
    mask = (position[None, :] < lengths[:, None]).astype(jnp.float32)[:, :, None]
    local_count = jnp.sum(mask)
    weights = [w_first, w_mid[0], w_mid[1], w_mid[2], w_last]
    gains = [gain_hidden[0], gain_hidden[1], gain_hidden[2], gain_hidden[3], gain_last]
    shifts = [bias_hidden[0], bias_hidden[1], bias_hidden[2], bias_hidden[3], bias_last]
    width = w_first.shape[0]
    kept = []
    count = None
    x = mel
    for layer in range(5):
        padded = with_halo(x, (("tm", 1),), 2)
        weight = weights[layer]
        h = jnp.zeros(x.shape[:2] + (weight.shape[2],), jnp.float32)
        for k in range(width):
            h = h + jnp.einsum(
                "btc,cd->btd", padded[:, k : k + frames], weight[k], precision=lax.Precision.HIGHEST
            )
        first_sum, square_sum, count = lax.psum(
            (jnp.sum(mask * h, axis=(0, 1)), jnp.sum(mask * h * h, axis=(0, 1)), local_count),
            ("dp", "tm"),
        )
        mean = first_sum / count
        rstd = lax.rsqrt(square_sum / count - mean * mean + 1e-05)
        normed = (h - mean) * rstd
        z_value = normed * gains[layer] + shifts[layer]
        if layer < 4:
            active = jnp.tanh(z_value)
            x = mask * active
        else:
            active = z_value
            x = mask * z_value
        kept.append((padded, normed, rstd, active))
    mel_after = mel + x
    grad = cotangent
    weight_grads = [None] * 5
    gain_grads = [None] * 5
    shift_grads = [None] * 5
    for layer in range(4, -1, -1):
        padded, normed, rstd, active = kept[layer]
        weight = weights[layer]
        gain = gains[layer]
        gz = grad * mask
        if layer < 4:
            gz = gz * (1.0 - active * active)
        d_gain, d_shift = lax.psum(
            (jnp.sum(gz * normed, axis=(0, 1)), jnp.sum(gz, axis=(0, 1))), ("dp", "tm")
        )
        gain_grads[layer] = d_gain
        shift_grads[layer] = d_shift
        d_pre = mask * rstd * gain * (gz - d_shift / count - normed * d_gain / count)
        local_dw = jnp.stack(
            [
                jnp.einsum(
                    "btc,btd->cd", padded[:, k : k + frames], d_pre, precision=lax.Precision.HIGHEST
                )
                for k in range(width)
            ]
        )
        weight_grads[layer] = lax.psum(local_dw, ("dp", "tm"))
        d_padded = with_halo(d_pre, (("tm", 1),), 2)
        grad = jnp.zeros(padded.shape[:1] + (frames, weight.shape[1]), jnp.float32)
        for k in range(width):
            grad = grad + jnp.einsum(
                "btd,cd->btc",
                d_padded[:, 4 - k : 4 - k + frames],
                weight[k],
                precision=lax.Precision.HIGHEST,
            )
    grad_mel = cotangent + grad
    grad_w_mid = jnp.stack([weight_grads[1], weight_grads[2], weight_grads[3]])
    grad_gain_hidden = jnp.stack(gain_grads[:4])
    grad_bias_hidden = jnp.stack(shift_grads[:4])
    return (
        mel_after,
        grad_mel,
        weight_grads[0],
        grad_w_mid,
        weight_grads[4],
        grad_gain_hidden,
        grad_bias_hidden,
        gain_grads[4],
        shift_grads[4],
    )


def solution(mesh):
    return jax.shard_map(
        shards,
        mesh=mesh,
        in_specs=(
            P("dp", "tm", None),
            P("dp", "tm", None),
            P("dp"),
            P(),
            P(),
            P(),
            P(),
            P(),
            P(),
            P(),
        ),
        out_specs=(P("dp", "tm", None), P("dp", "tm", None), P(), P(), P(), P(), P(), P(), P()),
        check_vma=False,
    )
```

profile of v0, /device:TPU:0, one launch (start us, length us, event | category | flops | bytes accessed | tf_op | source)
XLA Modules:
  0.0 985.4 jit_solution(3116748570032019531)
XLA Ops:
  28.5 44.2 %all-reduce.9 = (f32[512]{0:T(512)S(1)}, f32[]{:T(128)}, f32[512]{0:T(512)S(1)}) all-reduce(f32[512]{0:T(512)S(1)} %get-tuple-element.16, f32[]{:T(128)} %fusion.254, f32[512]{0:T(512)S(1)} %get-tuple-element.15), channel_id=1, replica_groups=mesh['dp'=8,'tm'=4] {'dp','tm'}, use_global_device_ids=true, to_apply=%region_5.0 | all-reduce | flops 1025 | bytes 8200 | tf_op jit(solution)/shard_map/psum | solution.py:42
  80.5 3.1 fusion.99
  83.6 3.1 fusion.108
  86.8 3.2 fusion.26
  90.0 3.3 multiply_reduce_fusion.2
  93.3 42.1 %all-reduce.8 = (f32[512]{0:T(512)S(1)}, f32[512]{0:T(512)S(1)}) all-reduce(f32[512]{0:T(512)S(1)} %get-tuple-element.14, f32[512]{0:T(512)S(1)} %get-tuple-element.13), channel_id=1, replica_groups=mesh['dp'=8,'tm'=4] {'dp','tm'}, use_global_device_ids=true, to_apply=%region_9.0 | all-reduce | flops 1024 | bytes 8192 | tf_op jit(solution)/shard_map/psum | solution.py:42
  140.9 3.4 collective-permute-start.4
  144.4 3.1 fusion.113
  147.5 3.1 fusion.122
  150.7 3.1 fusion.24
  153.8 4.3 multiply_reduce_fusion.1
  158.1 39.8 %all-reduce.7 = (f32[512]{0:T(512)S(1)}, f32[512]{0:T(512)S(1)}) all-reduce(f32[512]{0:T(512)S(1)} %get-tuple-element.12, f32[512]{0:T(512)S(1)} %get-tuple-element.11), channel_id=1, replica_groups=mesh['dp'=8,'tm'=4] {'dp','tm'}, use_global_device_ids=true, to_apply=%region_13.0 | all-reduce | flops 1024 | bytes 8192 | tf_op jit(solution)/shard_map/psum | solution.py:42
  204.3 3.2 collective-permute-start.6
  207.6 3.1 fusion.127
  210.7 3.1 fusion.136
  213.8 3.1 fusion.22
  217.0 4.8 multiply_reduce_fusion
  221.8 40.5 %all-reduce.6 = (f32[512]{0:T(512)}, f32[512]{0:T(512)}) all-reduce(f32[512]{0:T(512)} %get-tuple-element.10, f32[512]{0:T(512)} %get-tuple-element.9), channel_id=1, replica_groups=mesh['dp'=8,'tm'=4] {'dp','tm'}, use_global_device_ids=true, to_apply=%region_17.0 | all-reduce | flops 1024 | bytes 8192 | tf_op jit(solution)/shard_map/psum | solution.py:42
  278.4 3.4 fusion.192
  281.8 41.3 %all-reduce.5 = (f32[80]{0:T(128)}, f32[80]{0:T(128)}) all-reduce(f32[80]{0:T(128)} %get-tuple-element.28, f32[80]{0:T(128)} %get-tuple-element.27), channel_id=1, replica_groups=mesh['dp'=8,'tm'=4] {'dp','tm'}, use_global_device_ids=true, to_apply=%region_19.0 | all-reduce | flops 160 | bytes 1280 | tf_op jit(solution)/shard_map/psum | solution.py:42
  326.6 40.3 %all-reduce.4 = (f32[80]{0:T(128)}, f32[80]{0:T(128)}) all-reduce(f32[80]{0:T(128)} %get-tuple-element.26, f32[80]{0:T(128)} %get-tuple-element.25), channel_id=1, replica_groups=mesh['dp'=8,'tm'=4] {'dp','tm'}, use_global_device_ids=true, to_apply=%region_25.0 | all-reduce | flops 160 | bytes 1280 | tf_op jit(solution)/shard_map/psum | solution.py:69
  374.0 3.4 collective-permute-start.11
  387.8 3.2 fusion.314
  391.0 40.6 %all-reduce.3 = (f32[512]{0:T(512)}, f32[512]{0:T(512)}) all-reduce(f32[512]{0:T(512)} %get-tuple-element.24, f32[512]{0:T(512)} %get-tuple-element.23), channel_id=1, replica_groups=mesh['dp'=8,'tm'=4] {'dp','tm'}, use_global_device_ids=true, to_apply=%region_29.0 | all-reduce | flops 1024 | bytes 8192 | tf_op jit(solution)/shard_map/psum | solution.py:69
  435.2 3.1 fusion.131
  439.7 3.2 collective-permute-start.13
  452.5 4.2 fusion.94
  456.7 3.3 fusion.96
  460.1 3.1 fusion.20
  463.3 5.1 fusion.313
  468.4 40.5 %all-reduce.2 = (f32[512]{0:T(512)}, f32[512]{0:T(512)S(1)}) all-reduce(f32[512]{0:T(512)} %get-tuple-element.22, f32[512]{0:T(512)} %get-tuple-element.21), channel_id=1, replica_groups=mesh['dp'=8,'tm'=4] {'dp','tm'}, use_global_device_ids=true, to_apply=%region_33.0 | all-reduce | flops 1024 | bytes 8192 | tf_op jit(solution)/shard_map/psum | solution.py:69
  511.9 3.1 fusion.117
  516.3 3.4 collective-permute-start.15
  533.0 3.2 fusion.90
  536.2 3.3 fusion.92
  539.5 3.2 fusion.18
  542.8 5.1 fusion.312
  547.8 40.5 %all-reduce.1 = (f32[512]{0:T(512)S(1)}, f32[512]{0:T(512)S(1)}) all-reduce(f32[512]{0:T(512)} %get-tuple-element.20, f32[512]{0:T(512)} %get-tuple-element.19), channel_id=1, replica_groups=mesh['dp'=8,'tm'=4] {'dp','tm'}, use_global_device_ids=true, to_apply=%region_37.0 | all-reduce | flops 1024 | bytes 8192 | tf_op jit(solution)/shard_map/psum | solution.py:69
  591.3 3.1 fusion.103
  595.7 3.2 collective-permute-start.17
  610.9 3.2 fusion.86
  614.1 3.4 fusion.88
  617.5 3.2 fusion.16
  620.8 5.0 fusion.311
  625.8 40.2 %all-reduce = (f32[512]{0:T(512)S(1)}, f32[512]{0:T(512)S(1)}) all-reduce(f32[512]{0:T(512)} %get-tuple-element.18, f32[512]{0:T(512)} %get-tuple-element.17), channel_id=1, replica_groups=mesh['dp'=8,'tm'=4] {'dp','tm'}, use_global_device_ids=true, to_apply=%region_41.0 | all-reduce | flops 1024 | bytes 8192 | tf_op jit(solution)/shard_map/psum | solution.py:69
  676.8 3.3 collective-permute-start.19
  687.5 277.1 %all-reduce.13.cloned.1.call-done = (f32[5,80,512]{2,1,0:T(8,128)}, f32[1,5,512,512]{3,2,1,0:T(8,128)}, f32[1,5,512,512]{3,2,1,0:T(8,128)}, f32[1,5,512,512]{3,2,1,0:T(8,128)}, f32[5,512,80]{1,2,0:T(8,128)}) async-done(((f32[5,80,512]{2,1,0:T(8,128)}, f32[1,5,512,512]{3,2,1,0:T(8,128)}, f32[1,5,512,512]{3,2,1,0:T(8,128)}, f32[1,5,512,512]{3,2,1,0:T(8,128)}, f32[5,512,80]{1,2,0:T(8,128)}), ...) | async-done | bytes 17367056 | tf_op jit(solution)/shard_map/psum | solution.py:83
  964.6 11.7 %pad_maximum_fusion = f32[3,5,512,512]{3,2,1,0:T(8,128)} fusion(f32[1,5,512,512]{3,2,1,0:T(8,128)} %get-tuple-element.51, f32[1,5,512,512]{3,2,1,0:T(8,128)} %get-tuple-element.52, f32[1,5,512,512]{3,2,1,0:T(8,128)} %get-tuple-element.53), kind=kLoop, calls=%fused_computation | loop fusion | flops 7864320 | bytes 31457280 | tf_op jit(solution)/shard_map/stack | solution.py:94
  (291 shorter events, 145.4 us)
Async XLA Ops:
  7.2 957.5 %all-reduce.13.cloned.1.call-start = ((), (), s32[]{:S(2)}) async-start(), calls=%async_computation | async-start | bytes 34734080 | tf_op jit(solution)/shard_map/psum | solution.py:83
  8.2 13.7 %collective-permute-start = (f32[2,2,80]{1,2,0:T(8,128)S(1)}, f32[2,2,80]{1,2,0:T(8,128)S(1)}, u32[]{:S(2)}, u32[]{:S(2)}) collective-permute-start(f32[2,2,80]{1,2,0:T(8,128)S(1)} %get-tuple-element.77), channel_id=1, source_target_pairs={{0,1},{1,2},{2,3},{4,5},{5,6},{6,7},{8,9},{9,10},{10,11},{12,13},{... | collective-permute-start | bytes 3848 | tf_op jit(solution)/shard_map/ppermute | solution.py:12
  10.6 9.3 collective-permute-start.1
  14.3 59.0 %copy-start.56 = (f32[1,512]{1,0:T(1,128)}, f32[1,512]{1,0:T(1,128)S(1)}, u32[]{:S(2)}) copy-start(f32[1,512]{1,0:T(1,128)S(1)} %get-tuple-element.81) | copy-start | bytes 6148
  14.3 121.6 %copy-start.58 = (f32[1,512]{1,0:T(1,128)}, f32[1,512]{1,0:T(1,128)S(1)}, u32[]{:S(2)}) copy-start(f32[1,512]{1,0:T(1,128)S(1)} %get-tuple-element.80) | copy-start | bytes 6148
  14.3 184.1 %copy-start.60 = (f32[1,512]{1,0:T(1,128)}, f32[1,512]{1,0:T(1,128)S(1)}, u32[]{:S(2)}) copy-start(f32[1,512]{1,0:T(1,128)S(1)} %get-tuple-element.82) | copy-start | bytes 6148
  15.8 57.5 %copy-start.63 = (f32[1,512]{1,0:T(1,128)}, f32[1,512]{1,0:T(1,128)S(1)}, u32[]{:S(2)}) copy-start(f32[1,512]{1,0:T(1,128)S(1)} %get-tuple-element.85) | copy-start | bytes 6148
  15.8 120.2 %copy-start.65 = (f32[1,512]{1,0:T(1,128)}, f32[1,512]{1,0:T(1,128)S(1)}, u32[]{:S(2)}) copy-start(f32[1,512]{1,0:T(1,128)S(1)} %get-tuple-element.84) | copy-start | bytes 6148
  15.8 182.7 %copy-start.67 = (f32[1,512]{1,0:T(1,128)}, f32[1,512]{1,0:T(1,128)S(1)}, u32[]{:S(2)}) copy-start(f32[1,512]{1,0:T(1,128)S(1)} %get-tuple-element.86) | copy-start | bytes 6148
  18.6 198.4 %copy-start.17 = (f32[2,256]{1,0:T(2,128)}, f32[2,256]{1,0:T(2,128)S(1)}, u32[]{:S(2)}) copy-start(f32[2,256]{1,0:T(2,128)S(1)} %compare_convert_fusion.1) | copy-start | bytes 6148
  22.0 51.6 %copy-start.15 = (f32[2,2,80]{1,2,0:T(8,128)}, f32[2,2,80]{1,2,0:T(8,128)S(1)}, u32[]{:S(2)}) copy-start(f32[2,2,80]{1,2,0:T(8,128)S(1)} %collective-permute-done) | copy-start | bytes 3844
  28.5 58.2 %copy-start.2 = (f32[2,256,512]{2,1,0:T(8,128)}, f32[2,256,512]{2,1,0:T(8,128)S(1)}, u32[]{:S(2)}) copy-start(f32[2,256,512]{2,1,0:T(8,128)S(1)} %get-tuple-element.95) | copy-start | bytes 3145732
  73.6 10.0 %collective-permute-start.2 = (f32[2,2,512]{2,1,0:T(2,128)S(1)}, f32[2,2,512]{2,1,0:T(2,128)S(1)}, u32[]{:S(2)}, u32[]{:S(2)}) collective-permute-start(f32[2,2,512]{2,1,0:T(2,128)S(1)} %get-tuple-element.71), channel_id=1, source_target_pairs={{0,1},{1,2},{2,3},{4,5},{5,6},{6,7},{8,9},{9,10},{10,11},{12,13},{... | collective-permute-start | bytes 24584 | tf_op jit(solution)/shard_map/ppermute | solution.py:12
  74.9 5.6 collective-permute-start.3
  93.3 57.4 %copy-start.4 = (f32[2,256,512]{2,1,0:T(8,128)}, f32[2,256,512]{2,1,0:T(8,128)S(1)}, u32[]{:S(2)}) copy-start(f32[2,256,512]{2,1,0:T(8,128)S(1)} %get-tuple-element.96) | copy-start | bytes 3145732
  136.6 7.8 collective-permute-start.5
  140.9 6.6 collective-permute-start.4
  200.0 7.6 collective-permute-start.7
  204.3 6.4 collective-permute-start.6
  221.8 146.5 %copy-start.8 = (f32[2,256,80]{1,2,0:T(8,128)S(1)}, f32[2,256,80]{1,2,0:T(8,128)}, u32[]{:S(2)}) copy-start(f32[2,256,80]{1,2,0:T(8,128)} %param.10) | copy-start | bytes 491524
  262.3 16.1 %copy-start.18 = (f32[2,256]{1,0:T(2,128)S(1)}, f32[2,256]{1,0:T(2,128)}, u32[]{:S(2)}) copy-start(f32[2,256]{1,0:T(2,128)} %copy-done.17) | copy-start | bytes 6148
  265.0 13.3 %copy-start = (f32[2,256,512]{2,1,0:T(8,128)}, f32[2,256,512]{2,1,0:T(8,128)S(1)}, u32[]{:S(2)}) copy-start(f32[2,256,512]{2,1,0:T(8,128)S(1)} %fusion.173) | copy-start | bytes 3145732
  265.1 9.0 collective-permute-start.8
  266.3 5.6 collective-permute-start.9
  366.9 14.7 %copy-start.1 = (f32[2,256,512]{2,1,0:T(8,128)S(1)}, f32[2,256,512]{2,1,0:T(8,128)}, u32[]{:S(2)}) copy-start(f32[2,256,512]{2,1,0:T(8,128)} %copy-done) | copy-start | bytes 3145732
  366.9 15.5 %copy-start.38 = (f32[2,2,512]{2,1,0:T(2,128)S(1)}, f32[2,2,512]{2,1,0:T(2,128)}, u32[]{:S(2)}) copy-start(f32[2,2,512]{2,1,0:T(2,128)} %copy-done.37) | copy-start | bytes 24580
  366.9 17.3 %copy-start.13 = (f32[5,512,80]{1,2,0:T(8,128)S(1)}, f32[5,512,80]{1,2,0:T(8,128)}, u32[]{:S(2)}) copy-start(f32[5,512,80]{1,2,0:T(8,128)} %param.15) | copy-start | bytes 2457604
  372.7 12.7 %collective-permute-start.10 = (f32[2,2,80]{1,2,0:T(8,128)S(1)}, f32[2,2,80]{1,2,0:T(8,128)S(1)}, u32[]{:S(2)}, u32[]{:S(2)}) collective-permute-start(f32[2,2,80]{1,2,0:T(8,128)S(1)} %get-tuple-element.75), channel_id=1, source_target_pairs={{1,0},{2,1},{3,2},{5,4},{6,5},{7,6},{9,8},{10,9},{11,10},{13,12},{... | collective-permute-start | bytes 3848 | tf_op jit(solution)/shard_map/ppermute | solution.py:15
  374.0 10.2 %collective-permute-start.11 = (f32[2,2,80]{1,2,0:T(8,128)S(1)}, f32[2,2,80]{1,2,0:T(8,128)S(1)}, u32[]{:S(2)}, u32[]{:S(2)}) collective-permute-start(f32[2,2,80]{1,2,0:T(8,128)S(1)} %get-tuple-element.76), channel_id=1, source_target_pairs={{0,1},{1,2},{2,3},{4,5},{5,6},{6,7},{8,9},{9,10},{10,11},{12,13},{... | collective-permute-start | bytes 3848 | tf_op jit(solution)/shard_map/ppermute | solution.py:12
  431.6 11.3 %copy-start.36 = (f32[2,2,512]{2,1,0:T(2,128)S(1)}, f32[2,2,512]{2,1,0:T(2,128)}, u32[]{:S(2)}) copy-start(f32[2,2,512]{2,1,0:T(2,128)} %copy-done.35) | copy-start | bytes 24580
  438.4 18.3 %collective-permute-start.12 = (f32[2,2,512]{2,1,0:T(2,128)S(1)}, f32[2,2,512]{2,1,0:T(2,128)S(1)}, u32[]{:S(2)}, u32[]{:S(2)}) collective-permute-start(f32[2,2,512]{2,1,0:T(2,128)S(1)} %get-tuple-element.63), channel_id=1, source_target_pairs={{1,0},{2,1},{3,2},{5,4},{6,5},{7,6},{9,8},{10,9},{11,10},{13,12},{... | collective-permute-start | bytes 24584 | tf_op jit(solution)/shard_map/ppermute | solution.py:15
  439.7 12.8 %collective-permute-start.13 = (f32[2,2,512]{2,1,0:T(2,128)S(1)}, f32[2,2,512]{2,1,0:T(2,128)S(1)}, u32[]{:S(2)}, u32[]{:S(2)}) collective-permute-start(f32[2,2,512]{2,1,0:T(2,128)S(1)} %get-tuple-element.64), channel_id=1, source_target_pairs={{0,1},{1,2},{2,3},{4,5},{5,6},{6,7},{8,9},{9,10},{10,11},{12,13},{... | collective-permute-start | bytes 24584 | tf_op jit(solution)/shard_map/ppermute | solution.py:12
  452.4 10.8 %copy-start.9 = (f32[5,512,512]{2,1,0:T(8,128)}, f32[5,512,512]{2,1,0:T(8,128)S(1)}, u32[]{:S(2)}) copy-start(f32[5,512,512]{2,1,0:T(8,128)S(1)} %fusion) | copy-start | bytes 15728644
  452.4 10.8 %copy-start.6 = (f32[2,256,512]{2,1,0:T(8,128)S(1)}, f32[2,256,512]{2,1,0:T(8,128)}, u32[]{:S(2)}) copy-start(f32[2,256,512]{2,1,0:T(8,128)} %get-tuple-element.97) | copy-start | bytes 3145732
  452.4 10.8 %copy-start.20 = (f32[2,256]{1,0:T(2,128)S(1)}, f32[2,256]{1,0:T(2,128)}, u32[]{:S(2)}) copy-start(f32[2,256]{1,0:T(2,128)} %copy-done.17) | copy-start | bytes 6148
  452.4 10.8 %copy-start.49 = (f32[512]{0:T(512)S(1)}, f32[512]{0:T(512)}, u32[]{:S(2)}) copy-start(f32[512]{0:T(512)} %copy-done.48) | copy-start | bytes 6148
  452.5 10.8 %copy-start.51 = (f32[512]{0:T(512)S(1)}, f32[512]{0:T(512)}, u32[]{:S(2)}) copy-start(f32[512]{0:T(512)} %copy-done.50) | copy-start | bytes 6148
  515.0 11.8 %copy-start.31 = (f32[2,2,512]{2,1,0:T(2,128)S(1)}, f32[2,2,512]{2,1,0:T(2,128)}, u32[]{:S(2)}) copy-start(f32[2,2,512]{2,1,0:T(2,128)} %copy-done.30) | copy-start | bytes 24580
  515.0 21.2 %collective-permute-start.14 = (f32[2,2,512]{2,1,0:T(2,128)S(1)}, f32[2,2,512]{2,1,0:T(2,128)S(1)}, u32[]{:S(2)}, u32[]{:S(2)}) collective-permute-start(f32[2,2,512]{2,1,0:T(2,128)S(1)} %get-tuple-element.61), channel_id=1, source_target_pairs={{1,0},{2,1},{3,2},{5,4},{6,5},{7,6},{9,8},{10,9},{11,10},{13,12},{... | collective-permute-start | bytes 24584 | tf_op jit(solution)/shard_map/ppermute | solution.py:15
  516.3 16.7 %collective-permute-start.15 = (f32[2,2,512]{2,1,0:T(2,128)S(1)}, f32[2,2,512]{2,1,0:T(2,128)S(1)}, u32[]{:S(2)}, u32[]{:S(2)}) collective-permute-start(f32[2,2,512]{2,1,0:T(2,128)S(1)} %get-tuple-element.62), channel_id=1, source_target_pairs={{0,1},{1,2},{2,3},{4,5},{5,6},{6,7},{8,9},{9,10},{10,11},{12,13},{... | collective-permute-start | bytes 24584 | tf_op jit(solution)/shard_map/ppermute | solution.py:12
  547.8 51.1 %copy-start.29 = (f32[2,2,512]{2,1,0:T(2,128)S(1)}, f32[2,2,512]{2,1,0:T(2,128)}, u32[]{:S(2)}) copy-start(f32[2,2,512]{2,1,0:T(2,128)} %copy-done.28) | copy-start | bytes 24580
  588.3 14.5 %copy-start.73 = (f32[512]{0:T(512)}, f32[512]{0:T(512)S(1)}, u32[]{:S(2)}) copy-start(f32[512]{0:T(512)S(1)} %get-tuple-element.32) | copy-start | bytes 6148
  594.4 19.7 %collective-permute-start.16 = (f32[2,2,512]{2,1,0:T(2,128)S(1)}, f32[2,2,512]{2,1,0:T(2,128)S(1)}, u32[]{:S(2)}, u32[]{:S(2)}) collective-permute-start(f32[2,2,512]{2,1,0:T(2,128)S(1)} %get-tuple-element.59), channel_id=1, source_target_pairs={{1,0},{2,1},{3,2},{5,4},{6,5},{7,6},{9,8},{10,9},{11,10},{13,12},{... | collective-permute-start | bytes 24584 | tf_op jit(solution)/shard_map/ppermute | solution.py:15
  595.7 15.2 %collective-permute-start.17 = (f32[2,2,512]{2,1,0:T(2,128)S(1)}, f32[2,2,512]{2,1,0:T(2,128)S(1)}, u32[]{:S(2)}, u32[]{:S(2)}) collective-permute-start(f32[2,2,512]{2,1,0:T(2,128)S(1)} %get-tuple-element.60), channel_id=1, source_target_pairs={{0,1},{1,2},{2,3},{4,5},{5,6},{6,7},{8,9},{9,10},{10,11},{12,13},{... | collective-permute-start | bytes 24584 | tf_op jit(solution)/shard_map/ppermute | solution.py:12
  675.3 7.8 collective-permute-start.18
  676.8 5.2 collective-permute-start.19
  964.6 11.7 %copy-start.24 = (f32[5,80,512]{2,1,0:T(8,128)S(1)}, f32[5,80,512]{2,1,0:T(8,128)}, u32[]{:S(2)}) copy-start(f32[5,80,512]{2,1,0:T(8,128)} %get-tuple-element.108) | copy-start | bytes 2457604
  964.6 12.6 %copy-start.23 = (f32[5,512,80]{1,2,0:T(8,128)S(1)}, f32[5,512,80]{1,2,0:T(8,128)}, u32[]{:S(2)}) copy-start(f32[5,512,80]{1,2,0:T(8,128)} %get-tuple-element.110) | copy-start | bytes 2457604
  (58 other events, 376.6 us)
Sparse Core Ops, SparseCore 0:
  675.4 289.1 all-reduce.12
where the time goes:
time: 994 us; the launch traced here: 985 us
  blocking collectives  410 us (41%)
  waiting for transfers between devices  280 us (28%)
  matrix products  184 us (19%)
  starting transfers between devices  41.8 us (4%)
  other arithmetic  39.6 us (4%)
  between operations  16.4 us (2%)
  local copies, waits for them, and re-layouts  13.5 us (1%)
    psum x1, waiting for transfers between devices, shards(): weight_grads[layer] = lax.psum(local_dw, ('dp', 'tm'))  277 us
    psum x5, blocking collectives, shards(): lax.psum((jnp.sum(mask * h, axis=(0, 1)), jnp.sum(mask * h * h, axis=(0,...  208 us
    psum x5, blocking collectives, shards(): lax.psum((jnp.sum(gz * normed, axis=(0, 1)), jnp.sum(gz, axis=(0, 1))), (...  202 us
    dot_general x25, matrix products, shards(): jnp.einsum('btc,cd->btd', padded[:, k:k + frames], weight[k], precision=l...  72.2 us
    dot_general x25, matrix products, shards(): jnp.einsum('btd,cd->btc', d_padded[:, 4 - k:4 - k + frames], weight[k], p...  69.9 us
    dot_general x25, matrix products, shards(): jnp.einsum('btc,btd->cd', padded[:, k:k + frames], d_pre, precision=lax.P...  42.1 us
    ppermute x10, starting transfers between devices, with_halo(): lax.ppermute(lax.slice_in_dim(block, block.shape[dim] - width, None, axis...  28.3 us
  transfers between devices with their start and end apart: 21, of which 3 were waited for; matrix products, arithmetic and copies ran while one was open for 9% of the time, Pallas kernels for 0%

commit v1 on v0

v1 whole, which is shorter than its diff:
```python
import jax
import jax.numpy as jnp
from jax import lax
from jax.sharding import PartitionSpec as P

AXES = ("dp", "tm")
EDGE = 24
HIGH = lax.Precision.HIGH


def extend(block):
    count = lax.axis_size("tm")
    forward = [(i, i + 1) for i in range(count - 1)]
    backward = [(j, i) for i, j in forward]
    low = lax.ppermute(block[:, -EDGE:], "tm", forward)
    high = lax.ppermute(block[:, :EDGE], "tm", backward)
    return jnp.concatenate([low, block, high], axis=1)


def all_sum(parts):
    devices = lax.axis_size(AXES)
    copies = jnp.broadcast_to(parts[None], (devices,) + parts.shape)
    return jnp.sum(lax.all_to_all(copies, AXES, 0, 0), axis=0)


def shifted(x, width):
    rows = x.shape[0]
    padded = jnp.pad(x, ((width // 2, width // 2), (0, 0)))
    return jnp.concatenate([padded[k : k + rows] for k in range(width)], axis=1)


def shards(
    mel, cotangent, lengths, w_first, w_mid, w_last, gain_hidden, bias_hidden, gain_last, bias_last
):
    batch, frames, mels = mel.shape
    width = w_first.shape[0]
    span = frames + 2 * EDGE
    rows = batch * span
    both = extend(jnp.concatenate([mel, cotangent], axis=2)).reshape(rows, 2 * mels)
    mel_ext, cot_ext = both[:, :mels], both[:, mels:]
    local = jnp.arange(span, dtype=jnp.int32) - EDGE
    position = lax.axis_index("tm") * frames + local
    live = (position[None, :] >= 0) & (position[None, :] < lengths[:, None])
    mask = live.astype(jnp.float32).reshape(rows, 1)
    inside = (local >= 0) & (local < frames)
    own = (live & inside[None, :]).astype(jnp.float32).reshape(rows, 1)
    local_count = jnp.sum(own)
    weights = [w_first, w_mid[0], w_mid[1], w_mid[2], w_last]
    gains = [gain_hidden[0], gain_hidden[1], gain_hidden[2], gain_hidden[3], gain_last]
    shifts = [bias_hidden[0], bias_hidden[1], bias_hidden[2], bias_hidden[3], bias_last]
    kept = []
    count = None
    x = mel_ext
    last_sums = None
    for layer in range(5):
        weight = weights[layer]
        x_wide = shifted(x, width)
        h = jnp.dot(x_wide, weight.reshape(-1, weight.shape[2]), precision=HIGH)
        masked = own * h
        sums = [jnp.sum(masked, axis=0), jnp.sum(masked * h, axis=0)]
        if layer == 0:
            sums.append(jnp.broadcast_to(local_count, sums[0].shape))
        if layer == 4:
            sums += [jnp.sum(own * cot_ext, axis=0), jnp.sum(masked * cot_ext, axis=0)]
        sums = all_sum(jnp.stack(sums))
        if layer == 0:
            count = sums[2, 0]
        mean = sums[0] / count
        rstd = lax.rsqrt(sums[1] / count - mean * mean + 1e-05)
        normed = (h - mean) * rstd
        z_value = normed * gains[layer] + shifts[layer]
        if layer < 4:
            active = jnp.tanh(z_value)
            x = mask * active
        else:
            active = None
            x = mask * z_value
            last_sums = (rstd * (sums[3] - mean * sums[2]), sums[2])
        kept.append((x_wide, normed, rstd, active))

    def unextend(block):
        return block.reshape(batch, span, mels)[:, EDGE : EDGE + frames]

    mel_after = mel + unextend(x)
    grad = cot_ext
    weight_grads = [None] * 5
    gain_grads = [None] * 5
    shift_grads = [None] * 5
    for layer in range(4, -1, -1):
        x_wide, normed, rstd, active = kept[layer]
        weight = weights[layer]
        gz = grad * mask
        if layer < 4:
            gz = gz * (1.0 - active * active)
            mine = own * gz
            sums = all_sum(jnp.stack([jnp.sum(mine * normed, axis=0), jnp.sum(mine, axis=0)]))
            d_gain, d_shift = sums[0], sums[1]
        else:
            d_gain, d_shift = last_sums
        gain_grads[layer] = d_gain
        shift_grads[layer] = d_shift
        d_pre = mask * rstd * gains[layer] * (gz - d_shift / count - normed * d_gain / count)
        weight_grads[layer] = jnp.dot(x_wide.T, own * d_pre, precision=HIGH)
        flipped = jnp.transpose(weight[::-1], (0, 2, 1)).reshape(-1, weight.shape[1])
        grad = jnp.dot(shifted(d_pre, width), flipped, precision=HIGH)
    grad_mel = cotangent + unextend(grad)
    weight_grads = lax.psum(weight_grads, AXES)
    grad_w_mid = jnp.stack([weight_grads[i].reshape(w_mid.shape[1:]) for i in (1, 2, 3)])
    return (
        mel_after,
        grad_mel,
        weight_grads[0].reshape(w_first.shape),
        grad_w_mid,
        weight_grads[4].reshape(w_last.shape),
        jnp.stack(gain_grads[:4]),
        jnp.stack(shift_grads[:4]),
        gain_grads[4],
        shift_grads[4],
    )


def solution(mesh):
    return jax.shard_map(
        shards,
        mesh=mesh,
        in_specs=(P("dp", "tm", None), P("dp", "tm", None), P("dp")) + (P(),) * 7,
        out_specs=(P("dp", "tm", None), P("dp", "tm", None)) + (P(),) * 7,
        check_vma=False,
    )
```

time: 994 us -> 605 us (0.61)
  blocking collectives: 410 us -> 10.6 us
  matrix products: 184 us -> 97.8 us
  local copies, waits for them, and re-layouts: 13.5 us -> 84.4 us
  waiting for transfers between devices: 280 us -> 303 us
    psum x10 -> x0, blocking collectives: 410 us -> none  [the longest x5 208 us: shards(): lax.psum((jnp.sum(mask * h, axis=(0, 1)), jnp.sum(mask * h * h, axis=(0,...]
    dot_general x75 -> x15, matrix products: 184 us -> 97.8 us  [the longest x5 37.6 us: shards(): weight_grads[layer] = jnp.dot(x_wide.T, own * d_pre, precision=HIGH)]
    all_to_all x0 -> x8, starting transfers between devices: none -> 43.1 us  [all_sum(): return jnp.sum(lax.all_to_all(copies, AXES, 0, 0), axis=0)]
    ppermute x20 -> x2, starting transfers between devices: 41.7 us -> 3.7 us  [the longest x1 2.41 us: extend(): low = lax.ppermute(block[:, -EDGE:], 'tm', forward)]
    transpose x0 -> x7, local copies, waits for them, and re-layouts: none -> 34.3 us  [shards(): jnp.transpose(weight[::-1], (0, 2, 1)).reshape(-1, weight.shape[1])]
    all_to_all x0 -> x8, waiting for transfers between devices: none -> 18.5 us  [all_sum(): return jnp.sum(lax.all_to_all(copies, AXES, 0, 0), axis=0)]
    squeeze x0 -> x1, local copies, waits for them, and re-layouts: none -> 16.1 us  [shards(): weights = [w_first, w_mid[0], w_mid[1], w_mid[2], w_last]]
    all_to_all x0 -> x1, blocking collectives: none -> 10.6 us  [all_sum(): return jnp.sum(lax.all_to_all(copies, AXES, 0, 0), axis=0)]
  transfers between devices with their start and end apart: 21 -> 11, of which waited for: 3 -> 4; matrix products, arithmetic and copies ran while one was open for 9% -> 17% of each run, Pallas kernels for 0% -> 0%
where the time goes in v1:
time: 605 us; the launch traced here: 597 us
  waiting for transfers between devices  303 us (50%)
  matrix products  97.8 us (16%)
  local copies, waits for them, and re-layouts  84.4 us (14%)
  starting transfers between devices  47.1 us (8%)
  other arithmetic  38.2 us (6%)
  between operations  15.8 us (3%)
  blocking collectives  10.6 us (2%)
    psum x1, waiting for transfers between devices, shards(): weight_grads = lax.psum(weight_grads, AXES)  284 us
    all_to_all x8, starting transfers between devices, all_sum(): return jnp.sum(lax.all_to_all(copies, AXES, 0, 0), axis=0)  43.1 us
    dot_general x5, matrix products, shards(): weight_grads[layer] = jnp.dot(x_wide.T, own * d_pre, precision=HIGH)  37.6 us
    transpose x7, local copies, waits for them, and re-layouts, shards(): jnp.transpose(weight[::-1], (0, 2, 1)).reshape(-1, weight.shape[1])  34.3 us
    dot_general x5, matrix products, shards(): h = jnp.dot(x_wide, weight.reshape(-1, weight.shape[2]), precision=HIGH)  33.9 us
    dot_general x5, matrix products, shards(): grad = jnp.dot(shifted(d_pre, width), flipped, precision=HIGH)  26.3 us
    all_to_all x8, waiting for transfers between devices, all_sum(): return jnp.sum(lax.all_to_all(copies, AXES, 0, 0), axis=0)  18.5 us
    squeeze x1, local copies, waits for them, and re-layouts, shards(): weights = [w_first, w_mid[0], w_mid[1], w_mid[2], w_last]  16.1 us
  transfers between devices with their start and end apart: 11, of which 4 were waited for; matrix products, arithmetic and copies ran while one was open for 17% of the time, Pallas kernels for 0%

profile of v1, /device:TPU:0, one launch (start us, length us, event | category | flops | bytes accessed | tf_op | source)
XLA Modules:
  0.0 596.6 jit_solution(12259574147590169389)
XLA Ops:
  9.1 2.4 collective-permute-start
  11.6 1.3 collective-permute-start.1
  12.9 16.1 %slice_bitcast_fusion.3 = (f32[5,512,512]{2,1,0:T(8,128)}, f32[5,512,512]{2,1,0:T(8,128)}, f32[5,512,512]{2,1,0:T(8,128)}, f32[1,5,512,512]{3,2,1,0:T(8,128)}, f...) fusion(f32[3,5,512,512]{3,2,1,0:T(8,128)} %param.14), kind=kLoop, calls=%fused_computation.180 | loop fusion | bytes 47185920 | tf_op jit(solution)/shard_map/squeeze | solution.py:48
  32.8 1.4 multiply_reduce_fusion.3
  35.0 9.2 %all-to-all-start = ((f32[32,3,512]{2,1,0:T(4,128)}), f32[32,3,512]{2,1,0:T(4,128)S(1)}, u32[]{:S(2)}, u32[]{:S(2)}) async-start(f32[32,3,512]{2,1,0:T(4,128)} %broadcast_in_dim.18), calls=%async_computation | async-start | bytes 524288 | tf_op jit(solution)/shard_map/all_to_all | solution.py:23
  44.3 10.5 %all-to-all-done = f32[32,3,512]{2,1,0:T(4,128)S(1)} async-done(((f32[32,3,512]{2,1,0:T(4,128)}), f32[32,3,512]{2,1,0:T(4,128)S(1)}, u32[]{:S(2)}, u32[]{:S(2)}) %all-to-all-start) | async-done | bytes 196640 | tf_op jit(solution)/shard_map/all_to_all | solution.py:23
  57.3 9.9 %multiply_reduce_fusion.2 = (f32[512]{0:T(512)S(1)}, f32[512]{0:T(512)S(1)}, f32[608,512]{1,0:T(8,128)S(1)}) fusion(f32[608]{0:T(1024)S(1)} %reshape.148, f32[608,2560]{1,0:T(8,128)S(1)} %slice_dynamic-update-slice_fusion.28, f32[2560,512]{1,0:T(8,128)} %bitcast.147), kind=kOutput, calls=%fused_computation.11 | convolution fusion | flops 4782750720 | bytes 12720512 | tf_op jit(solution)/shard_map/dot_general | solution.py:58
  67.2 10.6 %all_to_all.45 = f32[32,2,512]{2,1,0:T(2,128)S(1)} all-to-all(f32[32,2,512]{2,1,0:T(2,128)S(1)} %broadcast_in_dim.19), channel_id=1, replica_groups=mesh['dp'=8,'tm'=4] {'dp','tm'}, dimensions={0} | all-to-all | bytes 262144 | tf_op jit(solution)/shard_map/all_to_all | solution.py:23
  79.8 9.9 %multiply_reduce_fusion.1 = (f32[512]{0:T(512)S(1)}, f32[512]{0:T(512)S(1)}, f32[608,512]{1,0:T(8,128)S(1)}) fusion(f32[608]{0:T(1024)S(1)} %reshape.148, f32[608,2560]{1,0:T(8,128)S(1)} %slice_dynamic-update-slice_fusion.24, f32[2560,512]{1,0:T(8,128)} %bitcast.146), kind=kOutput, calls=%fused_computation.9 | convolution fusion | flops 4782750720 | bytes 12720512 | tf_op jit(solution)/shard_map/dot_general | solution.py:58
  90.5 2.6 all-to-all-start.2
  93.1 2.1 copy.94
  95.1 6.1 %all-to-all-done.2 = f32[32,2,512]{2,1,0:T(2,128)S(1)} async-done(((f32[32,2,512]{2,1,0:T(2,128)}), f32[32,2,512]{2,1,0:T(2,128)S(1)}, u32[]{:S(2)}, u32[]{:S(2)}) %all-to-all-start.2) | async-done | bytes 131104 | tf_op jit(solution)/shard_map/all_to_all | solution.py:23
  103.2 9.9 %multiply_reduce_fusion = (f32[512]{0:T(512)S(1)}, f32[512]{0:T(512)S(1)}, f32[608,512]{1,0:T(8,128)S(1)}) fusion(f32[608]{0:T(1024)S(1)} %reshape.148, f32[608,2560]{1,0:T(8,128)S(1)} %slice_dynamic-update-slice_fusion.20, f32[2560,512]{1,0:T(8,128)} %bitcast.145), kind=kOutput, calls=%fused_computation.7 | convolution fusion | flops 4782750720 | bytes 12720512 | tf_op jit(solution)/shard_map/dot_general | solution.py:58
  113.9 2.8 all-to-all-start.3
  116.7 9.2 %reverse_bitcast_fusion = (f32[5,512,512]{1,2,0:T(8,128)}, f32[5,512,512]{1,2,0:T(8,128)}) fusion(f32[5,512,512]{2,1,0:T(8,128)} %get-tuple-element.84, f32[5,512,512]{2,1,0:T(8,128)} %get-tuple-element.85), kind=kLoop, calls=%fused_computation.3 | loop fusion | bytes 20971520 | tf_op jit(solution)/shard_map/transpose | solution.py:104
  129.0 2.9 multiply_reduce_fusion.13
  132.6 5.9 all-to-all-start.4
  138.5 5.7 reverse_bitcast_fusion.2
  144.3 2.1 rev.15
  146.4 5.9 copy.59
  152.3 5.9 copy.57
  158.2 5.9 copy.55
  166.1 1.6 subtract_multiply_fusion.8
  168.3 2.8 multiply_reduce_fusion.7
  171.7 6.3 %all-to-all-start.5 = ((f32[32,2,512]{2,1,0:T(2,128)}), f32[32,2,512]{2,1,0:T(2,128)S(1)}, u32[]{:S(2)}, u32[]{:S(2)}) async-start(f32[32,2,512]{2,1,0:T(2,128)} %broadcast_in_dim.23), calls=%async_computation.5 | async-start | bytes 262144 | tf_op jit(solution)/shard_map/all_to_all | solution.py:23
  178.1 4.7 fusion.31
  182.8 1.5 reshape.146
  184.3 1.9 all-to-all-done.5
  187.1 3.1 subtract_multiply_fusion.3
  192.1 6.8 %multiply_reduce_fusion.6 = (f32[512]{0:T(512)S(1)}, f32[512]{0:T(512)S(1)}, f32[608,512]{1,0:T(8,128)}) fusion(f32[608,512]{1,0:T(8,128)S(1)} %copy-done.4, f32[512]{0:T(512)S(1)} %bitcast.171, f32[512]{0:T(512)S(1)} %bitcast.175, f32[608]{0:T(1024)S(1)} %reshape.148, f32[512]{0:T(512)S(1)} %bitcast.205, f32[512]{0:T(512)S(1)} %bitcast.187, ...), kind=kOutput, calls=%fused_computation.51 | convolution fusion | flops 4785241088 | bytes 13976320 | tf_op jit(solution)/shard_map/dot_general | solution.py:105
  199.6 4.2 all-to-all-start.6
  203.8 10.2 %fusion.10 = f32[2560,512]{1,0:T(8,128)} fusion(f32[608,2560]{1,0:T(8,128)} %copy-done.7, f32[608,512]{1,0:T(8,128)S(1)} %subtract_multiply_fusion.3, f32[608]{0:T(1024)S(1)} %reshape.148), kind=kOutput, calls=%fused_computation.26 | convolution fusion | flops 4781817856 | bytes 12716416 | tf_op jit(solution)/shard_map/dot_general | solution.py:103
  214.8 3.1 subtract_multiply_fusion.2
  219.8 6.7 %multiply_reduce_fusion.5 = (f32[512]{0:T(512)S(1)}, f32[512]{0:T(512)S(1)}, f32[608,512]{1,0:T(8,128)}) fusion(f32[608,512]{1,0:T(8,128)S(1)} %copy-done.2, f32[512]{0:T(512)S(1)} %bitcast.163, f32[512]{0:T(512)S(1)} %bitcast.167, f32[608]{0:T(1024)S(1)} %reshape.148, f32[512]{0:T(512)S(1)} %bitcast.202, f32[512]{0:T(512)S(1)} %bitcast.183, ...), kind=kOutput, calls=%fused_computation.45 | convolution fusion | flops 4785241088 | bytes 13976320 | tf_op jit(solution)/shard_map/dot_general | solution.py:105
  227.2 6.2 %all-to-all-start.7 = ((f32[32,2,512]{2,1,0:T(2,128)}), f32[32,2,512]{2,1,0:T(2,128)S(1)}, u32[]{:S(2)}, u32[]{:S(2)}) async-start(f32[32,2,512]{2,1,0:T(2,128)} %broadcast_in_dim.25), calls=%async_computation.7 | async-start | bytes 262144 | tf_op jit(solution)/shard_map/all_to_all | solution.py:23
  233.4 10.3 %fusion.12 = f32[2560,512]{1,0:T(8,128)} fusion(f32[608,2560]{1,0:T(8,128)} %copy-done.6, f32[608,512]{1,0:T(8,128)S(1)} %subtract_multiply_fusion.2, f32[608]{0:T(1024)S(1)} %reshape.148), kind=kOutput, calls=%fused_computation.28 | convolution fusion | flops 4781817856 | bytes 12716416 | tf_op jit(solution)/shard_map/dot_general | solution.py:103
  244.5 3.1 subtract_multiply_fusion.1
  248.9 6.8 %multiply_reduce_fusion.4 = (f32[512]{0:T(512)S(1)}, f32[512]{0:T(512)S(1)}, f32[608,512]{1,0:T(8,128)}) fusion(f32[608,512]{1,0:T(8,128)S(1)} %get-tuple-element.117, f32[512]{0:T(512)S(1)} %bitcast.155, f32[512]{0:T(512)S(1)} %bitcast.159, f32[608]{0:T(1024)S(1)} %reshape.148, f32[512]{0:T(512)S(1)} %bitcast.199, f32[512]{0:T(512)S(1)} %bitcast.179, ...), kind=kOutput, calls=%fused_computation.39 | convolution fusion | flops 4785241088 | bytes 13976320 | tf_op jit(solution)/shard_map/dot_general | solution.py:105
  256.4 5.9 all-to-all-start.8
  262.6 10.3 %fusion.14 = f32[2560,512]{1,0:T(8,128)} fusion(f32[608,2560]{1,0:T(8,128)} %copy-done.5, f32[608,512]{1,0:T(8,128)S(1)} %subtract_multiply_fusion.1, f32[608]{0:T(1024)S(1)} %reshape.148), kind=kOutput, calls=%fused_computation.30 | convolution fusion | flops 4781817856 | bytes 12716416 | tf_op jit(solution)/shard_map/dot_general | solution.py:103
  273.7 2.5 subtract_multiply_fusion
  276.2 2.1 fusion.16
  279.5 1.6 copy.61
  281.2 1.8 reshape.149
  286.8 3.2 fusion.18
  290.0 284.2 %all-reduce.13.cloned.1.call-done = (f32[5,80,512]{2,1,0:T(8,128)}, f32[1,5,512,512]{3,2,1,0:T(8,128)}, f32[1,5,512,512]{3,2,1,0:T(8,128)}, f32[1,5,512,512]{3,2,1,0:T(8,128)}, f32[5,512,80]{1,0,2:T(8,128)}) async-done(((f32[5,80,512]{2,1,0:T(8,128)}, f32[1,5,512,512]{3,2,1,0:T(8,128)}, f32[1,5,512,512]{3,2,1,0:T(8,128)}, f32[1,5,512,512]{3,2,1,0:T(8,128)}, f32[5,512,80]{1,0,2:T(8,128)}), ...) | async-done | bytes 17367056 | tf_op jit(solution)/shard_map/psum | solution.py:107
  574.1 2.7 copy.62
  576.8 11.6 %pad_maximum_fusion = f32[3,5,512,512]{3,2,1,0:T(8,128)} fusion(f32[1,5,512,512]{3,2,1,0:T(8,128)} %get-tuple-element.66, f32[1,5,512,512]{3,2,1,0:T(8,128)} %get-tuple-element.67, f32[1,5,512,512]{3,2,1,0:T(8,128)} %get-tuple-element.68), kind=kLoop, calls=%fused_computation | loop fusion | flops 7864320 | bytes 31457280 | tf_op jit(solution)/shard_map/stack | solution.py:108
  (219 shorter events, 37.5 us)
Async XLA Ops:
  9.1 21.5 %collective-permute-start = (f32[2,24,160]{1,2,0:T(8,128)S(1)}, f32[2,24,160]{1,2,0:T(8,128)S(1)}, u32[]{:S(2)}, u32[]{:S(2)}) collective-permute-start(f32[2,24,160]{1,2,0:T(8,128)S(1)} %get-tuple-element.90), channel_id=1, source_target_pairs={{0,1},{1,2},{2,3},{4,5},{5,6},{6,7},{8,9},{9,10},{10,11},{12,13},{... | collective-permute-start | bytes 92168 | tf_op jit(solution)/shard_map/ppermute | solution.py:15
  11.6 19.1 %collective-permute-start.1 = (f32[2,24,160]{1,2,0:T(8,128)S(1)}, f32[2,24,160]{1,2,0:T(8,128)S(1)}, u32[]{:S(2)}, u32[]{:S(2)}) collective-permute-start(f32[2,24,160]{1,2,0:T(8,128)S(1)} %get-tuple-element.91), channel_id=1, source_target_pairs={{1,0},{2,1},{3,2},{5,4},{6,5},{7,6},{9,8},{10,9},{11,10},{13,12},{... | collective-permute-start | bytes 92168 | tf_op jit(solution)/shard_map/ppermute | solution.py:16
  12.9 16.1 %copy-start.39 = (s32[2]{0:T(128)S(1)}, s32[2]{0:T(128)}, u32[]{:S(2)}) copy-start(s32[2]{0:T(128)} %param.12) | copy-start | bytes 28
  32.1 2.0 copy-start.9
  32.8 11.5 %copy-start.37 = (f32[4,512]{1,0:T(4,128)S(1)}, f32[4,512]{1,0:T(4,128)}, u32[]{:S(2)}) copy-start(f32[4,512]{1,0:T(4,128)} %param.16) | copy-start | bytes 24580
  32.8 11.5 %copy-start.38 = (f32[4,512]{1,0:T(4,128)S(1)}, f32[4,512]{1,0:T(4,128)}, u32[]{:S(2)}) copy-start(f32[4,512]{1,0:T(4,128)} %param.17) | copy-start | bytes 24580
  35.0 19.8 %all-to-all-start = ((f32[32,3,512]{2,1,0:T(4,128)}), f32[32,3,512]{2,1,0:T(4,128)S(1)}, u32[]{:S(2)}, u32[]{:S(2)}) async-start(f32[32,3,512]{2,1,0:T(4,128)} %broadcast_in_dim.18), calls=%async_computation | async-start | bytes 524288 | tf_op jit(solution)/shard_map/all_to_all | solution.py:23
  44.2 58.3 %copy-start.18 = (f32[1,512]{1,0:T(1,128)}, f32[1,512]{1,0:T(1,128)S(1)}, u32[]{:S(2)}) copy-start(f32[1,512]{1,0:T(1,128)S(1)} %get-tuple-element.97) | copy-start | bytes 6148
  44.3 83.0 %copy-start.32 = (f32[1,512]{1,0:T(1,128)}, f32[1,512]{1,0:T(1,128)S(1)}, u32[]{:S(2)}) copy-start(f32[1,512]{1,0:T(1,128)S(1)} %get-tuple-element.94) | copy-start | bytes 6148
  44.3 12.4 %copy-start.26 = (f32[1,512]{1,0:T(1,128)}, f32[1,512]{1,0:T(1,128)S(1)}, u32[]{:S(2)}) copy-start(f32[1,512]{1,0:T(1,128)S(1)} %get-tuple-element.100) | copy-start | bytes 6148
  44.3 34.9 %copy-start.28 = (f32[1,512]{1,0:T(1,128)}, f32[1,512]{1,0:T(1,128)S(1)}, u32[]{:S(2)}) copy-start(f32[1,512]{1,0:T(1,128)S(1)} %get-tuple-element.99) | copy-start | bytes 6148
  44.3 58.3 %copy-start.30 = (f32[1,512]{1,0:T(1,128)}, f32[1,512]{1,0:T(1,128)S(1)}, u32[]{:S(2)}) copy-start(f32[1,512]{1,0:T(1,128)S(1)} %get-tuple-element.101) | copy-start | bytes 6148
  44.3 82.9 %copy-start.35 = (f32[1,512]{1,0:T(1,128)}, f32[1,512]{1,0:T(1,128)S(1)}, u32[]{:S(2)}) copy-start(f32[1,512]{1,0:T(1,128)S(1)} %get-tuple-element.98) | copy-start | bytes 6148
  57.3 9.9 %copy-start.5 = (f32[608,2560]{1,0:T(8,128)}, f32[608,2560]{1,0:T(8,128)S(1)}, u32[]{:S(2)}) copy-start(f32[608,2560]{1,0:T(8,128)S(1)} %slice_dynamic-update-slice_fusion.28) | copy-start | bytes 18677764
  67.2 12.0 %copy-start.1 = (f32[608,512]{1,0:T(8,128)}, f32[608,512]{1,0:T(8,128)S(1)}, u32[]{:S(2)}) copy-start(f32[608,512]{1,0:T(8,128)S(1)} %get-tuple-element.118) | copy-start | bytes 3735556
  79.8 9.9 %copy-start.6 = (f32[608,2560]{1,0:T(8,128)}, f32[608,2560]{1,0:T(8,128)S(1)}, u32[]{:S(2)}) copy-start(f32[608,2560]{1,0:T(8,128)S(1)} %slice_dynamic-update-slice_fusion.24) | copy-start | bytes 18677764
  89.7 12.9 %copy-start.3 = (f32[608,512]{1,0:T(8,128)}, f32[608,512]{1,0:T(8,128)S(1)}, u32[]{:S(2)}) copy-start(f32[608,512]{1,0:T(8,128)S(1)} %get-tuple-element.119) | copy-start | bytes 3735556
  90.5 10.8 %all-to-all-start.2 = ((f32[32,2,512]{2,1,0:T(2,128)}), f32[32,2,512]{2,1,0:T(2,128)S(1)}, u32[]{:S(2)}, u32[]{:S(2)}) async-start(f32[32,2,512]{2,1,0:T(2,128)} %broadcast_in_dim.20), calls=%async_computation.2 | async-start | bytes 262144 | tf_op jit(solution)/shard_map/all_to_all | solution.py:23
  103.2 9.9 %copy-start.7 = (f32[608,2560]{1,0:T(8,128)}, f32[608,2560]{1,0:T(8,128)S(1)}, u32[]{:S(2)}) copy-start(f32[608,2560]{1,0:T(8,128)S(1)} %slice_dynamic-update-slice_fusion.20) | copy-start | bytes 18677764
  113.1 55.1 %copy-start.8 = (f32[608,512]{1,0:T(8,128)}, f32[608,512]{1,0:T(8,128)S(1)}, u32[]{:S(2)}) copy-start(f32[608,512]{1,0:T(8,128)S(1)} %get-tuple-element.120) | copy-start | bytes 3735556
  113.9 12.0 %all-to-all-start.3 = ((f32[32,2,512]{2,1,0:T(2,128)}), f32[32,2,512]{2,1,0:T(2,128)S(1)}, u32[]{:S(2)}, u32[]{:S(2)}) async-start(f32[32,2,512]{2,1,0:T(2,128)} %broadcast_in_dim.21), calls=%async_computation.3 | async-start | bytes 262144 | tf_op jit(solution)/shard_map/all_to_all | solution.py:23
  127.7 1.3 copy-start.13
  127.9 4.0 copy-start
  132.6 31.5 %all-to-all-start.4 = ((f32[32,4,80]{2,1,0:T(4,128)}), f32[32,4,80]{2,1,0:T(4,128)S(1)}, u32[]{:S(2)}, u32[]{:S(2)}) async-start(f32[32,4,80]{2,1,0:T(4,128)} %broadcast_in_dim.22), calls=%async_computation.4 | async-start | bytes 131072 | tf_op jit(solution)/shard_map/all_to_all | solution.py:23
  166.1 2.2 copy-start.15
  166.1 2.2 copy-start.21
  166.1 2.2 copy-start.24
  166.1 2.2 copy-start.33
  166.1 2.2 copy-start.36
  171.7 14.5 %all-to-all-start.5 = ((f32[32,2,512]{2,1,0:T(2,128)}), f32[32,2,512]{2,1,0:T(2,128)S(1)}, u32[]{:S(2)}, u32[]{:S(2)}) async-start(f32[32,2,512]{2,1,0:T(2,128)} %broadcast_in_dim.23), calls=%async_computation.5 | async-start | bytes 262144 | tf_op jit(solution)/shard_map/all_to_all | solution.py:23
  182.8 4.3 copy-start.22
  182.8 4.3 copy-start.25
  182.8 4.3 copy-start.34
  187.0 3.8 slice-start.4
  190.7 1.4 copy-start.4
  190.7 1.4 copy-start.19
  190.7 1.4 copy-start.31
  199.6 14.4 %all-to-all-start.6 = ((f32[32,2,512]{2,1,0:T(2,128)}), f32[32,2,512]{2,1,0:T(2,128)S(1)}, u32[]{:S(2)}, u32[]{:S(2)}) async-start(f32[32,2,512]{2,1,0:T(2,128)} %broadcast_in_dim.24), calls=%async_computation.6 | async-start | bytes 262144 | tf_op jit(solution)/shard_map/all_to_all | solution.py:23
  214.8 3.8 slice-start.2
  218.4 1.4 copy-start.2
  218.4 1.4 copy-start.29
  227.2 16.4 %all-to-all-start.7 = ((f32[32,2,512]{2,1,0:T(2,128)}), f32[32,2,512]{2,1,0:T(2,128)S(1)}, u32[]{:S(2)}, u32[]{:S(2)}) async-start(f32[32,2,512]{2,1,0:T(2,128)} %broadcast_in_dim.25), calls=%async_computation.7 | async-start | bytes 262144 | tf_op jit(solution)/shard_map/all_to_all | solution.py:23
  244.5 3.8 slice-start
  256.4 16.6 %all-to-all-start.8 = ((f32[32,2,512]{2,1,0:T(2,128)}), f32[32,2,512]{2,1,0:T(2,128)S(1)}, u32[]{:S(2)}, u32[]{:S(2)}) async-start(f32[32,2,512]{2,1,0:T(2,128)} %broadcast_in_dim.26), calls=%async_computation.8 | async-start | bytes 262144 | tf_op jit(solution)/shard_map/all_to_all | solution.py:23
  262.3 311.8 %all-reduce.13.cloned.1.call-start = ((), (), s32[]{:S(2)}) async-start(), calls=%async_computation.9 | async-start | bytes 35717120 | tf_op jit(solution)/shard_map/psum | solution.py:107
  273.7 2.5 copy-start.10
  281.2 2.2 copy-start.17
  576.8 11.6 %copy-start.14 = (f32[5,80,512]{2,1,0:T(8,128)S(1)}, f32[5,80,512]{2,1,0:T(8,128)}, u32[]{:S(2)}) copy-start(f32[5,80,512]{2,1,0:T(8,128)} %get-tuple-element.132) | copy-start | bytes 2457604
  (9 other events, 9.0 us)
Sparse Core Ops, SparseCore 0:
  278.5 295.6 all-reduce.12

commit v2 on v1

--- a/solution.py
+++ b/solution.py
@@ -21,6 +21,45 @@
     devices = lax.axis_size(AXES)
     copies = jnp.broadcast_to(parts[None], (devices,) + parts.shape)
     return jnp.sum(lax.all_to_all(copies, AXES, 0, 0), axis=0)
+
+
+def swap(x, bit):
+    devices = lax.axis_size(AXES)
+    return lax.ppermute(x, AXES, [(i, i ^ (1 << bit)) for i in range(devices)])
+
+
+def halve(x, bit):
+    half = x.shape[0] // 2
+    upper = ((lax.axis_index(AXES) >> bit) & 1) == 1
+    low, high = x[:half], x[half:]
+    return jnp.where(upper, high, low) + swap(jnp.where(upper, low, high), bit)
+
+
+def double(x, bit):
+    upper = ((lax.axis_index(AXES) >> bit) & 1) == 1
+    other = swap(x, bit)
+    return jnp.concatenate([jnp.where(upper, other, x), jnp.where(upper, x, other)], axis=0)
+
+
+def exchange_sum(x, sizes):
+    bits = (lax.axis_size(AXES) - 1).bit_length()
+    near = list(range(1, 1 + len(sizes)))
+    orders = [near[i:] + near[:i] for i in range(len(sizes))]
+    rest = list(range(1 + len(sizes), bits))
+    x = halve(x, 0)
+    groups = jnp.split(x, [sum(sizes[: i + 1]) for i in range(len(sizes) - 1)])
+    for turn in range(len(near)):
+        groups = [halve(g, order[turn]) for g, order in zip(groups, orders)]
+    marks = [g.shape[0] for g in groups]
+    x = jnp.concatenate(groups)
+    for bit in rest:
+        x = halve(x, bit)
+    for bit in reversed(rest):
+        x = double(x, bit)
+    groups = jnp.split(x, [sum(marks[: i + 1]) for i in range(len(marks) - 1)])
+    for turn in reversed(range(len(near))):
+        groups = [double(g, order[turn]) for g, order in zip(groups, orders)]
+    return double(jnp.concatenate(groups), 0)
 
 
 def shifted(x, width):
@@ -104,7 +143,12 @@
         flipped = jnp.transpose(weight[::-1], (0, 2, 1)).reshape(-1, weight.shape[1])
         grad = jnp.dot(shifted(d_pre, width), flipped, precision=HIGH)
     grad_mel = cotangent + unextend(grad)
-    weight_grads = lax.psum(weight_grads, AXES)
+    weight_grads[3], weight_grads[4] = lax.psum((weight_grads[3], weight_grads[4]), AXES)
+    weight_grads[2] = exchange_sum(weight_grads[2], [512, 384, 384])
+    weight_grads[1] = exchange_sum(weight_grads[1], [512, 384, 384])
+    first = weight_grads[0]
+    padded = jnp.pad(first, ((0, -first.shape[0] % 512), (0, 0)))
+    weight_grads[0] = exchange_sum(padded, [padded.shape[0] // 2])[: first.shape[0]]
     grad_w_mid = jnp.stack([weight_grads[i].reshape(w_mid.shape[1:]) for i in (1, 2, 3)])
     return (
         mel_after,

time: 605 us -> 534 us (0.88)
  waiting for transfers between devices: 303 us -> 157 us
  starting transfers between devices: 47.1 us -> 92.5 us
  other arithmetic: 38.2 us -> 57.9 us
  blocking collectives: 10.6 us -> 20.6 us
    psum x1, waiting for transfers between devices: 284 us -> 0.01 us  [shards(): lax.psum((weight_grads[3], weight_grads[4]), AXES)]
    ppermute x0 -> x54, waiting for transfers between devices: none -> 141 us  [swap(): return lax.ppermute(x, AXES, [(i, i ^ 1 << bit) for i in range(devices)])]
    ppermute x0 -> x54, starting transfers between devices: none -> 46.9 us  [swap(): return lax.ppermute(x, AXES, [(i, i ^ 1 << bit) for i in range(devices)])]
    select_n x0 -> x46, other arithmetic: none -> 12.4 us  [the longest x25 6.3 us: halve(): return jnp.where(upper, high, low) + swap(jnp.where(upper, low, high), bit)]
    all_to_all x1 -> x2, blocking collectives: 10.6 us -> 20.6 us  [all_sum(): return jnp.sum(lax.all_to_all(copies, AXES, 0, 0), axis=0)]
    all_to_all x8 -> x7, waiting for transfers between devices: 18.5 us -> 15.8 us  [all_sum(): return jnp.sum(lax.all_to_all(copies, AXES, 0, 0), axis=0)]
    all_to_all x8 -> x7, starting transfers between devices: 43.1 us -> 41.7 us  [all_sum(): return jnp.sum(lax.all_to_all(copies, AXES, 0, 0), axis=0)]
    unnamed x131 -> x136, local copies, waits for them, and re-layouts: 15.8 us -> 15.1 us
  transfers between devices with their start and end apart: 11 -> 64, of which waited for: 4 -> 34; matrix products, arithmetic and copies ran while one was open for 17% -> 30% of each run, Pallas kernels for 0% -> 0%
where the time goes in v2:
time: 534 us; the launch traced here: 526 us
  waiting for transfers between devices  157 us (29%)
  matrix products  95.8 us (18%)
  starting transfers between devices  92.5 us (17%)
  local copies, waits for them, and re-layouts  85.3 us (16%)
  other arithmetic  57.9 us (11%)
  blocking collectives  20.6 us (4%)
  between operations  16.5 us (3%)
    ppermute x54, waiting for transfers between devices, swap(): return lax.ppermute(x, AXES, [(i, i ^ 1 << bit) for i in range(devices)])  141 us
    ppermute x54, starting transfers between devices, swap(): return lax.ppermute(x, AXES, [(i, i ^ 1 << bit) for i in range(devices)])  46.9 us
    all_to_all x7, starting transfers between devices, all_sum(): return jnp.sum(lax.all_to_all(copies, AXES, 0, 0), axis=0)  41.7 us
    dot_general x5, matrix products, shards(): weight_grads[layer] = jnp.dot(x_wide.T, own * d_pre, precision=HIGH)  35.7 us
    transpose x7, local copies, waits for them, and re-layouts, shards(): jnp.transpose(weight[::-1], (0, 2, 1)).reshape(-1, weight.shape[1])  35.5 us
    dot_general x5, matrix products, shards(): h = jnp.dot(x_wide, weight.reshape(-1, weight.shape[2]), precision=HIGH)  33.9 us
    dot_general x5, matrix products, shards(): grad = jnp.dot(shifted(d_pre, width), flipped, precision=HIGH)  26.3 us
    all_to_all x2, blocking collectives, all_sum(): return jnp.sum(lax.all_to_all(copies, AXES, 0, 0), axis=0)  20.6 us
  transfers between devices with their start and end apart: 64, of which 34 were waited for; matrix products, arithmetic and copies ran while one was open for 30% of the time, Pallas kernels for 0%

profile of v2, /device:TPU:0, one launch (start us, length us, event | category | flops | bytes accessed | tf_op | source)
XLA Modules:
  0.0 525.5 jit_solution(13027215765771242821)
XLA Ops:
  12.9 16.1 %slice_bitcast_fusion.3 = (f32[5,512,512]{2,1,0:T(8,128)}, f32[5,512,512]{2,1,0:T(8,128)}, f32[5,512,512]{2,1,0:T(8,128)}, f32[1,5,512,512]{3,2,1,0:T(8,128)}, f...) fusion(f32[3,5,512,512]{3,2,1,0:T(8,128)} %param.14), kind=kLoop, calls=%fused_computation.314 | loop fusion | bytes 47185920 | tf_op jit(solution)/shard_map/squeeze | solution.py:87
  35.0 9.2 %all-to-all-start = ((f32[32,3,512]{2,1,0:T(4,128)}), f32[32,3,512]{2,1,0:T(4,128)S(1)}, u32[]{:S(2)}, u32[]{:S(2)}) async-start(f32[32,3,512]{2,1,0:T(4,128)} %broadcast_in_dim.18), calls=%async_computation | async-start | bytes 524288 | tf_op jit(solution)/shard_map/all_to_all | solution.py:23
  44.3 10.5 %all-to-all-done = f32[32,3,512]{2,1,0:T(4,128)S(1)} async-done(((f32[32,3,512]{2,1,0:T(4,128)}), f32[32,3,512]{2,1,0:T(4,128)S(1)}, u32[]{:S(2)}, u32[]{:S(2)}) %all-to-all-start) | async-done | bytes 196640 | tf_op jit(solution)/shard_map/all_to_all | solution.py:23
  57.2 9.9 %multiply_reduce_fusion.2 = (f32[512]{0:T(512)S(1)}, f32[512]{0:T(512)S(1)}, f32[608,512]{1,0:T(8,128)S(1)}) fusion(f32[608]{0:T(1024)S(1)} %reshape.148, f32[608,2560]{1,0:T(8,128)S(1)} %slice_dynamic-update-slice_fusion.28, f32[2560,512]{1,0:T(8,128)} %bitcast.151), kind=kOutput, calls=%fused_computation.17 | convolution fusion | flops 4782750720 | bytes 12720512 | tf_op jit(solution)/shard_map/dot_general | solution.py:97
  67.2 10.6 %all_to_all.45 = f32[32,2,512]{2,1,0:T(2,128)S(1)} all-to-all(f32[32,2,512]{2,1,0:T(2,128)S(1)} %broadcast_in_dim.19), channel_id=1, replica_groups=mesh['dp'=8,'tm'=4] {'dp','tm'}, dimensions={0} | all-to-all | bytes 262144 | tf_op jit(solution)/shard_map/all_to_all | solution.py:23
  79.7 9.9 %multiply_reduce_fusion.1 = (f32[512]{0:T(512)S(1)}, f32[512]{0:T(512)S(1)}, f32[608,512]{1,0:T(8,128)S(1)}) fusion(f32[608]{0:T(1024)S(1)} %reshape.148, f32[608,2560]{1,0:T(8,128)S(1)} %slice_dynamic-update-slice_fusion.24, f32[2560,512]{1,0:T(8,128)} %bitcast.150), kind=kOutput, calls=%fused_computation.15 | convolution fusion | flops 4782750720 | bytes 12720512 | tf_op jit(solution)/shard_map/dot_general | solution.py:97
  89.7 10.0 %all_to_all.46 = f32[32,2,512]{2,1,0:T(2,128)S(1)} all-to-all(f32[32,2,512]{2,1,0:T(2,128)S(1)} %broadcast_in_dim.20), channel_id=1, replica_groups=mesh['dp'=8,'tm'=4] {'dp','tm'}, dimensions={0} | all-to-all | bytes 262144 | tf_op jit(solution)/shard_map/all_to_all | solution.py:23
  101.6 9.9 %multiply_reduce_fusion = (f32[512]{0:T(512)S(1)}, f32[512]{0:T(512)S(1)}, f32[608,512]{1,0:T(8,128)S(1)}) fusion(f32[608]{0:T(1024)S(1)} %reshape.148, f32[608,2560]{1,0:T(8,128)S(1)} %slice_dynamic-update-slice_fusion.20, f32[2560,512]{1,0:T(8,128)} %bitcast.149), kind=kOutput, calls=%fused_computation.13 | convolution fusion | flops 4782750720 | bytes 12720512 | tf_op jit(solution)/shard_map/dot_general | solution.py:97
  115.2 9.2 %reverse_bitcast_fusion = (f32[5,512,512]{1,2,0:T(8,128)}, f32[5,512,512]{1,2,0:T(8,128)}) fusion(f32[5,512,512]{2,1,0:T(8,128)} %get-tuple-element.81, f32[5,512,512]{2,1,0:T(8,128)} %get-tuple-element.82), kind=kLoop, calls=%fused_computation.5 | loop fusion | bytes 20971520 | tf_op jit(solution)/shard_map/transpose | solution.py:143
  128.6 5.9 %reverse_bitcast_fusion.2 = f32[5,512,512]{1,2,0:T(8,128)} fusion(f32[5,512,512]{2,1,0:T(8,128)} %get-tuple-element.83), kind=kLoop, calls=%fused_computation.7 | loop fusion | bytes 10485760 | tf_op jit(solution)/shard_map/transpose | solution.py:143
  141.1 5.9 %all-to-all-start.4 = ((f32[32,4,80]{2,1,0:T(4,128)}), f32[32,4,80]{2,1,0:T(4,128)S(1)}, u32[]{:S(2)}, u32[]{:S(2)}) async-start(f32[32,4,80]{2,1,0:T(4,128)} %broadcast_in_dim.22), calls=%async_computation.4 | async-start | bytes 131072 | tf_op jit(solution)/shard_map/all_to_all | solution.py:23
  152.5 5.9 %copy.59 = f32[5,512,512]{2,1,0:T(8,128)} copy(f32[5,512,512]{1,2,0:T(8,128)} %get-tuple-element.177) | data formatting | bytes 10485760 | tf_op jit(solution)/shard_map/transpose | solution.py:143
  158.4 5.9 %copy.57 = f32[5,512,512]{2,1,0:T(8,128)} copy(f32[5,512,512]{1,2,0:T(8,128)} %get-tuple-element.178) | data formatting | bytes 10485760 | tf_op jit(solution)/shard_map/transpose | solution.py:143
  164.4 5.9 %copy.55 = f32[5,512,512]{2,1,0:T(8,128)} copy(f32[5,512,512]{1,2,0:T(8,128)} %reverse_bitcast_fusion.2) | data formatting | bytes 10485760 | tf_op jit(solution)/shard_map/transpose | solution.py:143
  177.9 6.0 %all-to-all-start.5 = ((f32[32,2,512]{2,1,0:T(2,128)}), f32[32,2,512]{2,1,0:T(2,128)S(1)}, u32[]{:S(2)}, u32[]{:S(2)}) async-start(f32[32,2,512]{2,1,0:T(2,128)} %broadcast_in_dim.23), calls=%async_computation.5 | async-start | bytes 262144 | tf_op jit(solution)/shard_map/all_to_all | solution.py:23
  183.9 4.7 fusion.31
  197.9 6.7 %multiply_reduce_fusion.6 = (f32[512]{0:T(512)S(1)}, f32[512]{0:T(512)S(1)}, f32[608,512]{1,0:T(8,128)}) fusion(f32[608,512]{1,0:T(8,128)S(1)} %copy-done.4, f32[512]{0:T(512)S(1)} %bitcast.175, f32[512]{0:T(512)S(1)} %bitcast.179, f32[608]{0:T(1024)S(1)} %reshape.148, f32[512]{0:T(512)S(1)} %bitcast.209, f32[512]{0:T(512)S(1)} %bitcast.191, ...), kind=kOutput, calls=%fused_computation.61 | convolution fusion | flops 4785241088 | bytes 13976320 | tf_op jit(solution)/shard_map/dot_general | solution.py:144
  205.4 5.2 all-to-all-start.6
  210.8 10.4 %fusion.10 = f32[2560,512]{1,0:T(8,128)} fusion(f32[608,2560]{1,0:T(8,128)} %copy-done.7, f32[608,512]{1,0:T(8,128)S(1)} %subtract_multiply_fusion.3, f32[608]{0:T(1024)S(1)} %reshape.148), kind=kOutput, calls=%fused_computation.36 | convolution fusion | flops 4781817856 | bytes 12716416 | tf_op jit(solution)/shard_map/dot_general | solution.py:142
  227.0 6.7 %multiply_reduce_fusion.5 = (f32[512]{0:T(512)S(1)}, f32[512]{0:T(512)S(1)}, f32[608,512]{1,0:T(8,128)}) fusion(f32[608,512]{1,0:T(8,128)S(1)} %copy-done.2, f32[512]{0:T(512)S(1)} %bitcast.167, f32[512]{0:T(512)S(1)} %bitcast.171, f32[608]{0:T(1024)S(1)} %reshape.148, f32[512]{0:T(512)S(1)} %bitcast.206, f32[512]{0:T(512)S(1)} %bitcast.187, ...), kind=kOutput, calls=%fused_computation.55 | convolution fusion | flops 4785241088 | bytes 13976320 | tf_op jit(solution)/shard_map/dot_general | solution.py:144
  234.4 6.3 %all-to-all-start.7 = ((f32[32,2,512]{2,1,0:T(2,128)}), f32[32,2,512]{2,1,0:T(2,128)S(1)}, u32[]{:S(2)}, u32[]{:S(2)}) async-start(f32[32,2,512]{2,1,0:T(2,128)} %broadcast_in_dim.25), calls=%async_computation.7 | async-start | bytes 262144 | tf_op jit(solution)/shard_map/all_to_all | solution.py:23
  240.7 10.3 %fusion.12 = f32[2560,512]{1,0:T(8,128)} fusion(f32[608,2560]{1,0:T(8,128)} %copy-done.6, f32[608,512]{1,0:T(8,128)S(1)} %subtract_multiply_fusion.2, f32[608]{0:T(1024)S(1)} %reshape.148), kind=kOutput, calls=%fused_computation.38 | convolution fusion | flops 4781817856 | bytes 12716416 | tf_op jit(solution)/shard_map/dot_general | solution.py:142
  251.8 3.1 subtract_multiply_fusion.1
  256.3 6.7 %multiply_reduce_fusion.4 = (f32[512]{0:T(512)S(1)}, f32[512]{0:T(512)S(1)}, f32[608,512]{1,0:T(8,128)}) fusion(f32[608,512]{1,0:T(8,128)S(1)} %get-tuple-element.166, f32[512]{0:T(512)S(1)} %bitcast.159, f32[512]{0:T(512)S(1)} %bitcast.163, f32[608]{0:T(1024)S(1)} %reshape.148, f32[512]{0:T(512)S(1)} %bitcast.203, f32[512]{0:T(512)S(1)} %bitcast.183, ...), kind=kOutput, calls=%fused_computation.49 | convolution fusion | flops 4785241088 | bytes 13976320 | tf_op jit(solution)/shard_map/dot_general | solution.py:144
  263.8 6.1 %all-to-all-start.8 = ((f32[32,2,512]{2,1,0:T(2,128)}), f32[32,2,512]{2,1,0:T(2,128)S(1)}, u32[]{:S(2)}, u32[]{:S(2)}) async-start(f32[32,2,512]{2,1,0:T(2,128)} %broadcast_in_dim.26), calls=%async_computation.8 | async-start | bytes 262144 | tf_op jit(solution)/shard_map/all_to_all | solution.py:23
  269.8 4.8 slice_select_fusion
  274.9 4.6 all-to-all-done.8
  284.8 9.1 %fusion.14 = f32[2560,512]{1,0:T(8,128)S(1)} fusion(f32[608,2560]{1,0:T(8,128)} %copy-done.5, f32[608,512]{1,0:T(8,128)S(1)} %subtract_multiply_fusion.1, f32[608]{0:T(1024)S(1)} %reshape.148), kind=kOutput, calls=%fused_computation.40 | convolution fusion | flops 4781817856 | bytes 12716416 | tf_op jit(solution)/shard_map/dot_general | solution.py:142
  295.5 6.8 %collective-permute-done.3 = f32[128,512]{1,0:T(8,128)S(1)} collective-permute-done((f32[128,512]{1,0:T(8,128)S(1)}, f32[128,512]{1,0:T(8,128)S(1)}, u32[]{:S(2)}, u32[]{:S(2)}) %collective-permute-start.3) | collective-permute-done | bytes 262176 | tf_op jit(solution)/shard_map/ppermute | solution.py:28
  303.3 4.1 collective-permute-done.4
  312.9 5.8 %collective-permute-done.6 = f32[16,512]{1,0:T(8,128)S(1)} collective-permute-done((f32[16,512]{1,0:T(8,128)S(1)}, f32[16,512]{1,0:T(8,128)S(1)}, u32[]{:S(2)}, u32[]{:S(2)}) %collective-permute-start.6) | collective-permute-done | bytes 32800 | tf_op jit(solution)/shard_map/ppermute | solution.py:28
  319.4 4.2 collective-permute-done.7
  324.3 3.6 collective-permute-done.8
  328.2 6.5 %collective-permute-done.9 = f32[64,512]{1,0:T(8,128)S(1)} collective-permute-done((f32[64,512]{1,0:T(8,128)S(1)}, f32[64,512]{1,0:T(8,128)S(1)}, u32[]{:S(2)}, u32[]{:S(2)}) %collective-permute-start.9) | collective-permute-done | bytes 131104 | tf_op jit(solution)/shard_map/ppermute | solution.py:28
  344.3 6.7 %collective-permute-done.35 = f32[192,512]{1,0:T(8,128)S(1)} collective-permute-done((f32[192,512]{1,0:T(8,128)S(1)}, f32[192,512]{1,0:T(8,128)S(1)}, u32[]{:S(2)}, u32[]{:S(2)}) %collective-permute-start.35) | collective-permute-done | bytes 393248 | tf_op jit(solution)/shard_map/ppermute | solution.py:28
  356.2 23.2 %collective-permute-done.39 = f32[96,512]{1,0:T(8,128)S(1)} collective-permute-done((f32[96,512]{1,0:T(8,128)S(1)}, f32[96,512]{1,0:T(8,128)S(1)}, u32[]{:S(2)}, u32[]{:S(2)}) %collective-permute-start.39) | collective-permute-done | bytes 196640 | tf_op jit(solution)/shard_map/ppermute | solution.py:28
  380.9 8.9 %collective-permute-done.36 = f32[96,512]{1,0:T(8,128)S(1)} collective-permute-done((f32[96,512]{1,0:T(8,128)S(1)}, f32[96,512]{1,0:T(8,128)S(1)}, u32[]{:S(2)}, u32[]{:S(2)}) %collective-permute-start.36) | collective-permute-done | bytes 196640 | tf_op jit(solution)/shard_map/ppermute | solution.py:28
  392.9 4.8 collective-permute-done.40
  412.9 6.4 %collective-permute-done.44 = f32[80,512]{1,0:T(8,128)S(1)} collective-permute-done((f32[80,512]{1,0:T(8,128)S(1)}, f32[80,512]{1,0:T(8,128)S(1)}, u32[]{:S(2)}, u32[]{:S(2)}) %collective-permute-start.44) | collective-permute-done | bytes 163872 | tf_op jit(solution)/shard_map/ppermute | solution.py:28
  422.5 8.3 %collective-permute-done.45 = f32[80,512]{1,0:T(8,128)S(1)} collective-permute-done((f32[80,512]{1,0:T(8,128)S(1)}, f32[80,512]{1,0:T(8,128)S(1)}, u32[]{:S(2)}, u32[]{:S(2)}) %collective-permute-start.45) | collective-permute-done | bytes 163872 | tf_op jit(solution)/shard_map/ppermute | solution.py:28
  445.9 5.7 %collective-permute-done.30 = f32[48,512]{1,0:T(8,128)S(1)} collective-permute-done((f32[48,512]{1,0:T(8,128)S(1)}, f32[48,512]{1,0:T(8,128)S(1)}, u32[]{:S(2)}, u32[]{:S(2)}) %collective-permute-start.30) | collective-permute-done | bytes 98336 | tf_op jit(solution)/shard_map/ppermute | solution.py:28
  458.3 3.8 collective-permute-done.31
  463.7 4.1 collective-permute-done.28
  470.3 7.9 %collective-permute-done.48 = f32[256,512]{1,0:T(8,128)S(1)} collective-permute-done((f32[256,512]{1,0:T(8,128)S(1)}, f32[256,512]{1,0:T(8,128)S(1)}, u32[]{:S(2)}, u32[]{:S(2)}) %collective-permute-start.48) | collective-permute-done | bytes 524320 | tf_op jit(solution)/shard_map/ppermute | solution.py:28
  482.0 7.1 %collective-permute-done.26 = f32[256,512]{1,0:T(8,128)S(1)} collective-permute-done((f32[256,512]{1,0:T(8,128)S(1)}, f32[256,512]{1,0:T(8,128)S(1)}, u32[]{:S(2)}, u32[]{:S(2)}) %collective-permute-start.26) | collective-permute-done | bytes 524320 | tf_op jit(solution)/shard_map/ppermute | solution.py:28
  495.3 3.2 fusion.18
  506.6 3.2 broadcast_select_fusion.3
  512.3 6.1 %pad_maximum_fusion = f32[3,5,512,512]{3,2,1,0:T(8,128)} fusion(f32[1,5,512,512]{3,2,1,0:T(8,128)S(1)} %bitcast.148, f32[1,5,512,512]{3,2,1,0:T(8,128)S(1)} %bitcast.144, f32[1,5,512,512]{3,2,1,0:T(8,128)S(1)} %bitcast.145), kind=kLoop, calls=%fused_computation | loop fusion | flops 7864320 | bytes 31457280 | tf_op jit(solution)/shard_map/stack | solution.py:152
  (439 shorter events, 163.4 us)
Async XLA Ops:
  9.1 21.4 %collective-permute-start = (f32[2,24,160]{1,2,0:T(8,128)S(1)}, f32[2,24,160]{1,2,0:T(8,128)S(1)}, u32[]{:S(2)}, u32[]{:S(2)}) collective-permute-start(f32[2,24,160]{1,2,0:T(8,128)S(1)} %get-tuple-element.119), channel_id=1, source_target_pairs={{0,1},{1,2},{2,3},{4,5},{5,6},{6,7},{8,9},{9,10},{10,11},{12,13},{... | collective-permute-start | bytes 92168 | tf_op jit(solution)/shard_map/ppermute | solution.py:15
  11.6 19.0 %collective-permute-start.1 = (f32[2,24,160]{1,2,0:T(8,128)S(1)}, f32[2,24,160]{1,2,0:T(8,128)S(1)}, u32[]{:S(2)}, u32[]{:S(2)}) collective-permute-start(f32[2,24,160]{1,2,0:T(8,128)S(1)} %get-tuple-element.120), channel_id=1, source_target_pairs={{1,0},{2,1},{3,2},{5,4},{6,5},{7,6},{9,8},{10,9},{11,10},{13,12},{... | collective-permute-start | bytes 92168 | tf_op jit(solution)/shard_map/ppermute | solution.py:16
  35.0 19.8 %all-to-all-start = ((f32[32,3,512]{2,1,0:T(4,128)}), f32[32,3,512]{2,1,0:T(4,128)S(1)}, u32[]{:S(2)}, u32[]{:S(2)}) async-start(f32[32,3,512]{2,1,0:T(4,128)} %broadcast_in_dim.18), calls=%async_computation | async-start | bytes 524288 | tf_op jit(solution)/shard_map/all_to_all | solution.py:23
  112.2 22.2 %all-to-all-start.3 = ((f32[32,2,512]{2,1,0:T(2,128)}), f32[32,2,512]{2,1,0:T(2,128)S(1)}, u32[]{:S(2)}, u32[]{:S(2)}) async-start(f32[32,2,512]{2,1,0:T(2,128)} %broadcast_in_dim.21), calls=%async_computation.3 | async-start | bytes 262144 | tf_op jit(solution)/shard_map/all_to_all | solution.py:23
  141.1 29.1 %all-to-all-start.4 = ((f32[32,4,80]{2,1,0:T(4,128)}), f32[32,4,80]{2,1,0:T(4,128)S(1)}, u32[]{:S(2)}, u32[]{:S(2)}) async-start(f32[32,4,80]{2,1,0:T(4,128)} %broadcast_in_dim.22), calls=%async_computation.4 | async-start | bytes 131072 | tf_op jit(solution)/shard_map/all_to_all | solution.py:23
  177.9 14.2 %all-to-all-start.5 = ((f32[32,2,512]{2,1,0:T(2,128)}), f32[32,2,512]{2,1,0:T(2,128)S(1)}, u32[]{:S(2)}, u32[]{:S(2)}) async-start(f32[32,2,512]{2,1,0:T(2,128)} %broadcast_in_dim.23), calls=%async_computation.5 | async-start | bytes 262144 | tf_op jit(solution)/shard_map/all_to_all | solution.py:23
  205.4 15.9 %all-to-all-start.6 = ((f32[32,2,512]{2,1,0:T(2,128)}), f32[32,2,512]{2,1,0:T(2,128)S(1)}, u32[]{:S(2)}, u32[]{:S(2)}) async-start(f32[32,2,512]{2,1,0:T(2,128)} %broadcast_in_dim.24), calls=%async_computation.6 | async-start | bytes 262144 | tf_op jit(solution)/shard_map/all_to_all | solution.py:23
  210.6 290.4 %all-reduce.14.cloned.1.call-start = ((), (), s32[]{:S(2)}) async-start(), calls=%async_computation.9 | async-start | bytes 13107200 | tf_op jit(solution)/shard_map/psum | solution.py:146
  234.4 16.6 %all-to-all-start.7 = ((f32[32,2,512]{2,1,0:T(2,128)}), f32[32,2,512]{2,1,0:T(2,128)S(1)}, u32[]{:S(2)}, u32[]{:S(2)}) async-start(f32[32,2,512]{2,1,0:T(2,128)} %broadcast_in_dim.25), calls=%async_computation.7 | async-start | bytes 262144 | tf_op jit(solution)/shard_map/all_to_all | solution.py:23
  263.8 15.7 %all-to-all-start.8 = ((f32[32,2,512]{2,1,0:T(2,128)}), f32[32,2,512]{2,1,0:T(2,128)S(1)}, u32[]{:S(2)}, u32[]{:S(2)}) async-start(f32[32,2,512]{2,1,0:T(2,128)} %broadcast_in_dim.26), calls=%async_computation.8 | async-start | bytes 262144 | tf_op jit(solution)/shard_map/all_to_all | solution.py:23
  274.6 60.8 %collective-permute-start.34 = (f32[1280,512]{1,0:T(8,128)}, f32[1280,512]{1,0:T(8,128)}, u32[]{:S(2)}, u32[]{:S(2)}) collective-permute-start(f32[1280,512]{1,0:T(8,128)} %slice_select_fusion), channel_id=1, source_target_pairs={{0,1},{1,0},{2,3},{3,2},{4,5},{5,4},{6,7},{7,6},{8,9},{9,8},{10,11... | collective-permute-start | bytes 7864328 | tf_op jit(solution)/shard_map/ppermute | solution.py:28
  284.0 9.9 %collective-permute-start.2 = (f32[256,512]{1,0:T(8,128)S(1)}, f32[256,512]{1,0:T(8,128)S(1)}, u32[]{:S(2)}, u32[]{:S(2)}) collective-permute-start(f32[256,512]{1,0:T(8,128)S(1)} %slice_select_fusion.4), channel_id=1, source_target_pairs={{0,1},{1,0},{2,3},{3,2},{4,5},{5,4},{6,7},{7,6},{8,9},{9,8},{10,11... | collective-permute-start | bytes 1572872 | tf_op jit(solution)/shard_map/ppermute | solution.py:28
  294.1 8.3 %collective-permute-start.3 = (f32[128,512]{1,0:T(8,128)S(1)}, f32[128,512]{1,0:T(8,128)S(1)}, u32[]{:S(2)}, u32[]{:S(2)}) collective-permute-start(f32[128,512]{1,0:T(8,128)S(1)} %slice_select_fusion.11), channel_id=1, source_target_pairs={{0,2},{1,3},{2,0},{3,1},{4,6},{5,7},{6,4},{7,5},{8,10},{9,11},{10,... | collective-permute-start | bytes 786440 | tf_op jit(solution)/shard_map/ppermute | solution.py:28
  295.4 45.6 %collective-permute-start.12 = (f32[1280,512]{1,0:T(8,128)S(1)}, f32[1280,512]{1,0:T(8,128)S(1)}, u32[]{:S(2)}, u32[]{:S(2)}) collective-permute-start(f32[1280,512]{1,0:T(8,128)S(1)} %slice_select_fusion.1), channel_id=1, source_target_pairs={{0,1},{1,0},{2,3},{3,2},{4,5},{5,4},{6,7},{7,6},{8,9},{9,8},{10,11... | collective-permute-start | bytes 7864328 | tf_op jit(solution)/shard_map/ppermute | solution.py:28
  334.7 159.3 %collective-permute-start.10 = (f32[128,512]{1,0:T(8,128)S(1)}, f32[128,512]{1,0:T(8,128)S(1)}, u32[]{:S(2)}, u32[]{:S(2)}) collective-permute-start(f32[128,512]{1,0:T(8,128)S(1)} %pad_maximum_fusion.12), channel_id=1, source_target_pairs={{0,2},{1,3},{2,0},{3,1},{4,6},{5,7},{6,4},{7,5},{8,10},{9,11},{10,... | collective-permute-start | bytes 786440 | tf_op jit(solution)/shard_map/ppermute | solution.py:28
  338.3 17.2 %collective-permute-start.41 = (f32[256,512]{1,0:T(8,128)S(1)}, f32[256,512]{1,0:T(8,128)S(1)}, u32[]{:S(2)}, u32[]{:S(2)}) collective-permute-start(f32[256,512]{1,0:T(8,128)S(1)} %slice_select_fusion.2), channel_id=1, source_target_pairs={{0,2},{1,3},{2,0},{3,1},{4,6},{5,7},{6,4},{7,5},{8,10},{9,11},{10,... | collective-permute-start | bytes 1572872 | tf_op jit(solution)/shard_map/ppermute | solution.py:28
  339.9 11.1 %collective-permute-start.35 = (f32[192,512]{1,0:T(8,128)S(1)}, f32[192,512]{1,0:T(8,128)S(1)}, u32[]{:S(2)}, u32[]{:S(2)}) collective-permute-start(f32[192,512]{1,0:T(8,128)S(1)} %get-tuple-element.97), channel_id=1, source_target_pairs={{0,4},{1,5},{2,6},{3,7},{4,0},{5,1},{6,2},{7,3},{8,12},{9,13},{10,... | collective-permute-start | bytes 1179656 | tf_op jit(solution)/shard_map/ppermute | solution.py:28
  341.1 12.8 %collective-permute-start.38 = (f32[192,512]{1,0:T(8,128)S(1)}, f32[192,512]{1,0:T(8,128)S(1)}, u32[]{:S(2)}, u32[]{:S(2)}) collective-permute-start(f32[192,512]{1,0:T(8,128)S(1)} %get-tuple-element.98), channel_id=1, source_target_pairs={{0,8},{1,9},{2,10},{3,11},{4,12},{5,13},{6,14},{7,15},{8,0},{9,1},... | collective-permute-start | bytes 1179656 | tf_op jit(solution)/shard_map/ppermute | solution.py:28
  342.1 57.9 %collective-permute-start.19 = (f32[256,512]{1,0:T(8,128)S(1)}, f32[256,512]{1,0:T(8,128)S(1)}, u32[]{:S(2)}, u32[]{:S(2)}) collective-permute-start(f32[256,512]{1,0:T(8,128)S(1)} %slice_select_fusion.3), channel_id=1, source_target_pairs={{0,2},{1,3},{2,0},{3,1},{4,6},{5,7},{6,4},{7,5},{8,10},{9,11},{10,... | collective-permute-start | bytes 1572872 | tf_op jit(solution)/shard_map/ppermute | solution.py:28
  351.0 40.4 %collective-permute-start.13 = (f32[192,512]{1,0:T(8,128)S(1)}, f32[192,512]{1,0:T(8,128)S(1)}, u32[]{:S(2)}, u32[]{:S(2)}) collective-permute-start(f32[192,512]{1,0:T(8,128)S(1)} %get-tuple-element.93), channel_id=1, source_target_pairs={{0,4},{1,5},{2,6},{3,7},{4,0},{5,1},{6,2},{7,3},{8,12},{9,13},{10,... | collective-permute-start | bytes 1179656 | tf_op jit(solution)/shard_map/ppermute | solution.py:28
  353.9 38.2 %collective-permute-start.16 = (f32[192,512]{1,0:T(8,128)S(1)}, f32[192,512]{1,0:T(8,128)S(1)}, u32[]{:S(2)}, u32[]{:S(2)}) collective-permute-start(f32[192,512]{1,0:T(8,128)S(1)} %get-tuple-element.94), channel_id=1, source_target_pairs={{0,8},{1,9},{2,10},{3,11},{4,12},{5,13},{6,14},{7,15},{8,0},{9,1},... | collective-permute-start | bytes 1179656 | tf_op jit(solution)/shard_map/ppermute | solution.py:28
  355.5 23.9 %collective-permute-start.39 = (f32[96,512]{1,0:T(8,128)S(1)}, f32[96,512]{1,0:T(8,128)S(1)}, u32[]{:S(2)}, u32[]{:S(2)}) collective-permute-start(f32[96,512]{1,0:T(8,128)S(1)} %slice_select_fusion.12), channel_id=1, source_target_pairs={{0,2},{1,3},{2,0},{3,1},{4,6},{5,7},{6,4},{7,5},{8,10},{9,11},{10,... | collective-permute-start | bytes 589832 | tf_op jit(solution)/shard_map/ppermute | solution.py:28
  379.4 10.5 %collective-permute-start.36 = (f32[96,512]{1,0:T(8,128)S(1)}, f32[96,512]{1,0:T(8,128)S(1)}, u32[]{:S(2)}, u32[]{:S(2)}) collective-permute-start(f32[96,512]{1,0:T(8,128)S(1)} %slice_select_fusion.13), channel_id=1, source_target_pairs={{0,8},{1,9},{2,10},{3,11},{4,12},{5,13},{6,14},{7,15},{8,0},{9,1},... | collective-permute-start | bytes 589832 | tf_op jit(solution)/shard_map/ppermute | solution.py:28
  389.9 11.9 %collective-permute-start.42 = (f32[128,512]{1,0:T(8,128)S(1)}, f32[128,512]{1,0:T(8,128)S(1)}, u32[]{:S(2)}, u32[]{:S(2)}) collective-permute-start(f32[128,512]{1,0:T(8,128)S(1)} %slice_select_fusion.9), channel_id=1, source_target_pairs={{0,4},{1,5},{2,6},{3,7},{4,0},{5,1},{6,2},{7,3},{8,12},{9,13},{10,... | collective-permute-start | bytes 786440 | tf_op jit(solution)/shard_map/ppermute | solution.py:28
  392.1 7.0 %collective-permute-start.37 = (f32[48,512]{1,0:T(8,128)S(1)}, f32[48,512]{1,0:T(8,128)S(1)}, u32[]{:S(2)}, u32[]{:S(2)}) collective-permute-start(f32[48,512]{1,0:T(8,128)S(1)} %slice_select_fusion.20), channel_id=1, source_target_pairs={{0,2},{1,3},{2,0},{3,1},{4,6},{5,7},{6,4},{7,5},{8,10},{9,11},{10,... | collective-permute-start | bytes 294920 | tf_op jit(solution)/shard_map/ppermute | solution.py:28
  399.1 8.9 %collective-permute-start.14 = (f32[96,512]{1,0:T(8,128)S(1)}, f32[96,512]{1,0:T(8,128)S(1)}, u32[]{:S(2)}, u32[]{:S(2)}) collective-permute-start(f32[96,512]{1,0:T(8,128)S(1)} %slice_select_fusion.15), channel_id=1, source_target_pairs={{0,8},{1,9},{2,10},{3,11},{4,12},{5,13},{6,14},{7,15},{8,0},{9,1},... | collective-permute-start | bytes 589832 | tf_op jit(solution)/shard_map/ppermute | solution.py:28
  400.2 12.5 %collective-permute-start.20 = (f32[128,512]{1,0:T(8,128)S(1)}, f32[128,512]{1,0:T(8,128)S(1)}, u32[]{:S(2)}, u32[]{:S(2)}) collective-permute-start(f32[128,512]{1,0:T(8,128)S(1)} %slice_select_fusion.10), channel_id=1, source_target_pairs={{0,4},{1,5},{2,6},{3,7},{4,0},{5,1},{6,2},{7,3},{8,12},{9,13},{10,... | collective-permute-start | bytes 786440 | tf_op jit(solution)/shard_map/ppermute | solution.py:28
  401.9 7.5 %collective-permute-start.43 = (f32[64,512]{1,0:T(8,128)S(1)}, f32[64,512]{1,0:T(8,128)S(1)}, u32[]{:S(2)}, u32[]{:S(2)}) collective-permute-start(f32[64,512]{1,0:T(8,128)S(1)} %slice_select_fusion.16), channel_id=1, source_target_pairs={{0,8},{1,9},{2,10},{3,11},{4,12},{5,13},{6,14},{7,15},{8,0},{9,1},... | collective-permute-start | bytes 393224 | tf_op jit(solution)/shard_map/ppermute | solution.py:28
  409.4 9.9 %collective-permute-start.44 = (f32[80,512]{1,0:T(8,128)S(1)}, f32[80,512]{1,0:T(8,128)S(1)}, u32[]{:S(2)}, u32[]{:S(2)}) collective-permute-start(f32[80,512]{1,0:T(8,128)S(1)} %fusion.34), channel_id=1, source_target_pairs={{0,16},{1,17},{2,18},{3,19},{4,20},{5,21},{6,22},{7,23},{8,24},{9,... | collective-permute-start | bytes 491528 | tf_op jit(solution)/shard_map/ppermute | solution.py:28
  412.8 8.4 %collective-permute-start.21 = (f32[64,512]{1,0:T(8,128)S(1)}, f32[64,512]{1,0:T(8,128)S(1)}, u32[]{:S(2)}, u32[]{:S(2)}) collective-permute-start(f32[64,512]{1,0:T(8,128)S(1)} %slice_select_fusion.17), channel_id=1, source_target_pairs={{0,8},{1,9},{2,10},{3,11},{4,12},{5,13},{6,14},{7,15},{8,0},{9,1},... | collective-permute-start | bytes 393224 | tf_op jit(solution)/shard_map/ppermute | solution.py:28
  419.4 11.4 %collective-permute-start.45 = (f32[80,512]{1,0:T(8,128)S(1)}, f32[80,512]{1,0:T(8,128)S(1)}, u32[]{:S(2)}, u32[]{:S(2)}) collective-permute-start(f32[80,512]{1,0:T(8,128)S(1)} %select_add_fusion.16), channel_id=1, source_target_pairs={{0,16},{1,17},{2,18},{3,19},{4,20},{5,21},{6,22},{7,23},{8,24},{9,... | collective-permute-start | bytes 491528 | tf_op jit(solution)/shard_map/ppermute | solution.py:28
  421.3 11.5 %collective-permute-start.22 = (f32[80,512]{1,0:T(8,128)S(1)}, f32[80,512]{1,0:T(8,128)S(1)}, u32[]{:S(2)}, u32[]{:S(2)}) collective-permute-start(f32[80,512]{1,0:T(8,128)S(1)} %fusion.33), channel_id=1, source_target_pairs={{0,16},{1,17},{2,18},{3,19},{4,20},{5,21},{6,22},{7,23},{8,24},{9,... | collective-permute-start | bytes 491528 | tf_op jit(solution)/shard_map/ppermute | solution.py:28
  432.7 7.5 %collective-permute-start.46 = (f32[64,512]{1,0:T(8,128)S(1)}, f32[64,512]{1,0:T(8,128)S(1)}, u32[]{:S(2)}, u32[]{:S(2)}) collective-permute-start(f32[64,512]{1,0:T(8,128)S(1)} %split.32), channel_id=1, source_target_pairs={{0,8},{1,9},{2,10},{3,11},{4,12},{5,13},{6,14},{7,15},{8,0},{9,1},... | collective-permute-start | bytes 393224 | tf_op jit(solution)/shard_map/ppermute | solution.py:28
  432.8 8.4 %collective-permute-start.23 = (f32[80,512]{1,0:T(8,128)S(1)}, f32[80,512]{1,0:T(8,128)S(1)}, u32[]{:S(2)}, u32[]{:S(2)}) collective-permute-start(f32[80,512]{1,0:T(8,128)S(1)} %select_add_fusion.17), channel_id=1, source_target_pairs={{0,16},{1,17},{2,18},{3,19},{4,20},{5,21},{6,22},{7,23},{8,24},{9,... | collective-permute-start | bytes 491528 | tf_op jit(solution)/shard_map/ppermute | solution.py:28
  438.2 7.6 %collective-permute-start.53 = (f32[96,512]{1,0:T(8,128)S(1)}, f32[96,512]{1,0:T(8,128)S(1)}, u32[]{:S(2)}, u32[]{:S(2)}) collective-permute-start(f32[96,512]{1,0:T(8,128)S(1)} %pad_maximum_fusion.18), channel_id=1, source_target_pairs={{0,2},{1,3},{2,0},{3,1},{4,6},{5,7},{6,4},{7,5},{8,10},{9,11},{10,... | collective-permute-start | bytes 589832 | tf_op jit(solution)/shard_map/ppermute | solution.py:28
  440.2 13.8 %collective-permute-start.47 = (f32[128,512]{1,0:T(8,128)S(1)}, f32[128,512]{1,0:T(8,128)S(1)}, u32[]{:S(2)}, u32[]{:S(2)}) collective-permute-start(f32[128,512]{1,0:T(8,128)S(1)} %pad_maximum_fusion.14), channel_id=1, source_target_pairs={{0,4},{1,5},{2,6},{3,7},{4,0},{5,1},{6,2},{7,3},{8,12},{9,13},{10,... | collective-permute-start | bytes 786440 | tf_op jit(solution)/shard_map/ppermute | solution.py:28
  441.1 13.3 %collective-permute-start.50 = (f32[96,512]{1,0:T(8,128)S(1)}, f32[96,512]{1,0:T(8,128)S(1)}, u32[]{:S(2)}, u32[]{:S(2)}) collective-permute-start(f32[96,512]{1,0:T(8,128)S(1)} %pad_maximum_fusion.17), channel_id=1, source_target_pairs={{0,8},{1,9},{2,10},{3,11},{4,12},{5,13},{6,14},{7,15},{8,0},{9,1},... | collective-permute-start | bytes 589832 | tf_op jit(solution)/shard_map/ppermute | solution.py:28
  441.2 10.3 %collective-permute-start.30 = (f32[48,512]{1,0:T(8,128)S(1)}, f32[48,512]{1,0:T(8,128)S(1)}, u32[]{:S(2)}, u32[]{:S(2)}) collective-permute-start(f32[48,512]{1,0:T(8,128)S(1)} %split.31), channel_id=1, source_target_pairs={{0,4},{1,5},{2,6},{3,7},{4,0},{5,1},{6,2},{7,3},{8,12},{9,13},{10,... | collective-permute-start | bytes 294920 | tf_op jit(solution)/shard_map/ppermute | solution.py:28
  451.6 30.2 %collective-permute-start.54 = (f32[192,512]{1,0:T(8,128)S(1)}, f32[192,512]{1,0:T(8,128)S(1)}, u32[]{:S(2)}, u32[]{:S(2)}) collective-permute-start(f32[192,512]{1,0:T(8,128)S(1)} %pad_maximum_fusion.11), channel_id=1, source_target_pairs={{0,8},{1,9},{2,10},{3,11},{4,12},{5,13},{6,14},{7,15},{8,0},{9,1},... | collective-permute-start | bytes 1179656 | tf_op jit(solution)/shard_map/ppermute | solution.py:28
  454.0 8.0 %collective-permute-start.31 = (f32[96,512]{1,0:T(8,128)S(1)}, f32[96,512]{1,0:T(8,128)S(1)}, u32[]{:S(2)}, u32[]{:S(2)}) collective-permute-start(f32[96,512]{1,0:T(8,128)S(1)} %pad_maximum_fusion.16), channel_id=1, source_target_pairs={{0,2},{1,3},{2,0},{3,1},{4,6},{5,7},{6,4},{7,5},{8,10},{9,11},{10,... | collective-permute-start | bytes 589832 | tf_op jit(solution)/shard_map/ppermute | solution.py:28
  454.4 15.1 %collective-permute-start.25 = (f32[128,512]{1,0:T(8,128)S(1)}, f32[128,512]{1,0:T(8,128)S(1)}, u32[]{:S(2)}, u32[]{:S(2)}) collective-permute-start(f32[128,512]{1,0:T(8,128)S(1)} %pad_maximum_fusion.13), channel_id=1, source_target_pairs={{0,4},{1,5},{2,6},{3,7},{4,0},{5,1},{6,2},{7,3},{8,12},{9,13},{10,... | collective-permute-start | bytes 786440 | tf_op jit(solution)/shard_map/ppermute | solution.py:28
  457.8 22.0 %collective-permute-start.51 = (f32[192,512]{1,0:T(8,128)S(1)}, f32[192,512]{1,0:T(8,128)S(1)}, u32[]{:S(2)}, u32[]{:S(2)}) collective-permute-start(f32[192,512]{1,0:T(8,128)S(1)} %pad_maximum_fusion.10), channel_id=1, source_target_pairs={{0,4},{1,5},{2,6},{3,7},{4,0},{5,1},{6,2},{7,3},{8,12},{9,13},{10,... | collective-permute-start | bytes 1179656 | tf_op jit(solution)/shard_map/ppermute | solution.py:28
  467.7 10.5 %collective-permute-start.48 = (f32[256,512]{1,0:T(8,128)S(1)}, f32[256,512]{1,0:T(8,128)S(1)}, u32[]{:S(2)}, u32[]{:S(2)}) collective-permute-start(f32[256,512]{1,0:T(8,128)S(1)} %pad_maximum_fusion.6), channel_id=1, source_target_pairs={{0,2},{1,3},{2,0},{3,1},{4,6},{5,7},{6,4},{7,5},{8,10},{9,11},{10,... | collective-permute-start | bytes 1572872 | tf_op jit(solution)/shard_map/ppermute | solution.py:28
  469.6 22.9 %collective-permute-start.32 = (f32[192,512]{1,0:T(8,128)S(1)}, f32[192,512]{1,0:T(8,128)S(1)}, u32[]{:S(2)}, u32[]{:S(2)}) collective-permute-start(f32[192,512]{1,0:T(8,128)S(1)} %pad_maximum_fusion.9), channel_id=1, source_target_pairs={{0,8},{1,9},{2,10},{3,11},{4,12},{5,13},{6,14},{7,15},{8,0},{9,1},... | collective-permute-start | bytes 1179656 | tf_op jit(solution)/shard_map/ppermute | solution.py:28
  478.2 12.6 %collective-permute-start.29 = (f32[192,512]{1,0:T(8,128)S(1)}, f32[192,512]{1,0:T(8,128)S(1)}, u32[]{:S(2)}, u32[]{:S(2)}) collective-permute-start(f32[192,512]{1,0:T(8,128)S(1)} %pad_maximum_fusion.8), channel_id=1, source_target_pairs={{0,4},{1,5},{2,6},{3,7},{4,0},{5,1},{6,2},{7,3},{8,12},{9,13},{10,... | collective-permute-start | bytes 1179656 | tf_op jit(solution)/shard_map/ppermute | solution.py:28
  479.9 9.2 %collective-permute-start.26 = (f32[256,512]{1,0:T(8,128)S(1)}, f32[256,512]{1,0:T(8,128)S(1)}, u32[]{:S(2)}, u32[]{:S(2)}) collective-permute-start(f32[256,512]{1,0:T(8,128)S(1)} %pad_maximum_fusion.5), channel_id=1, source_target_pairs={{0,2},{1,3},{2,0},{3,1},{4,6},{5,7},{6,4},{7,5},{8,10},{9,11},{10,... | collective-permute-start | bytes 1572872 | tf_op jit(solution)/shard_map/ppermute | solution.py:28
  481.9 21.7 %collective-permute-start.55 = (f32[1280,512]{1,0:T(8,128)S(1)}, f32[1280,512]{1,0:T(8,128)}, u32[]{:S(2)}, u32[]{:S(2)}) collective-permute-start(f32[1280,512]{1,0:T(8,128)S(1)} %select_dynamic-update-slice_fusion.4), channel_id=1, source_target_pairs={{0,1},{1,0},{2,3},{3,2},{4,5},{5,4},{6,7},{7,6},{8,9},{9,8},{10,11... | collective-permute-start | bytes 7864328 | tf_op jit(solution)/shard_map/ppermute | solution.py:28
  494.1 12.6 %collective-permute-start.33 = (f32[1280,512]{1,0:T(8,128)}, f32[1280,512]{1,0:T(8,128)}, u32[]{:S(2)}, u32[]{:S(2)}) collective-permute-start(f32[1280,512]{1,0:T(8,128)} %select_dynamic-update-slice_fusion.8), channel_id=1, source_target_pairs={{0,1},{1,0},{2,3},{3,2},{4,5},{5,4},{6,7},{7,6},{8,9},{9,8},{10,11... | collective-permute-start | bytes 7864328 | tf_op jit(solution)/shard_map/ppermute | solution.py:28
  (65 other events, 727.3 us)
Sparse Core Ops, SparseCore 0:
  221.4 178.7 all-reduce.13

commit v3 on v1

v3 whole, which is shorter than its diff:
```python
import functools

import jax
import jax.numpy as jnp
from jax import lax
from jax.experimental import pallas as pl
from jax.experimental.pallas import tpu as pltpu
from jax.sharding import PartitionSpec as P

AXES = ("dp", "tm")
EDGE = 24
PAD = 8
F32 = jnp.float32
BF16 = jnp.bfloat16
NN = ((1,), (0,))
NT = ((1,), (1,))
TN = ((0,), (0,))
WHOLE = pl.BlockSpec(memory_space=pltpu.VMEM)
FAR = pl.BlockSpec(memory_space=pltpu.HBM)
SCALARS = pl.BlockSpec(memory_space=pltpu.SMEM)


def split(value):
    high = value.astype(BF16)
    return high, (value - high.astype(F32)).astype(BF16)


def product(left, right, dims):
    def one(a, b):
        return lax.dot_general(a, b, (dims, ((), ())), preferred_element_type=F32)

    return one(left[0], right[0]) + (one(left[0], right[1]) + one(left[1], right[0]))


def sum_over_devices(ref):
    return jnp.sum(ref[...], axis=0)


def masks(meta_ref, shape, batch, span):
    rows, own = [], []
    for b in range(batch):
        local = lax.broadcasted_iota(jnp.int32, (span, shape[1]), 0) - EDGE
        position = local + meta_ref[batch]
        live = (position >= 0) & (position < meta_ref[b])
        rows.append(live)
        own.append(live & (local >= 0) & (local < span - 2 * EDGE))
    return jnp.concatenate(rows, axis=0), jnp.concatenate(own, axis=0)


def put_copies(ref, rows):
    ref[...] = jnp.broadcast_to(jnp.concatenate(rows, axis=0)[None], ref.shape)


def column_sum(value):
    return jnp.sum(value, axis=0, keepdims=True)


def fetch(refs, names):
    copies = {n: pltpu.make_async_copy(refs[n], refs[n + "_here"], refs["sem_" + n]) for n in names}
    for copy in copies.values():
        copy.start()

    def get(name):
        copies[name].wait()
        return refs[name + "_here"][...]

    return get


def fetch_scratch(arrays):
    scratch = {}
    for name, array in arrays.items():
        scratch[name + "_here"] = pltpu.VMEM(array.shape, F32)
        scratch["sem_" + name] = pltpu.SemaphoreType.DMA
    return scratch


def weight_copy(layer, refs, k):
    source = refs["w"] if layer is None else refs["w"].at[layer]
    return pltpu.make_async_copy(source.at[k], refs["w_here"].at[k], refs["arrived"].at[k])


def fetch_weights(layer, refs):
    for k in range(refs["w_here"].shape[0]):
        weight_copy(layer, refs, k).start()


def taps(out_ref, layer, refs, value, step, dims):
    rows = value.shape[0]
    w_ref, padded_ref, high_ref, low_ref = (refs[n] for n in ("w_here", "padded", "high", "low"))
    width = w_ref.shape[0]
    edge = jnp.zeros((PAD, value.shape[1]), F32)
    padded_ref[0:PAD, :] = edge
    padded_ref[PAD : PAD + rows, :] = value
    padded_ref[PAD + rows : PAD + rows + PAD, :] = edge
    for k in range(width):
        start = PAD + step * (k - width // 2)
        high_ref[k], low_ref[k] = split(padded_ref[start : start + rows, :])
    out_ref[...] = jnp.zeros(out_ref.shape, F32)

    def tap(k, carry):
        weight_copy(layer, refs, k).wait()
        out_ref[...] += product((high_ref[k], low_ref[k]), split(w_ref[k]), dims)
        return carry

    lax.fori_loop(0, width, tap, 0)


def tap_scratch(rows, dims, contracted):
    wide = (dims[0], rows, contracted)
    return dict(
        padded=pltpu.VMEM((rows + 2 * PAD, contracted), F32), high=pltpu.VMEM(wide, BF16), low=pltpu.VMEM(wide, BF16),
        w_here=pltpu.VMEM(dims, F32), arrived=pltpu.SemaphoreType.DMA((dims[0],)),
    )


def normalizer(sums, inverse):
    mean = sums[0:1] * inverse
    return mean, lax.rsqrt(sums[1:2] * inverse - mean * mean + 1e-05)


def first_forward(batch, refs):
    fetch_weights(None, refs)
    meta_ref, mel_ref, cot_ref, before_ref, after_ref, h_ref, copies_ref, mel_ext_ref, cot_ext_ref = (
        refs[n] for n in ("meta", "mel", "cot", "before", "after", "h", "copies", "mel_ext", "cot_ext")
    )
    frames = mel_ref.shape[1]
    span = frames + 2 * EDGE
    for b in range(batch):
        base = b * span
        for i, (ref, out) in enumerate(((mel_ref, mel_ext_ref), (cot_ref, cot_ext_ref))):
            out[base : base + EDGE, :] = before_ref[i, b]
            out[base + EDGE : base + EDGE + frames, :] = ref[b]
            out[base + EDGE + frames : base + span, :] = after_ref[i, b]
    taps(h_ref, None, refs, mel_ext_ref[...], 1, NN)
    h = h_ref[...]
    _, own = masks(meta_ref, h.shape, batch, span)
    h = jnp.where(own, h, 0.0)
    put_copies(copies_ref, [column_sum(h), column_sum(h * h), column_sum(own.astype(F32))])


def forward(batch, layer, last, refs):
    fetch_weights(layer, refs)
    meta_ref, h_in_ref, sums_ref, gain_ref, bias_ref, h_ref, copies_ref, x_ref, stats_ref = (
        refs[n] for n in ("meta", "h_in", "sums", "gain", "bias", "h", "copies", "x", "stats")
    )
    span = h_in_ref.shape[0] // batch
    sums = sum_over_devices(sums_ref)
    count = refs["count"][...] if "count" in refs else sums[2:3]
    mean, rstd = normalizer(sums, 1.0 / count)
    stats_ref[0:1, :] = mean
    stats_ref[1:2, :] = rstd
    stats_ref[2:3, :] = count
    h = h_in_ref[...]
    live, own = masks(meta_ref, h.shape, batch, span)
    x = jnp.where(live, jnp.tanh((h - mean) * rstd * gain_ref[...] + bias_ref[...]), 0.0)
    x_ref[...] = x
    taps(h_ref, layer, refs, x, 1, NT if last else NN)
    h = h_ref[...]
    _, own = masks(meta_ref, h.shape, batch, span)
    h = jnp.where(own, h, 0.0)
    sums = [column_sum(h), column_sum(h * h)]
    if last:
        cot = jnp.where(own, refs["cot"][...], 0.0)
        sums += [column_sum(cot), column_sum(h * cot)]
    put_copies(copies_ref, sums)


def backward(batch, layer, kind, refs):
    get = fetch(refs, ["h"])
    fetch_weights(layer, refs)
    get_below = None if kind == "first" else fetch(refs, ["x", "below_h"])
    meta_ref, sums_ref, h_ref, gz_ref, stats_ref, gain_ref = (
        refs[n] for n in ("meta", "sums", "h", "gz", "stats", "gain")
    )
    rows = h_ref.shape[0]
    span = rows // batch
    frames = span - 2 * EDGE
    channels = h_ref.shape[1]
    sums = sum_over_devices(sums_ref)
    inverse = 1.0 / stats_ref[2:3, :channels]
    if kind == "last":
        mean, rstd = normalizer(sums, inverse)
        shift = sums[2:3]
        gain = rstd * (sums[3:4] - mean * shift)
    else:
        mean, rstd = stats_ref[0:1, :], stats_ref[1:2, :]
        gain, shift = sums[0:1], sums[1:2]
    refs["param_grads"][0:1, :] = gain
    refs["param_grads"][1:2, :] = shift
    live, _ = masks(meta_ref, h_ref.shape, batch, span)
    normed = (get("h") - mean) * rstd
    if kind == "last":
        x = jnp.where(live, normed * gain_ref[...] + refs["bias"][...], 0.0)
        for b in range(batch):
            at = b * span + EDGE
            refs["mel_after"][b] = refs["mel"][b] + x[at : at + frames]
    gz = gz_ref[...]
    dh = rstd * gain_ref[...] * (gz - shift * inverse - normed * (gain * inverse))
    dh = jnp.where(live, dh, 0.0)
    refs["dh"][...] = dh
    e_ref = refs["e"]
    taps(e_ref, layer, refs, dh, -1, NN if kind == "last" else NT)
    if kind == "first":
        for b in range(batch):
            at = b * span + EDGE
            refs["grad_mel"][b] = refs["cot"][b] + e_ref[at : at + frames, :]
        return
    live, own = masks(meta_ref, e_ref.shape, batch, span)
    x = get_below("x")
    gz = jnp.where(live, e_ref[...] * (1.0 - x * x), 0.0)
    refs["gz_out"][...] = gz
    below = refs["below_stats"]
    normed = (get_below("below_h") - below[0:1, :]) * below[1:2, :]
    gz = jnp.where(own, gz, 0.0)
    put_copies(refs["copies"], [column_sum(gz * normed), column_sum(gz)])


def weight_gradient(batch, turned, refs):
    get = fetch(refs, ["x"])
    dh_ref, shifted_ref = refs["dh"], refs["shifted"]
    span = dh_ref.shape[0] // batch
    frames = span - 2 * EDGE
    width = shifted_ref.shape[0]
    dh = jnp.concatenate([dh_ref[b * span + EDGE : b * span + EDGE + frames, :] for b in range(batch)], axis=0)
    dh = split(dh.T if turned else dh)
    get("x")
    for k in range(width):
        for b in range(batch):
            start = b * span + EDGE + k - width // 2
            shifted_ref[k, b * frames : (b + 1) * frames] = refs["x_here"][start : start + frames, :]
    upper = refs["meta"][batch + 1] == 1

    def tap(k, carry):
        if turned:
            dw = product(dh, split(shifted_ref[k]), NN)
        else:
            dw = product(split(shifted_ref[k].T), dh, NN)
        if "whole" in refs:
            refs["whole"][k] = dw
        else:
            half = refs["mine"].shape[1]
            refs["mine"][k] = jnp.where(upper, dw[half:], dw[:half])
            refs["other"][k] = jnp.where(upper, dw[:half], dw[half:])
        return carry

    lax.fori_loop(0, width, tap, 0)


def place_whole(index, refs):
    copy = pltpu.make_async_copy(refs["value"], refs["out"].at[index], refs["sem"])
    copy.start()
    copy.wait()


def place(index, refs):
    meta_ref, mine_ref, other_ref, sems, out_ref = (refs[n] for n in ("meta", "mine", "other", "sems", "out"))
    half = mine_ref.shape[1]
    target = out_ref if index is None else out_ref.at[index]
    upper = meta_ref[meta_ref.shape[0] - 1]
    first = pltpu.make_async_copy(mine_ref, target.at[:, pl.ds(upper * half, half)], sems.at[0])
    second = pltpu.make_async_copy(other_ref, target.at[:, pl.ds((1 - upper) * half, half)], sems.at[1])
    first.start()
    second.start()
    first.wait()
    second.wait()


def shape(*dims):
    return jax.ShapeDtypeStruct(dims, F32)


def call(body, name, ins, outs, scratch, flops, far=("w",), far_outs=(), alias=None):
    names = list(ins) + list(outs) + list(scratch)

    def kernel(*refs):
        body(dict(zip(names, refs)))

    size = sum(4 * v.size for v in list(ins.values()) + list(outs.values()))
    results = pl.pallas_call(
        kernel,
        name=name,
        out_shape=list(outs.values()),
        in_specs=[SCALARS if n == "meta" else FAR if n in far else WHOLE for n in ins],
        out_specs=[FAR if n in far_outs else WHOLE for n in outs],
        input_output_aliases={} if alias is None else {list(ins).index(alias[0]): list(outs).index(alias[1])},
        scratch_shapes=list(scratch.values()),
        cost_estimate=pl.CostEstimate(flops=flops, bytes_accessed=size if flops else 0, transcendentals=0),
        compiler_params=pltpu.CompilerParams(vmem_limit_bytes=50 * 2**20),
    )(*ins.values())
    return dict(zip(outs, results))


def edges(mel, cotangent):
    count = lax.axis_size("tm")
    up = [(i, i + 1) for i in range(count - 1)]
    down = [(j, i) for i, j in up]
    low = lax.ppermute(jnp.stack([mel[:, -EDGE:], cotangent[:, -EDGE:]]), "tm", up)
    high = lax.ppermute(jnp.stack([mel[:, :EDGE], cotangent[:, :EDGE]]), "tm", down)
    return low, high


def to_all(copies):
    return lax.all_to_all(copies, AXES, 0, 0)


def swap(x, bit):
    devices = lax.axis_size(AXES)
    return lax.ppermute(x, AXES, [(i, i ^ (1 << bit)) for i in range(devices)])


def upper_half(bit):
    return ((lax.axis_index(AXES) >> bit) & 1) == 1


def halve(x, bit):
    half = x.shape[0] // 2
    upper = upper_half(bit)
    low, high = x[:half], x[half:]
    return jnp.where(upper, high, low) + swap(jnp.where(upper, low, high), bit)


def double(x, bit):
    upper = upper_half(bit)
    other = swap(x, bit)
    return jnp.concatenate([jnp.where(upper, other, x), jnp.where(upper, x, other)], axis=0)


def assemble(parts, sizes):
    rows = sum(p.shape[0] for p in parts)
    spare = sum(sizes) - rows
    parts = list(parts)
    if spare:
        parts.append(jnp.zeros((spare, parts[0].shape[1]), F32))
    groups, start = [], 0
    for size in sizes:
        pieces, at = [], 0
        for p in parts:
            low, high = max(start, at), min(start + size, at + p.shape[0])
            if low < high:
                pieces.append(p[low - at : high - at])
            at += p.shape[0]
        groups.append(pieces[0] if len(pieces) == 1 else jnp.concatenate(pieces))
        start += size
    return groups


class Exchange:
    def __init__(self, pairs, sizes):
        bits = (lax.axis_size(AXES) - 1).bit_length()
        near = list(range(1, 1 + len(sizes)))
        orders = [near[i:] + near[:i] for i in range(len(sizes))]
        rest = list(range(1 + len(sizes), bits))
        marks = [s >> len(near) for s in sizes]
        self.state = [m for m, _ in pairs] + [o for _, o in pairs]
        count = len(pairs)
        self.steps = [lambda s: assemble([m + swap(o, 0) for m, o in zip(s[:count], s[count:])], sizes)]
        for turn in range(len(near)):
            self.steps.append(lambda s, turn=turn: [halve(g, order[turn]) for g, order in zip(s, orders)])
        for i, bit in enumerate(rest):
            self.steps.append(lambda s, bit=bit: [halve(jnp.concatenate(s), bit)])
        for bit in reversed(rest):
            self.steps.append(lambda s, bit=bit: [double(s[0], bit)])
        for turn in reversed(range(len(near))):
            first = turn == len(near) - 1 and bool(rest)
            self.steps.append(
                lambda s, turn=turn, first=first: [
                    double(g, order[turn]) for g, order in zip(assemble(s, marks) if first else s, orders)
                ]
            )

        def finish(s):
            x = jnp.concatenate(s)
            return [x, swap(x, 0)]

        self.steps.append(finish)

    def advance(self):
        if self.steps:
            self.state = self.steps.pop(0)(self.state)


def tie(value, exchanges):
    states = [e.state for e in exchanges]
    value, states = lax.optimization_barrier((value, states))
    for e, state in zip(exchanges, states):
        e.state = state
    return value


def shards(
    mel, cotangent, lengths, w_first, w_mid, w_last, gain_hidden, bias_hidden, gain_last, bias_last
):
    batch, frames, mels = mel.shape
    width, channels = w_first.shape[0], w_first.shape[2]
    rows = batch * (frames + 2 * EDGE)
    devices = lax.axis_size(AXES)
    meta = jnp.concatenate([lengths, jnp.stack([lax.axis_index("tm") * frames, lax.axis_index(AXES) & 1]).astype(jnp.int32)])
    before, after = edges(mel, cotangent)
    weights = [(w_first, None, w_first.shape)]
    weights += [(w_mid, i, w_mid.shape[1:]) for i in range(w_mid.shape[0])]
    w_turned = w_last.transpose(0, 2, 1)
    weights += [(w_turned, None, w_turned.shape)]
    wide = [channels] * 4 + [mels]
    gains = [gain_hidden[i : i + 1] for i in range(4)] + [gain_last[None]]
    biases = [bias_hidden[i : i + 1] for i in range(4)] + [bias_last[None]]

    def work(dims):
        return 6 * rows * dims[0] * dims[1] * dims[2]

    out = call(
        functools.partial(first_forward, batch), "forward_first",
        dict(meta=meta, mel=mel, cot=cotangent, before=before, after=after, w=w_first),
        dict(h=shape(rows, channels), copies=shape(devices, 3, channels), mel_ext=shape(rows, mels), cot_ext=shape(rows, mels)),
        tap_scratch(rows, w_first.shape, mels), work(w_first.shape),
    )
    mel_ext, cot_ext = out["mel_ext"], out["cot_ext"]
    h = [out["h"]]
    x = [mel_ext]
    stats = []
    count = None
    gathered = to_all(out["copies"])
    for layer in range(1, 5):
        last = layer == 4
        weight, index, dims = weights[layer]
        ins = dict(meta=meta, h_in=h[-1], sums=gathered, gain=gains[layer - 1], bias=biases[layer - 1], w=weight)
        if count is not None:
            ins["count"] = count
        if last:
            ins["cot"] = cot_ext
        out = call(
            functools.partial(forward, batch, index, last), "forward",
            ins,
            dict(h=shape(rows, wide[layer]), copies=shape(devices, 4 if last else 2, wide[layer]),
                 x=shape(rows, channels), stats=shape(3, channels)),
            tap_scratch(rows, dims, channels), work(dims),
        )
        h.append(out["h"])
        x.append(out["x"])
        stats.append(out["stats"])
        if count is None:
            count = out["stats"][2:3]
        gathered = to_all(out["copies"])
    gz = cot_ext
    param_grads = [None] * 5
    exchanges = []
    for layer in range(4, -1, -1):
        kind = "last" if layer == 4 else "first" if layer == 0 else "inner"
        weight, index, dims = weights[layer]
        above, below = wide[layer], wide[layer - 1] if layer else mels
        ins = dict(meta=meta, sums=gathered, h=h[layer], gz=gz, stats=stats[min(layer, 3)], gain=gains[layer], w=weight)
        outs = dict(dh=shape(rows, above), param_grads=shape(2, above))
        scratch = dict(tap_scratch(rows, dims, above), e=pltpu.VMEM((rows, below), F32))
        far = dict(h=h[layer])
        if kind == "last":
            ins.update(bias=biases[layer], mel=mel)
            outs.update(mel_after=shape(*mel.shape))
        if kind == "first":
            ins.update(cot=cotangent)
            outs.update(grad_mel=shape(*mel.shape))
        else:
            ins.update(x=x[layer], below_h=h[layer - 1], below_stats=stats[layer - 1])
            far.update(x=x[layer], below_h=h[layer - 1])
            outs.update(gz_out=shape(rows, below), copies=shape(devices, 2, below))
        scratch.update(fetch_scratch(far))
        out = call(functools.partial(backward, batch, index, kind), "backward", ins, outs, scratch, 0, far=("w", *far))
        param_grads[layer] = out["param_grads"]
        if kind == "last":
            mel_after = out["mel_after"]
        if kind == "first":
            grad_mel = out["grad_mel"]
        else:
            gz = out["gz_out"]
            gathered = to_all(out["copies"])

        for e in exchanges:
            e.advance()
        dh = tie(out["dh"], exchanges)
        if layer >= 3:
            pieces = dict(whole=shape(*dims))
        else:
            pieces = dict(mine=shape(dims[0], dims[1] // 2, dims[2]), other=shape(dims[0], dims[1] // 2, dims[2]))
        pieces = call(
            functools.partial(weight_gradient, batch, kind == "last"), "weight_gradient",
            dict(meta=meta, x=x[layer], dh=dh), pieces,
            dict(shifted=pltpu.VMEM((width, batch * frames, below), F32), **fetch_scratch(dict(x=x[layer]))), 0, far=("x",),
        )
        for e in exchanges:
            e.advance()
        pieces = [v.reshape(-1, channels) if layer < 3 else v for v in pieces.values()]
        if layer == 4:
            held = pieces[0]
            gathered, held = lax.optimization_barrier((gathered, held))
        elif layer == 3:
            gathered, whole = lax.optimization_barrier((gathered, pieces[0]))
            summed = lax.psum((whole, held), AXES)
        elif layer == 2:
            tile = pieces[0].shape[0] // 10
            exchanges.append(Exchange([pieces], [4 * tile, 3 * tile, 3 * tile]))
            gathered = tie(gathered, exchanges)
        elif layer == 1:
            held = pieces
            gathered, held = lax.optimization_barrier((gathered, held))
            gathered = tie(gathered, exchanges)
        else:
            rows_all = held[0].shape[0] + pieces[0].shape[0]
            exchanges.append(Exchange([held, pieces], [-(-rows_all // 192) * 64] * 3))
    early, late = exchanges
    while late.steps:
        late.advance()
        early.advance()
        early.state, _ = lax.optimization_barrier((early.state, late.state))
    half = channels // 2
    mid = (width, half, channels)
    small = (width, mels // 2, channels)
    mid_rows, small_rows = width * half, width * mels // 2
    grad_w_mid = call(
        functools.partial(place_whole, 2), "place_whole", dict(value=summed[0]), dict(out=shape(*w_mid.shape)),
        dict(sem=pltpu.SemaphoreType.DMA), 0, far=(), far_outs=("out",),
    )["out"]
    for index, e in ((1, exchanges[0]), (0, exchanges[1])):
        grad_w_mid = call(
            functools.partial(place, index), "place",
            dict(meta=meta, mine=e.state[0][:mid_rows].reshape(mid), other=e.state[1][:mid_rows].reshape(mid), before=grad_w_mid),
            dict(out=shape(*w_mid.shape)), dict(sems=pltpu.SemaphoreType.DMA((2,))), 0,
            far=("before",), far_outs=("out",), alias=("before", "out"),
        )["out"]
    mine, other = (v[mid_rows : mid_rows + small_rows].reshape(small) for v in exchanges[1].state)
    upper = upper_half(0)
    grad_w_first = jnp.concatenate([jnp.where(upper, other, mine), jnp.where(upper, mine, other)], axis=1)
    return (
        mel_after,
        grad_mel,
        grad_w_first,
        grad_w_mid,
        summed[1].transpose(0, 2, 1),
        jnp.concatenate([p[0:1] for p in param_grads[:4]]),
        jnp.concatenate([p[1:2] for p in param_grads[:4]]),
        param_grads[4][0],
        param_grads[4][1],
    )


def solution(mesh):
    return jax.shard_map(
        shards,
        mesh=mesh,
        in_specs=(P("dp", "tm", None), P("dp", "tm", None), P("dp")) + (P(),) * 7,
        out_specs=(P("dp", "tm", None), P("dp", "tm", None)) + (P(),) * 7,
        check_vma=False,
    )
```

time: 605 us -> 473 us (0.78)
  waiting for transfers between devices: 303 us -> 141 us
  Pallas kernels: 0 us -> 145 us
  matrix products: 97.8 us -> 0 us
  local copies, waits for them, and re-layouts: 84.4 us -> 32.7 us
  starting transfers between devices: 47.1 us -> 77.2 us
  blocking collectives: 10.6 us -> 29.3 us
  other arithmetic: 38.2 us -> 23.3 us
    psum x1, waiting for transfers between devices: 284 us -> 0.02 us  [shards(): summed = lax.psum((whole, held), AXES)]
    pallas_call x0 -> x18, Pallas kernels: none -> 145 us  [call(): pl.pallas_call(kernel, name=name, out_shape=list(outs.values()), in_specs...]
    ppermute x2 -> x47, waiting for transfers between devices: 0.01 us -> 120 us  [the longest x45 116 us: swap(): return lax.ppermute(x, AXES, [(i, i ^ 1 << bit) for i in range(devices)])]
    dot_general x15 -> x0, matrix products: 97.8 us -> none  [the longest x5 37.6 us: shards(): weight_grads[layer] = jnp.dot(x_wide.T, own * d_pre, precision=HIGH)]
    ppermute x2 -> x47, starting transfers between devices: 3.7 us -> 48.9 us  [the longest x45 45.2 us: swap(): return lax.ppermute(x, AXES, [(i, i ^ 1 << bit) for i in range(devices)])]
    transpose x7 -> x0, local copies, waits for them, and re-layouts: 34.3 us -> none  [shards(): jnp.transpose(weight[::-1], (0, 2, 1)).reshape(-1, weight.shape[1])]
    all_to_all x1 -> x3, blocking collectives: 10.6 us -> 29.3 us  [to_all(): return lax.all_to_all(copies, AXES, 0, 0)]
    mul x10 -> x0, other arithmetic: 15.6 us -> none  [the longest x5 13.3 us: shards(): mask * rstd * gains[layer]]
  transfers between devices with their start and end apart: 11 -> 54, of which waited for: 4 -> 26; matrix products, arithmetic and copies ran while one was open for 17% -> 5% of each run, Pallas kernels for 0% -> 13%
where the time goes in v3:
time: 473 us; the launch traced here: 464 us
  Pallas kernels  145 us (31%)
  waiting for transfers between devices  141 us (30%)
  starting transfers between devices  77.2 us (16%)
  local copies, waits for them, and re-layouts  32.7 us (7%)
  blocking collectives  29.3 us (6%)
  other arithmetic  23.3 us (5%)
  between operations  15.6 us (3%)
    pallas_call x18, Pallas kernels, call(): pl.pallas_call(kernel, name=name, out_shape=list(outs.values()), in_specs...  145 us
    ppermute x45, waiting for transfers between devices, swap(): return lax.ppermute(x, AXES, [(i, i ^ 1 << bit) for i in range(devices)])  116 us
    ppermute x45, starting transfers between devices, swap(): return lax.ppermute(x, AXES, [(i, i ^ 1 << bit) for i in range(devices)])  45.2 us
    all_to_all x3, blocking collectives, to_all(): return lax.all_to_all(copies, AXES, 0, 0)  29.3 us
    all_to_all x6, starting transfers between devices, to_all(): return lax.all_to_all(copies, AXES, 0, 0)  28.1 us
    unnamed x101, local copies, waits for them, and re-layouts  28.1 us
    all_to_all x6, waiting for transfers between devices, to_all(): return lax.all_to_all(copies, AXES, 0, 0)  21.6 us
  transfers between devices with their start and end apart: 54, of which 26 were waited for; matrix products, arithmetic and copies ran while one was open for 5% of the time, Pallas kernels for 13%

profile of v3, /device:TPU:0, one launch (start us, length us, event | category | flops | bytes accessed | tf_op | source)
XLA Modules:
  0.0 464.1 jit_solution(11321834909346791654)
XLA Ops:
  13.8 3.2 collective-permute-done.1.refs_4_
  18.1 6.3 %forward_first.1 = (f32[608,512]{1,0:T(8,128)S(1)}, f32[32,3,512]{2,1,0:T(4,128)}, f32[608,80]{1,0:T(8,128)S(1)}, f32[608,80]{1,0:T(8,128)S(1)}) custom-call(s32[4]{0:T(128)S(1)} %pad_add_fusion.refs_0_, f32[2,256,80]{2,1,0:T(8,128)S(1)} %copy.25.refs_1_.refs_8_, f32[2,256,80]{2,1,0:T(8,128)S(1)} %copy.26.refs_2_.refs_7_, ...), custom_call_target="tpu_custom_call" | custom-call | flops 747110400 | bytes 3039248 | tf_op jit(solution)/shard_map/forward_first/pallas_call | solution.py:280
  26.2 7.3 %all-to-all-start = ((f32[32,3,512]{2,1,0:T(4,128)}), f32[32,3,512]{2,1,0:T(4,128)S(1)}, u32[]{:S(2)}, u32[]{:S(2)}) async-start(f32[32,3,512]{2,1,0:T(4,128)} %get-tuple-element.98), calls=%async_computation | async-start | bytes 524288 | tf_op jit(solution)/shard_map/all_to_all | solution.py:304
  33.5 10.5 %all-to-all-done.refs_2_ = f32[32,3,512]{2,1,0:T(4,128)S(1)} async-done(((f32[32,3,512]{2,1,0:T(4,128)}), f32[32,3,512]{2,1,0:T(4,128)S(1)}, u32[]{:S(2)}, u32[]{:S(2)}) %all-to-all-start) | async-done | bytes 196640 | tf_op jit(solution)/shard_map/all_to_all | solution.py:304
  44.1 10.9 %forward.4 = (f32[608,512]{1,0:T(8,128)S(1)}, f32[32,2,512]{2,1,0:T(2,128)}, f32[608,512]{1,0:T(8,128)S(1)}, f32[3,512]{1,0:T(4,128)S(1)}) custom-call(s32[4]{0:T(128)S(1)} %pad_add_fusion.refs_0_, f32[608,512]{1,0:T(8,128)} %copy-done.2, f32[32,3,512]{2,1,0:T(4,128)S(1)} %all-to-all-done.refs_2_, f32[1,512]{1,0:T(1,128)S(1)} %get-tuple-element.282.refs_3_.refs_5_, ...), custom_call_target="tpu_custom_call" | custom-call | flops 4781506560 | bytes 19802128 | tf_op jit(solution)/shard_map/forward/pallas_call | solution.py:280
  58.6 8.2 %all-to-all-done.1.refs_2_ = f32[32,2,512]{2,1,0:T(2,128)S(1)} async-done(((f32[32,2,512]{2,1,0:T(2,128)}), f32[32,2,512]{2,1,0:T(2,128)S(1)}, u32[]{:S(2)}, u32[]{:S(2)}) %all-to-all-start.1) | async-done | bytes 131104 | tf_op jit(solution)/shard_map/all_to_all | solution.py:304
  66.8 9.5 %forward.5 = (f32[608,512]{1,0:T(8,128)S(1)}, f32[32,2,512]{2,1,0:T(2,128)S(1)}, f32[608,512]{1,0:T(8,128)S(1)}, f32[3,512]{1,0:T(4,128)S(1)}) custom-call(s32[4]{0:T(128)S(1)} %pad_add_fusion.refs_0_, f32[608,512]{1,0:T(8,128)S(1)} %get-tuple-element.99.refs_1_.refs_8_.refs_2_, f32[32,2,512]{2,1,0:T(2,128)S(1)} %all-to-all-done.1.refs_2_, ...), custom_call_target="tpu_custom_call" | custom-call | flops 4781506560 | bytes 19738640 | tf_op jit(solution)/shard_map/forward/pallas_call | solution.py:280
  77.3 10.1 %all_to_all.45.refs_2_ = f32[32,2,512]{2,1,0:T(2,128)S(1)} all-to-all(f32[32,2,512]{2,1,0:T(2,128)S(1)} %get-tuple-element.103), channel_id=1, replica_groups=mesh['dp'=8,'tm'=4] {'dp','tm'}, dimensions={0} | all-to-all | bytes 262144 | tf_op jit(solution)/shard_map/all_to_all | solution.py:304
  87.4 9.4 %forward.6 = (f32[608,512]{1,0:T(8,128)S(1)}, f32[32,2,512]{2,1,0:T(2,128)S(1)}, f32[608,512]{1,0:T(8,128)S(1)}, f32[3,512]{1,0:T(4,128)S(1)}) custom-call(s32[4]{0:T(128)S(1)} %pad_add_fusion.refs_0_, f32[608,512]{1,0:T(8,128)S(1)} %get-tuple-element.102.refs_1_.refs_8_.refs_2_, f32[32,2,512]{2,1,0:T(2,128)S(1)} %all_to_all.45.refs_2_, ...), custom_call_target="tpu_custom_call" | custom-call | flops 4781506560 | bytes 19738640 | tf_op jit(solution)/shard_map/forward/pallas_call | solution.py:280
  98.9 10.0 %all_to_all.46.refs_2_ = f32[32,2,512]{2,1,0:T(2,128)S(1)} all-to-all(f32[32,2,512]{2,1,0:T(2,128)S(1)} %get-tuple-element.105), channel_id=1, replica_groups=mesh['dp'=8,'tm'=4] {'dp','tm'}, dimensions={0} | all-to-all | bytes 262144 | tf_op jit(solution)/shard_map/all_to_all | solution.py:304
  109.0 8.8 %forward.7 = (f32[608,80]{1,0:T(8,128)S(1)}, f32[32,4,80]{2,1,0:T(4,128)S(1)}, f32[608,512]{1,0:T(8,128)S(1)}, f32[3,512]{1,0:T(4,128)S(1)}) custom-call(s32[4]{0:T(128)S(1)} %pad_add_fusion.refs_0_, f32[608,512]{1,0:T(8,128)} %copy-done.4, f32[32,2,512]{2,1,0:T(2,128)S(1)} %all_to_all.46.refs_2_, f32[1,512]{1,0:T(1,128)S(1)} %get-tuple-element.284.refs_3_.refs_5_, ...), custom_call_target="tpu_custom_call" | custom-call | flops 747110400 | bytes 3883024 | tf_op jit(solution)/shard_map/forward/pallas_call | solution.py:280
  118.8 9.2 %all_to_all.47.refs_1_ = f32[32,4,80]{2,1,0:T(4,128)S(1)} all-to-all(f32[32,4,80]{2,1,0:T(4,128)S(1)} %get-tuple-element.107), channel_id=1, replica_groups=mesh['dp'=8,'tm'=4] {'dp','tm'}, dimensions={0} | all-to-all | bytes 81920 | tf_op jit(solution)/shard_map/all_to_all | solution.py:304
  128.0 7.1 %backward.5 = (f32[608,80]{1,0:T(8,128)S(1)}, f32[2,80]{1,0:T(2,128)S(1)}, f32[2,256,80]{2,1,0:T(8,128)S(1)}, f32[608,512]{1,0:T(8,128)S(1)}, f32[32,2,512]{2,1,0:T(2,128)}) custom-call(s32[4]{0:T(128)S(1)} %pad_add_fusion.refs_0_, f32[32,4,80]{2,1,0:T(4,128)S(1)} %all_to_all.47.refs_1_, f32[608,80]{1,0:T(8,128)S(1)} %get-tuple-element.108.refs_2_, ...), custom_call_target="tpu_custom_call" | custom-call | tf_op jit(solution)/shard_map/backward/pallas_call | solution.py:280
  137.7 2.8 all-to-all-start.5
  141.4 4.3 weight_gradient.5
  145.8 2.9 all-to-all-done.5.refs_1_
  148.7 12.2 %backward.6 = (f32[608,512]{1,0:T(8,128)S(1)}, f32[2,512]{1,0:T(2,128)S(1)}, f32[608,512]{1,0:T(8,128)S(1)}, f32[32,2,512]{2,1,0:T(2,128)}) custom-call(s32[4]{0:T(128)S(1)} %pad_add_fusion.refs_0_, f32[32,2,512]{2,1,0:T(2,128)S(1)} %all-to-all-done.5.refs_1_, f32[608,512]{1,0:T(8,128)S(1)} %copy-done.5, f32[608,512]{1,0:T(8,128)} %copy-done.26, ...), custom_call_target="tpu_custom_call" | custom-call | tf_op jit(solution)/shard_map/backward/pallas_call | solution.py:280
  162.9 3.4 all-to-all-start.6
  167.6 8.9 %weight_gradient.6 = f32[5,512,512]{2,1,0:T(8,128)} custom-call(s32[4]{0:T(128)S(1)} %pad_add_fusion.refs_0_, f32[608,512]{1,0:T(8,128)S(1)} %copy-done.11, f32[608,512]{1,0:T(8,128)S(1)} %copy-done.24), custom_call_target="tpu_custom_call" | custom-call | tf_op jit(solution)/shard_map/weight_gradient/pallas_call | solution.py:280
  176.5 12.2 %backward.7 = (f32[608,512]{1,0:T(8,128)S(1)}, f32[2,512]{1,0:T(2,128)S(1)}, f32[608,512]{1,0:T(8,128)S(1)}, f32[32,2,512]{2,1,0:T(2,128)}) custom-call(s32[4]{0:T(128)S(1)} %pad_add_fusion.refs_0_, f32[32,2,512]{2,1,0:T(2,128)S(1)} %all-to-all-done.6.refs_1_, f32[608,512]{1,0:T(8,128)S(1)} %copy-done.15, f32[608,512]{1,0:T(8,128)} %copy-done.27, ...), custom_call_target="tpu_custom_call" | custom-call | tf_op jit(solution)/shard_map/backward/pallas_call | solution.py:280
  190.8 6.4 %all-to-all-start.7 = ((f32[32,2,512]{2,1,0:T(2,128)}), f32[32,2,512]{2,1,0:T(2,128)S(1)}, u32[]{:S(2)}, u32[]{:S(2)}) async-start(f32[32,2,512]{2,1,0:T(2,128)} %get-tuple-element.124), calls=%async_computation.7 | async-start | bytes 262144 | tf_op jit(solution)/shard_map/all_to_all | solution.py:304
  198.5 8.9 %weight_gradient.7 = (f32[5,256,512]{2,1,0:T(8,128)}, f32[5,256,512]{2,1,0:T(8,128)}) custom-call(s32[4]{0:T(128)S(1)} %pad_add_fusion.refs_0_, f32[608,512]{1,0:T(8,128)S(1)} %copy-done.9, f32[608,512]{1,0:T(8,128)S(1)} %copy-done.22), custom_call_target="tpu_custom_call" | custom-call | tf_op jit(solution)/shard_map/weight_gradient/pallas_call | solution.py:280
  207.8 12.1 %backward.8 = (f32[608,512]{1,0:T(8,128)S(1)}, f32[2,512]{1,0:T(2,128)S(1)}, f32[608,512]{1,0:T(8,128)S(1)}, f32[32,2,512]{2,1,0:T(2,128)}) custom-call(s32[4]{0:T(128)S(1)} %pad_add_fusion.refs_0_, f32[32,2,512]{2,1,0:T(2,128)S(1)} %all-to-all-done.7.refs_1_, f32[608,512]{1,0:T(8,128)S(1)} %copy-done.13, f32[608,512]{1,0:T(8,128)} %copy-done.25, ...), custom_call_target="tpu_custom_call" | custom-call | tf_op jit(solution)/shard_map/backward/pallas_call | solution.py:280
  222.0 5.7 %all-to-all-start.8 = ((f32[32,2,512]{2,1,0:T(2,128)}), f32[32,2,512]{2,1,0:T(2,128)S(1)}, u32[]{:S(2)}, u32[]{:S(2)}) async-start(f32[32,2,512]{2,1,0:T(2,128)} %get-tuple-element.131), calls=%async_computation.8 | async-start | bytes 262144 | tf_op jit(solution)/shard_map/all_to_all | solution.py:304
  227.9 3.1 add.55
  240.4 8.9 %weight_gradient.8 = (f32[5,256,512]{2,1,0:T(8,128)}, f32[5,256,512]{2,1,0:T(8,128)}) custom-call(s32[4]{0:T(128)S(1)} %pad_add_fusion.refs_0_, f32[608,512]{1,0:T(8,128)S(1)} %copy-done.7, f32[608,512]{1,0:T(8,128)S(1)} %copy-done.20), custom_call_target="tpu_custom_call" | custom-call | tf_op jit(solution)/shard_map/weight_gradient/pallas_call | solution.py:280
  252.4 6.2 %collective-permute-done.3 = f32[256,512]{1,0:T(8,128)} collective-permute-done((f32[256,512]{1,0:T(8,128)}, f32[256,512]{1,0:T(8,128)}, u32[]{:S(2)}, u32[]{:S(2)}) %collective-permute-start.3) | collective-permute-done | bytes 524320 | tf_op jit(solution)/shard_map/ppermute | solution.py:309
  262.2 9.1 %backward.9 = (f32[608,512]{1,0:T(8,128)S(1)}, f32[2,512]{1,0:T(2,128)S(1)}, f32[2,256,80]{2,1,0:T(8,128)S(1)}) custom-call(s32[4]{0:T(128)S(1)} %pad_add_fusion.refs_0_, f32[32,2,512]{2,1,0:T(2,128)S(1)} %all-to-all-done.8.refs_1_, f32[608,512]{1,0:T(8,128)S(1)} %copy-done.3, f32[608,512]{1,0:T(8,128)} %copy-done.18, ...), custom_call_target="tpu_custom_call" | custom-call | tf_op jit(solution)/shard_map/backward/pallas_call | solution.py:280
  275.8 3.3 weight_gradient.9
  291.5 10.3 %collective-permute-done.36 = f32[80,512]{1,0:T(8,128)S(1)} collective-permute-done((f32[80,512]{1,0:T(8,128)S(1)}, f32[80,512]{1,0:T(8,128)S(1)}, u32[]{:S(2)}, u32[]{:S(2)}) %collective-permute-start.36) | collective-permute-done | bytes 163872 | tf_op jit(solution)/shard_map/ppermute | solution.py:309
  305.9 7.2 %collective-permute-done.8 = f32[128,512]{1,0:T(8,128)S(1)} collective-permute-done((f32[128,512]{1,0:T(8,128)S(1)}, f32[128,512]{1,0:T(8,128)S(1)}, u32[]{:S(2)}, u32[]{:S(2)}) %collective-permute-start.8) | collective-permute-done | bytes 262176 | tf_op jit(solution)/shard_map/ppermute | solution.py:309
  315.4 3.1 collective-permute-done.9
  318.5 9.6 %collective-permute-done.19 = f32[64,512]{1,0:T(8,128)S(1)} collective-permute-done((f32[64,512]{1,0:T(8,128)S(1)}, f32[64,512]{1,0:T(8,128)S(1)}, u32[]{:S(2)}, u32[]{:S(2)}) %collective-permute-start.19) | collective-permute-done | bytes 131104 | tf_op jit(solution)/shard_map/ppermute | solution.py:309
  333.1 3.4 collective-permute-done.38
  336.6 4.4 collective-permute-done.15
  348.7 16.9 %collective-permute-done.20 = f32[96,512]{1,0:T(8,128)S(1)} collective-permute-done((f32[96,512]{1,0:T(8,128)S(1)}, f32[96,512]{1,0:T(8,128)S(1)}, u32[]{:S(2)}, u32[]{:S(2)}) %collective-permute-start.20) | collective-permute-done | bytes 196640 | tf_op jit(solution)/shard_map/ppermute | solution.py:309
  365.8 6.6 %collective-permute-done.21 = f32[96,512]{1,0:T(8,128)S(1)} collective-permute-done((f32[96,512]{1,0:T(8,128)S(1)}, f32[96,512]{1,0:T(8,128)S(1)}, u32[]{:S(2)}, u32[]{:S(2)}) %collective-permute-start.21) | collective-permute-done | bytes 196640 | tf_op jit(solution)/shard_map/ppermute | solution.py:309
  377.9 2.8 collective-permute-done.22
  383.6 8.6 %collective-permute-done.44 = f32[192,512]{1,0:T(8,128)S(1)} collective-permute-done((f32[192,512]{1,0:T(8,128)S(1)}, f32[192,512]{1,0:T(8,128)S(1)}, u32[]{:S(2)}, u32[]{:S(2)}) %collective-permute-start.44) | collective-permute-done | bytes 393248 | tf_op jit(solution)/shard_map/ppermute | solution.py:309
  392.2 3.4 collective-permute-start.29
  395.9 8.1 %collective-permute-done.25 = f32[64,512]{1,0:T(8,128)S(1)} collective-permute-done((f32[64,512]{1,0:T(8,128)S(1)}, f32[64,512]{1,0:T(8,128)S(1)}, u32[]{:S(2)}, u32[]{:S(2)}) %collective-permute-start.25) | collective-permute-done | bytes 131104 | tf_op jit(solution)/shard_map/ppermute | solution.py:309
  406.0 3.6 collective-permute-done.29
  410.7 8.1 %collective-permute-done.26 = f32[128,512]{1,0:T(8,128)S(1)} collective-permute-done((f32[128,512]{1,0:T(8,128)S(1)}, f32[128,512]{1,0:T(8,128)S(1)}, u32[]{:S(2)}, u32[]{:S(2)}) %collective-permute-start.26) | collective-permute-done | bytes 262176 | tf_op jit(solution)/shard_map/ppermute | solution.py:309
  421.8 6.4 %collective-permute-done.27 = f32[256,512]{1,0:T(8,128)S(1)} collective-permute-done((f32[256,512]{1,0:T(8,128)S(1)}, f32[256,512]{1,0:T(8,128)S(1)}, u32[]{:S(2)}, u32[]{:S(2)}) %collective-permute-start.27) | collective-permute-done | bytes 524320 | tf_op jit(solution)/shard_map/ppermute | solution.py:309
  435.1 4.9 %place_whole.1.refs_3_ = f32[3,5,512,512]{3,2,1,0:T(8,128)} custom-call(f32[5,512,512]{2,1,0:T(8,128)} %get-tuple-element.194.refs_0_), custom_call_target="tpu_custom_call" | custom-call | tf_op jit(solution)/shard_map/place_whole/pallas_call | solution.py:280
  444.1 4.1 place.2.refs_3_
  448.2 3.7 slice.340
  452.0 4.2 place.3
  (283 shorter events, 108.5 us)
Async XLA Ops:
  26.2 17.9 %all-to-all-start = ((f32[32,3,512]{2,1,0:T(4,128)}), f32[32,3,512]{2,1,0:T(4,128)S(1)}, u32[]{:S(2)}, u32[]{:S(2)}) async-start(f32[32,3,512]{2,1,0:T(4,128)} %get-tuple-element.98), calls=%async_computation | async-start | bytes 524288 | tf_op jit(solution)/shard_map/all_to_all | solution.py:304
  56.0 10.8 %all-to-all-start.1 = ((f32[32,2,512]{2,1,0:T(2,128)}), f32[32,2,512]{2,1,0:T(2,128)S(1)}, u32[]{:S(2)}, u32[]{:S(2)}) async-start(f32[32,2,512]{2,1,0:T(2,128)} %get-tuple-element.100), calls=%async_computation.1 | async-start | bytes 262144 | tf_op jit(solution)/shard_map/all_to_all | solution.py:304
  137.7 11.0 %all-to-all-start.5 = ((f32[32,2,512]{2,1,0:T(2,128)}), f32[32,2,512]{2,1,0:T(2,128)S(1)}, u32[]{:S(2)}, u32[]{:S(2)}) async-start(f32[32,2,512]{2,1,0:T(2,128)} %get-tuple-element.112), calls=%async_computation.5 | async-start | bytes 262144 | tf_op jit(solution)/shard_map/all_to_all | solution.py:304
  162.9 13.6 %all-to-all-start.6 = ((f32[32,2,512]{2,1,0:T(2,128)}), f32[32,2,512]{2,1,0:T(2,128)S(1)}, u32[]{:S(2)}, u32[]{:S(2)}) async-start(f32[32,2,512]{2,1,0:T(2,128)} %get-tuple-element.118), calls=%async_computation.6 | async-start | bytes 262144 | tf_op jit(solution)/shard_map/all_to_all | solution.py:304
  190.8 16.6 %all-to-all-start.7 = ((f32[32,2,512]{2,1,0:T(2,128)}), f32[32,2,512]{2,1,0:T(2,128)S(1)}, u32[]{:S(2)}, u32[]{:S(2)}) async-start(f32[32,2,512]{2,1,0:T(2,128)} %get-tuple-element.124), calls=%async_computation.7 | async-start | bytes 262144 | tf_op jit(solution)/shard_map/all_to_all | solution.py:304
  207.4 20.6 %collective-permute-start.2 = (f32[1280,512]{1,0:T(8,128)}, f32[1280,512]{1,0:T(8,128)}, u32[]{:S(2)}, u32[]{:S(2)}) collective-permute-start(f32[1280,512]{1,0:T(8,128)} %bitcast.44), channel_id=1, source_target_pairs={{0,1},{1,0},{2,3},{3,2},{4,5},{5,4},{6,7},{7,6},{8,9},{9,8},{10,11... | collective-permute-start | bytes 7864328 | tf_op jit(solution)/shard_map/ppermute | solution.py:309
  222.0 27.3 %all-to-all-start.8 = ((f32[32,2,512]{2,1,0:T(2,128)}), f32[32,2,512]{2,1,0:T(2,128)S(1)}, u32[]{:S(2)}, u32[]{:S(2)}) async-start(f32[32,2,512]{2,1,0:T(2,128)} %get-tuple-element.131), calls=%async_computation.8 | async-start | bytes 262144 | tf_op jit(solution)/shard_map/all_to_all | solution.py:304
  227.7 207.3 %all-reduce.4.cloned.1.call-start = ((), (), s32[]{:S(2)}) async-start(), calls=%async_computation.9 | async-start | bytes 12124160 | tf_op jit(solution)/shard_map/psum | solution.py:496
  232.3 17.1 %collective-permute-start.5 = (f32[192,512]{1,0:T(8,128)}, f32[192,512]{1,0:T(8,128)}, u32[]{:S(2)}, u32[]{:S(2)}) collective-permute-start(f32[192,512]{1,0:T(8,128)} %slice_select_fusion.5), channel_id=1, source_target_pairs={{0,8},{1,9},{2,10},{3,11},{4,12},{5,13},{6,14},{7,15},{8,0},{9,1},... | collective-permute-start | bytes 1179656 | tf_op jit(solution)/shard_map/ppermute | solution.py:309
  234.9 16.0 %collective-permute-start.4 = (f32[192,512]{1,0:T(8,128)}, f32[192,512]{1,0:T(8,128)}, u32[]{:S(2)}, u32[]{:S(2)}) collective-permute-start(f32[192,512]{1,0:T(8,128)} %slice_select_fusion.6), channel_id=1, source_target_pairs={{0,4},{1,5},{2,6},{3,7},{4,0},{5,1},{6,2},{7,3},{8,12},{9,13},{10,... | collective-permute-start | bytes 1179656 | tf_op jit(solution)/shard_map/ppermute | solution.py:309
  237.3 21.3 %collective-permute-start.3 = (f32[256,512]{1,0:T(8,128)}, f32[256,512]{1,0:T(8,128)}, u32[]{:S(2)}, u32[]{:S(2)}) collective-permute-start(f32[256,512]{1,0:T(8,128)} %slice_select_fusion.2), channel_id=1, source_target_pairs={{0,2},{1,3},{2,0},{3,1},{4,6},{5,7},{6,4},{7,5},{8,10},{9,11},{10,... | collective-permute-start | bytes 1572872 | tf_op jit(solution)/shard_map/ppermute | solution.py:309
  249.3 35.2 %collective-permute-start.6 = (f32[1280,512]{1,0:T(8,128)}, f32[1280,512]{1,0:T(8,128)S(1)}, u32[]{:S(2)}, u32[]{:S(2)}) collective-permute-start(f32[1280,512]{1,0:T(8,128)} %bitcast.43), channel_id=1, source_target_pairs={{0,1},{1,0},{2,3},{3,2},{4,5},{5,4},{6,7},{7,6},{8,9},{9,8},{10,11... | collective-permute-start | bytes 7864328 | tf_op jit(solution)/shard_map/ppermute | solution.py:309
  259.8 11.5 %collective-permute-start.12 = (f32[96,512]{1,0:T(8,128)S(1)}, f32[96,512]{1,0:T(8,128)S(1)}, u32[]{:S(2)}, u32[]{:S(2)}) collective-permute-start(f32[96,512]{1,0:T(8,128)S(1)} %slice_select_fusion.11), channel_id=1, source_target_pairs={{0,2},{1,3},{2,0},{3,1},{4,6},{5,7},{6,4},{7,5},{8,10},{9,11},{10,... | collective-permute-start | bytes 589832 | tf_op jit(solution)/shard_map/ppermute | solution.py:309
  261.9 10.6 %collective-permute-start.11 = (f32[96,512]{1,0:T(8,128)S(1)}, f32[96,512]{1,0:T(8,128)S(1)}, u32[]{:S(2)}, u32[]{:S(2)}) collective-permute-start(f32[96,512]{1,0:T(8,128)S(1)} %slice_select_fusion.12), channel_id=1, source_target_pairs={{0,8},{1,9},{2,10},{3,11},{4,12},{5,13},{6,14},{7,15},{8,0},{9,1},... | collective-permute-start | bytes 589832 | tf_op jit(solution)/shard_map/ppermute | solution.py:309
  262.1 10.5 %collective-permute-start.10 = (f32[128,512]{1,0:T(8,128)S(1)}, f32[128,512]{1,0:T(8,128)S(1)}, u32[]{:S(2)}, u32[]{:S(2)}) collective-permute-start(f32[128,512]{1,0:T(8,128)S(1)} %slice_select_fusion.10), channel_id=1, source_target_pairs={{0,4},{1,5},{2,6},{3,7},{4,0},{5,1},{6,2},{7,3},{8,12},{9,13},{10,... | collective-permute-start | bytes 786440 | tf_op jit(solution)/shard_map/ppermute | solution.py:309
  272.6 6.6 %collective-permute-start.33 = (f32[48,512]{1,0:T(8,128)S(1)}, f32[48,512]{1,0:T(8,128)S(1)}, u32[]{:S(2)}, u32[]{:S(2)}) collective-permute-start(f32[48,512]{1,0:T(8,128)S(1)} %slice_select_fusion.17), channel_id=1, source_target_pairs={{0,4},{1,5},{2,6},{3,7},{4,0},{5,1},{6,2},{7,3},{8,12},{9,13},{10,... | collective-permute-start | bytes 294920 | tf_op jit(solution)/shard_map/ppermute | solution.py:309
  273.7 8.0 %collective-permute-start.34 = (f32[64,512]{1,0:T(8,128)S(1)}, f32[64,512]{1,0:T(8,128)S(1)}, u32[]{:S(2)}, u32[]{:S(2)}) collective-permute-start(f32[64,512]{1,0:T(8,128)S(1)} %slice_select_fusion.16), channel_id=1, source_target_pairs={{0,8},{1,9},{2,10},{3,11},{4,12},{5,13},{6,14},{7,15},{8,0},{9,1},... | collective-permute-start | bytes 393224 | tf_op jit(solution)/shard_map/ppermute | solution.py:309
  279.1 12.3 %collective-permute-start.13 = (f32[200,512]{1,0:T(8,128)S(1)}, f32[200,512]{1,0:T(8,128)S(1)}, u32[]{:S(2)}, u32[]{:S(2)}) collective-permute-start(f32[200,512]{1,0:T(8,128)S(1)} %bitcast.37), channel_id=1, source_target_pairs={{0,1},{1,0},{2,3},{3,2},{4,5},{5,4},{6,7},{7,6},{8,9},{9,8},{10,11... | collective-permute-start | bytes 1228808 | tf_op jit(solution)/shard_map/ppermute | solution.py:309
  281.8 9.5 %collective-permute-start.35 = (f32[80,512]{1,0:T(8,128)S(1)}, f32[80,512]{1,0:T(8,128)S(1)}, u32[]{:S(2)}, u32[]{:S(2)}) collective-permute-start(f32[80,512]{1,0:T(8,128)S(1)} %fusion.13), channel_id=1, source_target_pairs={{0,16},{1,17},{2,18},{3,19},{4,20},{5,21},{6,22},{7,23},{8,24},{9,... | collective-permute-start | bytes 491528 | tf_op jit(solution)/shard_map/ppermute | solution.py:309
  285.4 16.4 %collective-permute-start.17 = (f32[256,512]{1,0:T(8,128)S(1)}, f32[256,512]{1,0:T(8,128)S(1)}, u32[]{:S(2)}, u32[]{:S(2)}) collective-permute-start(f32[256,512]{1,0:T(8,128)S(1)} %get-tuple-element.203), channel_id=1, source_target_pairs={{0,2},{1,3},{2,0},{3,1},{4,6},{5,7},{6,4},{7,5},{8,10},{9,11},{10,... | collective-permute-start | bytes 1572872 | tf_op jit(solution)/shard_map/ppermute | solution.py:309
  287.4 15.3 %collective-permute-start.7 = (f32[256,512]{1,0:T(8,128)S(1)}, f32[256,512]{1,0:T(8,128)S(1)}, u32[]{:S(2)}, u32[]{:S(2)}) collective-permute-start(f32[256,512]{1,0:T(8,128)S(1)} %get-tuple-element.204), channel_id=1, source_target_pairs={{0,4},{1,5},{2,6},{3,7},{4,0},{5,1},{6,2},{7,3},{8,12},{9,13},{10,... | collective-permute-start | bytes 1572872 | tf_op jit(solution)/shard_map/ppermute | solution.py:309
  291.3 10.5 %collective-permute-start.36 = (f32[80,512]{1,0:T(8,128)S(1)}, f32[80,512]{1,0:T(8,128)S(1)}, u32[]{:S(2)}, u32[]{:S(2)}) collective-permute-start(f32[80,512]{1,0:T(8,128)S(1)} %select_add_fusion.12), channel_id=1, source_target_pairs={{0,16},{1,17},{2,18},{3,19},{4,20},{5,21},{6,22},{7,23},{8,24},{9,... | collective-permute-start | bytes 491528 | tf_op jit(solution)/shard_map/ppermute | solution.py:309
  303.2 9.9 %collective-permute-start.8 = (f32[128,512]{1,0:T(8,128)S(1)}, f32[128,512]{1,0:T(8,128)S(1)}, u32[]{:S(2)}, u32[]{:S(2)}) collective-permute-start(f32[128,512]{1,0:T(8,128)S(1)} %slice_select_fusion.9), channel_id=1, source_target_pairs={{0,8},{1,9},{2,10},{3,11},{4,12},{5,13},{6,14},{7,15},{8,0},{9,1},... | collective-permute-start | bytes 786440 | tf_op jit(solution)/shard_map/ppermute | solution.py:309
  303.4 10.9 %collective-permute-start.18 = (f32[128,512]{1,0:T(8,128)S(1)}, f32[128,512]{1,0:T(8,128)S(1)}, u32[]{:S(2)}, u32[]{:S(2)}) collective-permute-start(f32[128,512]{1,0:T(8,128)S(1)} %slice_select_fusion.7), channel_id=1, source_target_pairs={{0,4},{1,5},{2,6},{3,7},{4,0},{5,1},{6,2},{7,3},{8,12},{9,13},{10,... | collective-permute-start | bytes 786440 | tf_op jit(solution)/shard_map/ppermute | solution.py:309
  304.5 23.6 %collective-permute-start.14 = (f32[256,512]{1,0:T(8,128)S(1)}, f32[256,512]{1,0:T(8,128)S(1)}, u32[]{:S(2)}, u32[]{:S(2)}) collective-permute-start(f32[256,512]{1,0:T(8,128)S(1)} %get-tuple-element.201), channel_id=1, source_target_pairs={{0,8},{1,9},{2,10},{3,11},{4,12},{5,13},{6,14},{7,15},{8,0},{9,1},... | collective-permute-start | bytes 1572872 | tf_op jit(solution)/shard_map/ppermute | solution.py:309
  314.4 13.7 %collective-permute-start.19 = (f32[64,512]{1,0:T(8,128)S(1)}, f32[64,512]{1,0:T(8,128)S(1)}, u32[]{:S(2)}, u32[]{:S(2)}) collective-permute-start(f32[64,512]{1,0:T(8,128)S(1)} %slice_select_fusion.13), channel_id=1, source_target_pairs={{0,8},{1,9},{2,10},{3,11},{4,12},{5,13},{6,14},{7,15},{8,0},{9,1},... | collective-permute-start | bytes 393224 | tf_op jit(solution)/shard_map/ppermute | solution.py:309
  330.5 11.0 %collective-permute-start.37 = (f32[64,512]{1,0:T(8,128)S(1)}, f32[64,512]{1,0:T(8,128)S(1)}, u32[]{:S(2)}, u32[]{:S(2)}) collective-permute-start(f32[64,512]{1,0:T(8,128)S(1)} %slice.297), channel_id=1, source_target_pairs={{0,8},{1,9},{2,10},{3,11},{4,12},{5,13},{6,14},{7,15},{8,0},{9,1},... | collective-permute-start | bytes 393224 | tf_op jit(solution)/shard_map/ppermute | solution.py:309
  331.1 9.9 %collective-permute-start.15 = (f32[128,512]{1,0:T(8,128)S(1)}, f32[128,512]{1,0:T(8,128)S(1)}, u32[]{:S(2)}, u32[]{:S(2)}) collective-permute-start(f32[128,512]{1,0:T(8,128)S(1)} %slice_select_fusion.8), channel_id=1, source_target_pairs={{0,2},{1,3},{2,0},{3,1},{4,6},{5,7},{6,4},{7,5},{8,10},{9,11},{10,... | collective-permute-start | bytes 786440 | tf_op jit(solution)/shard_map/ppermute | solution.py:309
  341.1 6.4 %collective-permute-start.16 = (f32[64,512]{1,0:T(8,128)S(1)}, f32[64,512]{1,0:T(8,128)S(1)}, u32[]{:S(2)}, u32[]{:S(2)}) collective-permute-start(f32[64,512]{1,0:T(8,128)S(1)} %slice_select_fusion.14), channel_id=1, source_target_pairs={{0,4},{1,5},{2,6},{3,7},{4,0},{5,1},{6,2},{7,3},{8,12},{9,13},{10,... | collective-permute-start | bytes 393224 | tf_op jit(solution)/shard_map/ppermute | solution.py:309
  341.5 7.1 %collective-permute-start.41 = (f32[96,512]{1,0:T(8,128)S(1)}, f32[96,512]{1,0:T(8,128)S(1)}, u32[]{:S(2)}, u32[]{:S(2)}) collective-permute-start(f32[96,512]{1,0:T(8,128)S(1)} %pad_maximum_fusion.18), channel_id=1, source_target_pairs={{0,8},{1,9},{2,10},{3,11},{4,12},{5,13},{6,14},{7,15},{8,0},{9,1},... | collective-permute-start | bytes 589832 | tf_op jit(solution)/shard_map/ppermute | solution.py:309
  342.4 6.2 %collective-permute-start.42 = (f32[96,512]{1,0:T(8,128)S(1)}, f32[96,512]{1,0:T(8,128)S(1)}, u32[]{:S(2)}, u32[]{:S(2)}) collective-permute-start(f32[96,512]{1,0:T(8,128)S(1)} %pad_maximum_fusion.19), channel_id=1, source_target_pairs={{0,2},{1,3},{2,0},{3,1},{4,6},{5,7},{6,4},{7,5},{8,10},{9,11},{10,... | collective-permute-start | bytes 589832 | tf_op jit(solution)/shard_map/ppermute | solution.py:309
  343.1 29.6 %collective-permute-start.40 = (f32[128,512]{1,0:T(8,128)S(1)}, f32[128,512]{1,0:T(8,128)S(1)}, u32[]{:S(2)}, u32[]{:S(2)}) collective-permute-start(f32[128,512]{1,0:T(8,128)S(1)} %pad_maximum_fusion.15), channel_id=1, source_target_pairs={{0,4},{1,5},{2,6},{3,7},{4,0},{5,1},{6,2},{7,3},{8,12},{9,13},{10,... | collective-permute-start | bytes 786440 | tf_op jit(solution)/shard_map/ppermute | solution.py:309
  347.6 18.1 %collective-permute-start.20 = (f32[96,512]{1,0:T(8,128)S(1)}, f32[96,512]{1,0:T(8,128)S(1)}, u32[]{:S(2)}, u32[]{:S(2)}) collective-permute-start(f32[96,512]{1,0:T(8,128)S(1)} %fusion.12), channel_id=1, source_target_pairs={{0,16},{1,17},{2,18},{3,19},{4,20},{5,21},{6,22},{7,23},{8,24},{9,... | collective-permute-start | bytes 589832 | tf_op jit(solution)/shard_map/ppermute | solution.py:309
  365.7 6.7 %collective-permute-start.21 = (f32[96,512]{1,0:T(8,128)S(1)}, f32[96,512]{1,0:T(8,128)S(1)}, u32[]{:S(2)}, u32[]{:S(2)}) collective-permute-start(f32[96,512]{1,0:T(8,128)S(1)} %select_add_fusion.9), channel_id=1, source_target_pairs={{0,16},{1,17},{2,18},{3,19},{4,20},{5,21},{6,22},{7,23},{8,24},{9,... | collective-permute-start | bytes 589832 | tf_op jit(solution)/shard_map/ppermute | solution.py:309
  372.5 8.2 %collective-permute-start.22 = (f32[64,512]{1,0:T(8,128)S(1)}, f32[64,512]{1,0:T(8,128)S(1)}, u32[]{:S(2)}, u32[]{:S(2)}) collective-permute-start(f32[64,512]{1,0:T(8,128)S(1)} %slice.334), channel_id=1, source_target_pairs={{0,8},{1,9},{2,10},{3,11},{4,12},{5,13},{6,14},{7,15},{8,0},{9,1},... | collective-permute-start | bytes 393224 | tf_op jit(solution)/shard_map/ppermute | solution.py:309
  372.6 9.1 %collective-permute-start.28 = (f32[64,512]{1,0:T(8,128)S(1)}, f32[64,512]{1,0:T(8,128)S(1)}, u32[]{:S(2)}, u32[]{:S(2)}) collective-permute-start(f32[64,512]{1,0:T(8,128)S(1)} %slice.337), channel_id=1, source_target_pairs={{0,4},{1,5},{2,6},{3,7},{4,0},{5,1},{6,2},{7,3},{8,12},{9,13},{10,... | collective-permute-start | bytes 393224 | tf_op jit(solution)/shard_map/ppermute | solution.py:309
  372.8 19.4 %collective-permute-start.44 = (f32[192,512]{1,0:T(8,128)S(1)}, f32[192,512]{1,0:T(8,128)S(1)}, u32[]{:S(2)}, u32[]{:S(2)}) collective-permute-start(f32[192,512]{1,0:T(8,128)S(1)} %pad_maximum_fusion.9), channel_id=1, source_target_pairs={{0,4},{1,5},{2,6},{3,7},{4,0},{5,1},{6,2},{7,3},{8,12},{9,13},{10,... | collective-permute-start | bytes 1179656 | tf_op jit(solution)/shard_map/ppermute | solution.py:309
  374.8 20.8 %collective-permute-start.45 = (f32[192,512]{1,0:T(8,128)S(1)}, f32[192,512]{1,0:T(8,128)S(1)}, u32[]{:S(2)}, u32[]{:S(2)}) collective-permute-start(f32[192,512]{1,0:T(8,128)S(1)} %pad_maximum_fusion.10), channel_id=1, source_target_pairs={{0,8},{1,9},{2,10},{3,11},{4,12},{5,13},{6,14},{7,15},{8,0},{9,1},... | collective-permute-start | bytes 1179656 | tf_op jit(solution)/shard_map/ppermute | solution.py:309
  376.8 28.3 %collective-permute-start.43 = (f32[256,512]{1,0:T(8,128)S(1)}, f32[256,512]{1,0:T(8,128)S(1)}, u32[]{:S(2)}, u32[]{:S(2)}) collective-permute-start(f32[256,512]{1,0:T(8,128)S(1)} %pad_maximum_fusion.7), channel_id=1, source_target_pairs={{0,2},{1,3},{2,0},{3,1},{4,6},{5,7},{6,4},{7,5},{8,10},{9,11},{10,... | collective-permute-start | bytes 1572872 | tf_op jit(solution)/shard_map/ppermute | solution.py:309
  381.7 22.2 %collective-permute-start.25 = (f32[64,512]{1,0:T(8,128)S(1)}, f32[64,512]{1,0:T(8,128)S(1)}, u32[]{:S(2)}, u32[]{:S(2)}) collective-permute-start(f32[64,512]{1,0:T(8,128)S(1)} %get-tuple-element.258), channel_id=1, source_target_pairs={{0,2},{1,3},{2,0},{3,1},{4,6},{5,7},{6,4},{7,5},{8,10},{9,11},{10,... | collective-permute-start | bytes 393224 | tf_op jit(solution)/shard_map/ppermute | solution.py:309
  382.6 22.6 %collective-permute-start.23 = (f32[128,512]{1,0:T(8,128)S(1)}, f32[128,512]{1,0:T(8,128)S(1)}, u32[]{:S(2)}, u32[]{:S(2)}) collective-permute-start(f32[128,512]{1,0:T(8,128)S(1)} %pad_maximum_fusion.12), channel_id=1, source_target_pairs={{0,4},{1,5},{2,6},{3,7},{4,0},{5,1},{6,2},{7,3},{8,12},{9,13},{10,... | collective-permute-start | bytes 786440 | tf_op jit(solution)/shard_map/ppermute | solution.py:309
  392.2 17.4 %collective-permute-start.29 = (f32[128,512]{1,0:T(8,128)S(1)}, f32[128,512]{1,0:T(8,128)S(1)}, u32[]{:S(2)}, u32[]{:S(2)}) collective-permute-start(f32[128,512]{1,0:T(8,128)S(1)} %pad_maximum_fusion.14), channel_id=1, source_target_pairs={{0,2},{1,3},{2,0},{3,1},{4,6},{5,7},{6,4},{7,5},{8,10},{9,11},{10,... | collective-permute-start | bytes 786440 | tf_op jit(solution)/shard_map/ppermute | solution.py:309
  404.0 14.9 %collective-permute-start.26 = (f32[128,512]{1,0:T(8,128)S(1)}, f32[128,512]{1,0:T(8,128)S(1)}, u32[]{:S(2)}, u32[]{:S(2)}) collective-permute-start(f32[128,512]{1,0:T(8,128)S(1)} %pad_maximum_fusion.13), channel_id=1, source_target_pairs={{0,8},{1,9},{2,10},{3,11},{4,12},{5,13},{6,14},{7,15},{8,0},{9,1},... | collective-permute-start | bytes 786440 | tf_op jit(solution)/shard_map/ppermute | solution.py:309
  405.3 14.7 %collective-permute-start.24 = (f32[256,512]{1,0:T(8,128)S(1)}, f32[256,512]{1,0:T(8,128)S(1)}, u32[]{:S(2)}, u32[]{:S(2)}) collective-permute-start(f32[256,512]{1,0:T(8,128)S(1)} %pad_maximum_fusion.4), channel_id=1, source_target_pairs={{0,2},{1,3},{2,0},{3,1},{4,6},{5,7},{6,4},{7,5},{8,10},{9,11},{10,... | collective-permute-start | bytes 1572872 | tf_op jit(solution)/shard_map/ppermute | solution.py:309
  409.6 20.3 %collective-permute-start.30 = (f32[256,512]{1,0:T(8,128)S(1)}, f32[256,512]{1,0:T(8,128)S(1)}, u32[]{:S(2)}, u32[]{:S(2)}) collective-permute-start(f32[256,512]{1,0:T(8,128)S(1)} %pad_maximum_fusion.6), channel_id=1, source_target_pairs={{0,8},{1,9},{2,10},{3,11},{4,12},{5,13},{6,14},{7,15},{8,0},{9,1},... | collective-permute-start | bytes 1572872 | tf_op jit(solution)/shard_map/ppermute | solution.py:309
  418.9 9.2 %collective-permute-start.27 = (f32[256,512]{1,0:T(8,128)S(1)}, f32[256,512]{1,0:T(8,128)S(1)}, u32[]{:S(2)}, u32[]{:S(2)}) collective-permute-start(f32[256,512]{1,0:T(8,128)S(1)} %pad_maximum_fusion.5), channel_id=1, source_target_pairs={{0,4},{1,5},{2,6},{3,7},{4,0},{5,1},{6,2},{7,3},{8,12},{9,13},{10,... | collective-permute-start | bytes 1572872 | tf_op jit(solution)/shard_map/ppermute | solution.py:309
  432.1 9.9 %collective-permute-start.31 = (f32[1536,512]{1,0:T(8,128)}, f32[1536,512]{1,0:T(8,128)}, u32[]{:S(2)}, u32[]{:S(2)}) collective-permute-start(f32[1536,512]{1,0:T(8,128)} %get-tuple-element.196), channel_id=1, source_target_pairs={{0,1},{1,0},{2,3},{3,2},{4,5},{5,4},{6,7},{7,6},{8,9},{9,8},{10,11... | collective-permute-start | bytes 9437192 | tf_op jit(solution)/shard_map/ppermute | solution.py:309
  433.6 8.3 %collective-permute-start.46 = (f32[1280,512]{1,0:T(8,128)S(1)}, f32[1280,512]{1,0:T(8,128)}, u32[]{:S(2)}, u32[]{:S(2)}) collective-permute-start(f32[1280,512]{1,0:T(8,128)S(1)} %constant_dynamic-update-slice_fusion.1), channel_id=1, source_target_pairs={{0,1},{1,0},{2,3},{3,2},{4,5},{5,4},{6,7},{7,6},{8,9},{9,8},{10,11... | collective-permute-start | bytes 7864328 | tf_op jit(solution)/shard_map/ppermute | solution.py:309
  (53 other events, 410.2 us)
Sparse Core Ops, SparseCore 0:
  238.9 185.3 all-reduce.3

commit v4 on v3

--- a/solution.py
+++ b/solution.py
@@ -26,10 +26,9 @@
 
 
 def product(left, right, dims):
-    def one(a, b):
-        return lax.dot_general(a, b, (dims, ((), ())), preferred_element_type=F32)
-
-    return one(left[0], right[0]) + (one(left[0], right[1]) + one(left[1], right[0]))
+    l = jnp.concatenate([left[0], left[0], left[1]], axis=dims[0][0])
+    r = jnp.concatenate([right[0], right[1], right[0]], axis=dims[1][0])
+    return lax.dot_general(l, r, (dims, ((), ())), preferred_element_type=F32)
 
 
 def sum_over_devices(ref):
@@ -103,7 +102,7 @@
         out_ref[...] += product((high_ref[k], low_ref[k]), split(w_ref[k]), dims)
         return carry
 
-    lax.fori_loop(0, width, tap, 0)
+    lax.fori_loop(0, width, tap, 0, unroll=True)
 
 
 def tap_scratch(rows, dims, contracted):
@@ -244,7 +243,7 @@
             refs["other"][k] = jnp.where(upper, dw[:half], dw[half:])
         return carry
 
-    lax.fori_loop(0, width, tap, 0)
+    lax.fori_loop(0, width, tap, 0, unroll=True)
 
 
 def place_whole(index, refs):
@@ -254,16 +253,18 @@
 
 
 def place(index, refs):
-    meta_ref, mine_ref, other_ref, sems, out_ref = (refs[n] for n in ("meta", "mine", "other", "sems", "out"))
-    half = mine_ref.shape[1]
-    target = out_ref if index is None else out_ref.at[index]
+    meta_ref, out_ref = refs["meta"], refs["out"]
+    width, half = out_ref.shape[1], out_ref.shape[2] // 2
     upper = meta_ref[meta_ref.shape[0] - 1]
-    first = pltpu.make_async_copy(mine_ref, target.at[:, pl.ds(upper * half, half)], sems.at[0])
-    second = pltpu.make_async_copy(other_ref, target.at[:, pl.ds((1 - upper) * half, half)], sems.at[1])
-    first.start()
-    second.start()
-    first.wait()
-    second.wait()
+    copies = []
+    for i, (name, at) in enumerate((("mine", upper), ("other", 1 - upper))):
+        for k in range(width):
+            source = refs[name].at[pl.ds(k * half, half)]
+            copies.append(pltpu.make_async_copy(source, out_ref.at[index, k, pl.ds(at * half, half)], refs["sems"].at[i, k]))
+    for copy in copies:
+        copy.start()
+    for copy in copies:
+        copy.wait()
 
 
 def shape(*dims):
@@ -463,7 +464,7 @@
             far.update(x=x[layer], below_h=h[layer - 1])
             outs.update(gz_out=shape(rows, below), copies=shape(devices, 2, below))
         scratch.update(fetch_scratch(far))
-        out = call(functools.partial(backward, batch, index, kind), "backward", ins, outs, scratch, 0, far=("w", *far))
+        out = call(functools.partial(backward, batch, index, kind), "backward", ins, outs, scratch, 8 * work(dims), far=("w", *far))
         param_grads[layer] = out["param_grads"]
         if kind == "last":
             mel_after = out["mel_after"]
@@ -483,7 +484,7 @@
         pieces = call(
             functools.partial(weight_gradient, batch, kind == "last"), "weight_gradient",
             dict(meta=meta, x=x[layer], dh=dh), pieces,
-            dict(shifted=pltpu.VMEM((width, batch * frames, below), F32), **fetch_scratch(dict(x=x[layer]))), 0, far=("x",),
+            dict(shifted=pltpu.VMEM((width, batch * frames, below), F32), **fetch_scratch(dict(x=x[layer]))), 8 * work(dims), far=("x",),
         )
         for e in exchanges:
             e.advance()
@@ -506,25 +507,30 @@
             rows_all = held[0].shape[0] + pieces[0].shape[0]
             exchanges.append(Exchange([held, pieces], [-(-rows_all // 192) * 64] * 3))
     early, late = exchanges
+
+    def placed(index, e, before):
+        ins = dict(meta=meta, mine=e.state[0], other=e.state[1])
+        if before is not None:
+            ins["before"] = before
+        return call(
+            functools.partial(place, index), "place", ins, dict(out=shape(*w_mid.shape)), dict(sems=pltpu.SemaphoreType.DMA((2, width))), 0,
+            far=("before",), far_outs=("out",), alias=None if before is None else ("before", "out"),
+        )["out"]
+
     while late.steps:
         late.advance()
-        early.advance()
-        early.state, _ = lax.optimization_barrier((early.state, late.state))
+        if early.steps:
+            early.advance()
+            early.state, _ = lax.optimization_barrier((early.state, late.state))
     half = channels // 2
-    mid = (width, half, channels)
     small = (width, mels // 2, channels)
     mid_rows, small_rows = width * half, width * mels // 2
     grad_w_mid = call(
         functools.partial(place_whole, 2), "place_whole", dict(value=summed[0]), dict(out=shape(*w_mid.shape)),
         dict(sem=pltpu.SemaphoreType.DMA), 0, far=(), far_outs=("out",),
     )["out"]
-    for index, e in ((1, exchanges[0]), (0, exchanges[1])):
-        grad_w_mid = call(
-            functools.partial(place, index), "place",
-            dict(meta=meta, mine=e.state[0][:mid_rows].reshape(mid), other=e.state[1][:mid_rows].reshape(mid), before=grad_w_mid),
-            dict(out=shape(*w_mid.shape)), dict(sems=pltpu.SemaphoreType.DMA((2,))), 0,
-            far=("before",), far_outs=("out",), alias=("before", "out"),
-        )["out"]
+    grad_w_mid = placed(1, early, grad_w_mid)
+    grad_w_mid = placed(0, late, grad_w_mid)
     mine, other = (v[mid_rows : mid_rows + small_rows].reshape(small) for v in exchanges[1].state)
     upper = upper_half(0)
     grad_w_first = jnp.concatenate([jnp.where(upper, other, mine), jnp.where(upper, mine, other)], axis=1)

time: 473 us -> 458 us (0.968)
  Pallas kernels: 145 us -> 134 us
  blocking collectives: 29.3 us -> 20.4 us
  waiting for transfers between devices: 141 us -> 148 us
    pallas_call x18, Pallas kernels: 145 us -> 134 us  [call(): pl.pallas_call(kernel, name=name, out_shape=list(outs.values()), in_specs...]
    all_to_all x3 -> x2, blocking collectives: 29.3 us -> 20.4 us  [to_all(): return lax.all_to_all(copies, AXES, 0, 0)]
    all_to_all x6 -> x7, waiting for transfers between devices: 21.6 us -> 29.5 us  [to_all(): return lax.all_to_all(copies, AXES, 0, 0)]
    all_to_all x6 -> x7, starting transfers between devices: 28.1 us -> 32.6 us  [to_all(): return lax.all_to_all(copies, AXES, 0, 0)]
    unnamed x101 -> x95, local copies, waits for them, and re-layouts: 28.1 us -> 29 us
  transfers between devices with their start and end apart: 54 -> 55, of which waited for: 26 -> 28; matrix products, arithmetic and copies ran while one was open for 5% -> 5% of each run, Pallas kernels for 13% -> 13%
where the time goes in v4:
time: 458 us; the launch traced here: 451 us
  waiting for transfers between devices  148 us (32%)
  Pallas kernels  134 us (29%)
  starting transfers between devices  81.7 us (18%)
  local copies, waits for them, and re-layouts  29.9 us (7%)
  other arithmetic  21.6 us (5%)
  blocking collectives  20.4 us (4%)
  between operations  15.6 us (3%)
    pallas_call x18, Pallas kernels, call(): pl.pallas_call(kernel, name=name, out_shape=list(outs.values()), in_specs...  134 us
    ppermute x45, waiting for transfers between devices, swap(): return lax.ppermute(x, AXES, [(i, i ^ 1 << bit) for i in range(devices)])  118 us
    ppermute x45, starting transfers between devices, swap(): return lax.ppermute(x, AXES, [(i, i ^ 1 << bit) for i in range(devices)])  44.4 us
    all_to_all x7, starting transfers between devices, to_all(): return lax.all_to_all(copies, AXES, 0, 0)  32.6 us
    all_to_all x7, waiting for transfers between devices, to_all(): return lax.all_to_all(copies, AXES, 0, 0)  29.5 us
    unnamed x95, local copies, waits for them, and re-layouts  29 us
    all_to_all x2, blocking collectives, to_all(): return lax.all_to_all(copies, AXES, 0, 0)  20.4 us
  transfers between devices with their start and end apart: 55, of which 28 were waited for; matrix products, arithmetic and copies ran while one was open for 5% of the time, Pallas kernels for 13%

profile of v4, /device:TPU:0, one launch (start us, length us, event | category | flops | bytes accessed | tf_op | source)
XLA Modules:
  0.0 450.6 jit_solution(5227221588654977505)
XLA Ops:
  10.7 3.0 collective-permute-start
  15.7 4.3 forward_first.1
  21.8 9.5 %all-to-all-start = ((f32[32,3,512]{2,1,0:T(4,128)}), f32[32,3,512]{2,1,0:T(4,128)S(1)}, u32[]{:S(2)}, u32[]{:S(2)}) async-start(f32[32,3,512]{2,1,0:T(4,128)} %get-tuple-element.90), calls=%async_computation | async-start | bytes 524288 | tf_op jit(solution)/shard_map/all_to_all | solution.py:305
  31.3 10.5 %all-to-all-done.refs_2_ = f32[32,3,512]{2,1,0:T(4,128)S(1)} async-done(((f32[32,3,512]{2,1,0:T(4,128)}), f32[32,3,512]{2,1,0:T(4,128)S(1)}, u32[]{:S(2)}, u32[]{:S(2)}) %all-to-all-start) | async-done | bytes 196640 | tf_op jit(solution)/shard_map/all_to_all | solution.py:305
  41.8 10.2 %forward.4 = (f32[608,512]{1,0:T(8,128)S(1)}, f32[32,2,512]{2,1,0:T(2,128)}, f32[608,512]{1,0:T(8,128)S(1)}, f32[3,512]{1,0:T(4,128)S(1)}) custom-call(s32[4]{0:T(128)S(1)} %pad_add_fusion.refs_0_, f32[608,512]{1,0:T(8,128)} %copy-done.11, f32[32,3,512]{2,1,0:T(4,128)S(1)} %all-to-all-done.refs_2_, f32[1,512]{1,0:T(1,128)S(1)} %get-tuple-element.257.refs_3_.refs_5_, ...), custom_call_target="tpu_custom_call" | custom-call | flops 4781506560 | bytes 19802128 | tf_op jit(solution)/shard_map/forward/pallas_call | solution.py:281
  53.1 2.7 all-to-all-start.1
  55.9 8.2 %all-to-all-done.1.refs_2_ = f32[32,2,512]{2,1,0:T(2,128)S(1)} async-done(((f32[32,2,512]{2,1,0:T(2,128)}), f32[32,2,512]{2,1,0:T(2,128)S(1)}, u32[]{:S(2)}, u32[]{:S(2)}) %all-to-all-start.1) | async-done | bytes 131104 | tf_op jit(solution)/shard_map/all_to_all | solution.py:305
  65.4 8.8 %forward.5 = (f32[608,512]{1,0:T(8,128)S(1)}, f32[32,2,512]{2,1,0:T(2,128)S(1)}, f32[608,512]{1,0:T(8,128)S(1)}, f32[3,512]{1,0:T(4,128)S(1)}) custom-call(s32[4]{0:T(128)S(1)} %pad_add_fusion.refs_0_, f32[608,512]{1,0:T(8,128)S(1)} %copy-done.16, f32[32,2,512]{2,1,0:T(2,128)S(1)} %all-to-all-done.1.refs_2_, ...), custom_call_target="tpu_custom_call" | custom-call | flops 4781506560 | bytes 19738640 | tf_op jit(solution)/shard_map/forward/pallas_call | solution.py:281
  75.2 10.1 %all_to_all.45.refs_2_ = f32[32,2,512]{2,1,0:T(2,128)S(1)} all-to-all(f32[32,2,512]{2,1,0:T(2,128)S(1)} %get-tuple-element.95), channel_id=1, replica_groups=mesh['dp'=8,'tm'=4] {'dp','tm'}, dimensions={0} | all-to-all | bytes 262144 | tf_op jit(solution)/shard_map/all_to_all | solution.py:305
  85.3 8.8 %forward.6 = (f32[608,512]{1,0:T(8,128)S(1)}, f32[32,2,512]{2,1,0:T(2,128)S(1)}, f32[608,512]{1,0:T(8,128)S(1)}, f32[3,512]{1,0:T(4,128)S(1)}) custom-call(s32[4]{0:T(128)S(1)} %pad_add_fusion.refs_0_, f32[608,512]{1,0:T(8,128)S(1)} %get-tuple-element.94.refs_1_.refs_8_.refs_2_, f32[32,2,512]{2,1,0:T(2,128)S(1)} %all_to_all.45.refs_2_, ...), custom_call_target="tpu_custom_call" | custom-call | flops 4781506560 | bytes 19738640 | tf_op jit(solution)/shard_map/forward/pallas_call | solution.py:281
  96.3 10.3 %all_to_all.46.refs_2_ = f32[32,2,512]{2,1,0:T(2,128)S(1)} all-to-all(f32[32,2,512]{2,1,0:T(2,128)S(1)} %get-tuple-element.97), channel_id=1, replica_groups=mesh['dp'=8,'tm'=4] {'dp','tm'}, dimensions={0} | all-to-all | bytes 262144 | tf_op jit(solution)/shard_map/all_to_all | solution.py:305
  106.5 9.2 %forward.7 = (f32[608,80]{1,0:T(8,128)S(1)}, f32[32,4,80]{2,1,0:T(4,128)}, f32[608,512]{1,0:T(8,128)S(1)}, f32[3,512]{1,0:T(4,128)S(1)}) custom-call(s32[4]{0:T(128)S(1)} %pad_add_fusion.refs_0_, f32[608,512]{1,0:T(8,128)} %copy-done.7, f32[32,2,512]{2,1,0:T(2,128)S(1)} %all_to_all.46.refs_2_, f32[1,512]{1,0:T(1,128)S(1)} %get-tuple-element.259.refs_3_.refs_5_, ...), custom_call_target="tpu_custom_call" | custom-call | flops 747110400 | bytes 3883024 | tf_op jit(solution)/shard_map/forward/pallas_call | solution.py:281
  119.4 7.4 %all-to-all-done.4.refs_1_ = f32[32,4,80]{2,1,0:T(4,128)S(1)} async-done(((f32[32,4,80]{2,1,0:T(4,128)}), f32[32,4,80]{2,1,0:T(4,128)S(1)}, u32[]{:S(2)}, u32[]{:S(2)}) %all-to-all-start.4) | async-done | bytes 40992 | tf_op jit(solution)/shard_map/all_to_all | solution.py:305
  126.8 5.2 %backward.5 = (f32[608,80]{1,0:T(8,128)S(1)}, f32[2,80]{1,0:T(2,128)S(1)}, f32[2,256,80]{2,1,0:T(8,128)S(1)}, f32[608,512]{1,0:T(8,128)S(1)}, f32[32,2,512]{2,1,0:T(2,128)}) custom-call(s32[4]{0:T(128)S(1)} %pad_add_fusion.refs_0_, f32[32,4,80]{2,1,0:T(4,128)S(1)} %all-to-all-done.4.refs_1_, f32[608,80]{1,0:T(8,128)S(1)} %get-tuple-element.100.refs_2_, ...), custom_call_target="tpu_custom_call" | custom-call | flops 5976883200 | bytes 5651728 | tf_op jit(solution)/shard_map/backward/pallas_call | solution.py:281
  133.1 3.0 all-to-all-start.5
  137.5 3.5 weight_gradient.5
  141.0 3.4 all-to-all-done.5.refs_1_
  144.4 11.4 %backward.6 = (f32[608,512]{1,0:T(8,128)S(1)}, f32[2,512]{1,0:T(2,128)S(1)}, f32[608,512]{1,0:T(8,128)S(1)}, f32[32,2,512]{2,1,0:T(2,128)}) custom-call(s32[4]{0:T(128)S(1)} %pad_add_fusion.refs_0_, f32[32,2,512]{2,1,0:T(2,128)S(1)} %all-to-all-done.5.refs_1_, f32[608,512]{1,0:T(8,128)S(1)} %copy-done.8, f32[608,512]{1,0:T(8,128)} %copy-done.26, ...), custom_call_target="tpu_custom_call" | custom-call | flops 38252052480 | bytes 23480336 | tf_op jit(solution)/shard_map/backward/pallas_call | solution.py:281
  158.0 2.8 all-to-all-start.6
  163.3 7.7 %weight_gradient.6 = f32[5,512,512]{2,1,0:T(8,128)} custom-call(s32[4]{0:T(128)S(1)} %pad_add_fusion.refs_0_, f32[608,512]{1,0:T(8,128)S(1)} %copy-done.23, f32[608,512]{1,0:T(8,128)S(1)} %copy-done.35), custom_call_target="tpu_custom_call" | custom-call | flops 38252052480 | bytes 7733264 | tf_op jit(solution)/shard_map/weight_gradient/pallas_call | solution.py:281
  172.4 11.5 %backward.7 = (f32[608,512]{1,0:T(8,128)S(1)}, f32[2,512]{1,0:T(2,128)S(1)}, f32[608,512]{1,0:T(8,128)S(1)}, f32[32,2,512]{2,1,0:T(2,128)}) custom-call(s32[4]{0:T(128)S(1)} %pad_add_fusion.refs_0_, f32[32,2,512]{2,1,0:T(2,128)S(1)} %all-to-all-done.6.refs_1_, f32[608,512]{1,0:T(8,128)S(1)} %copy-done.21, f32[608,512]{1,0:T(8,128)} %copy-done.31, ...), custom_call_target="tpu_custom_call" | custom-call | flops 38252052480 | bytes 23480336 | tf_op jit(solution)/shard_map/backward/pallas_call | solution.py:281
  186.0 6.0 %all-to-all-start.7 = ((f32[32,2,512]{2,1,0:T(2,128)}), f32[32,2,512]{2,1,0:T(2,128)S(1)}, u32[]{:S(2)}, u32[]{:S(2)}) async-start(f32[32,2,512]{2,1,0:T(2,128)} %get-tuple-element.116), calls=%async_computation.7 | async-start | bytes 262144 | tf_op jit(solution)/shard_map/all_to_all | solution.py:305
  193.8 7.7 %weight_gradient.7 = (f32[5,256,512]{2,1,0:T(8,128)}, f32[5,256,512]{2,1,0:T(8,128)}) custom-call(s32[4]{0:T(128)S(1)} %pad_add_fusion.refs_0_, f32[608,512]{1,0:T(8,128)S(1)} %copy-done.19, f32[608,512]{1,0:T(8,128)S(1)} %copy-done.33), custom_call_target="tpu_custom_call" | custom-call | flops 38252052480 | bytes 7733264 | tf_op jit(solution)/shard_map/weight_gradient/pallas_call | solution.py:281
  202.8 11.5 %backward.8 = (f32[608,512]{1,0:T(8,128)S(1)}, f32[2,512]{1,0:T(2,128)S(1)}, f32[608,512]{1,0:T(8,128)S(1)}, f32[32,2,512]{2,1,0:T(2,128)}) custom-call(s32[4]{0:T(128)S(1)} %pad_add_fusion.refs_0_, f32[32,2,512]{2,1,0:T(2,128)S(1)} %all-to-all-done.7.refs_1_, f32[608,512]{1,0:T(8,128)S(1)} %copy-done.17, f32[608,512]{1,0:T(8,128)} %copy-done.28, ...), custom_call_target="tpu_custom_call" | custom-call | flops 38252052480 | bytes 23480336 | tf_op jit(solution)/shard_map/backward/pallas_call | solution.py:281
  216.4 6.0 %all-to-all-start.8 = ((f32[32,2,512]{2,1,0:T(2,128)}), f32[32,2,512]{2,1,0:T(2,128)S(1)}, u32[]{:S(2)}, u32[]{:S(2)}) async-start(f32[32,2,512]{2,1,0:T(2,128)} %get-tuple-element.123), calls=%async_computation.8 | async-start | bytes 262144 | tf_op jit(solution)/shard_map/all_to_all | solution.py:305
  222.4 3.3 add.55
  233.3 7.8 %weight_gradient.8 = (f32[5,256,512]{2,1,0:T(8,128)}, f32[5,256,512]{2,1,0:T(8,128)}) custom-call(s32[4]{0:T(128)S(1)} %pad_add_fusion.refs_0_, f32[608,512]{1,0:T(8,128)S(1)} %copy-done.14, f32[608,512]{1,0:T(8,128)S(1)} %copy-done.30), custom_call_target="tpu_custom_call" | custom-call | flops 38252052480 | bytes 7733264 | tf_op jit(solution)/shard_map/weight_gradient/pallas_call | solution.py:281
  241.2 6.3 %collective-permute-done.5 = f32[192,512]{1,0:T(8,128)} collective-permute-done((f32[192,512]{1,0:T(8,128)}, f32[192,512]{1,0:T(8,128)}, u32[]{:S(2)}, u32[]{:S(2)}) %collective-permute-start.5) | collective-permute-done | bytes 393248 | tf_op jit(solution)/shard_map/ppermute | solution.py:310
  255.2 9.1 %backward.9 = (f32[608,512]{1,0:T(8,128)S(1)}, f32[2,512]{1,0:T(2,128)S(1)}, f32[2,256,80]{2,1,0:T(8,128)S(1)}) custom-call(s32[4]{0:T(128)S(1)} %pad_add_fusion.refs_0_, f32[32,2,512]{2,1,0:T(2,128)S(1)} %all-to-all-done.8.refs_1_, f32[608,512]{1,0:T(8,128)S(1)} %copy-done.12, f32[608,512]{1,0:T(8,128)} %copy-done.27, f32[3,512]{1,0:T(4,128)S(1)} %copy-done.1, ...), custom_call_target="tpu_custom_call" | custom-call | flops 5976883200 | bytes 5025808 | tf_op jit(solution)/shard_map/backward/pallas_call | solution.py:281
  267.2 2.6 weight_gradient.9
  276.6 5.4 %collective-permute-done.35 = f32[80,512]{1,0:T(8,128)S(1)} collective-permute-done((f32[80,512]{1,0:T(8,128)S(1)}, f32[80,512]{1,0:T(8,128)S(1)}, u32[]{:S(2)}, u32[]{:S(2)}) %collective-permute-start.35) | collective-permute-done | bytes 163872 | tf_op jit(solution)/shard_map/ppermute | solution.py:310
  282.2 10.9 %collective-permute-done.36 = f32[80,512]{1,0:T(8,128)S(1)} collective-permute-done((f32[80,512]{1,0:T(8,128)S(1)}, f32[80,512]{1,0:T(8,128)S(1)}, u32[]{:S(2)}, u32[]{:S(2)}) %collective-permute-start.36) | collective-permute-done | bytes 163872 | tf_op jit(solution)/shard_map/ppermute | solution.py:310
  296.8 3.6 collective-permute-done.18
  300.7 15.6 %collective-permute-done.8 = f32[128,512]{1,0:T(8,128)S(1)} collective-permute-done((f32[128,512]{1,0:T(8,128)S(1)}, f32[128,512]{1,0:T(8,128)S(1)}, u32[]{:S(2)}, u32[]{:S(2)}) %collective-permute-start.8) | collective-permute-done | bytes 262176 | tf_op jit(solution)/shard_map/ppermute | solution.py:310
  316.4 3.4 collective-permute-start.9
  319.8 6.5 %collective-permute-done.9 = f32[64,512]{1,0:T(8,128)S(1)} collective-permute-done((f32[64,512]{1,0:T(8,128)S(1)}, f32[64,512]{1,0:T(8,128)S(1)}, u32[]{:S(2)}, u32[]{:S(2)}) %collective-permute-start.9) | collective-permute-done | bytes 131104 | tf_op jit(solution)/shard_map/ppermute | solution.py:310
  333.8 5.7 %collective-permute-done.15 = f32[128,512]{1,0:T(8,128)S(1)} collective-permute-done((f32[128,512]{1,0:T(8,128)S(1)}, f32[128,512]{1,0:T(8,128)S(1)}, u32[]{:S(2)}, u32[]{:S(2)}) %collective-permute-start.15) | collective-permute-done | bytes 262176 | tf_op jit(solution)/shard_map/ppermute | solution.py:310
  345.7 2.8 collective-permute-done.42
  348.6 2.7 collective-permute-done.41
  351.3 9.2 %collective-permute-done.20 = f32[96,512]{1,0:T(8,128)S(1)} collective-permute-done((f32[96,512]{1,0:T(8,128)S(1)}, f32[96,512]{1,0:T(8,128)S(1)}, u32[]{:S(2)}, u32[]{:S(2)}) %collective-permute-start.20) | collective-permute-done | bytes 196640 | tf_op jit(solution)/shard_map/ppermute | solution.py:310
  361.3 12.0 %collective-permute-done.21 = f32[96,512]{1,0:T(8,128)S(1)} collective-permute-done((f32[96,512]{1,0:T(8,128)S(1)}, f32[96,512]{1,0:T(8,128)S(1)}, u32[]{:S(2)}, u32[]{:S(2)}) %collective-permute-start.21) | collective-permute-done | bytes 196640 | tf_op jit(solution)/shard_map/ppermute | solution.py:310
  378.4 3.7 collective-permute-done.22
  384.3 12.5 %collective-permute-done.45 = f32[192,512]{1,0:T(8,128)S(1)} collective-permute-done((f32[192,512]{1,0:T(8,128)S(1)}, f32[192,512]{1,0:T(8,128)S(1)}, u32[]{:S(2)}, u32[]{:S(2)}) %collective-permute-start.45) | collective-permute-done | bytes 393248 | tf_op jit(solution)/shard_map/ppermute | solution.py:310
  399.1 6.8 %collective-permute-done.23 = f32[128,512]{1,0:T(8,128)S(1)} collective-permute-done((f32[128,512]{1,0:T(8,128)S(1)}, f32[128,512]{1,0:T(8,128)S(1)}, u32[]{:S(2)}, u32[]{:S(2)}) %collective-permute-start.23) | collective-permute-done | bytes 262176 | tf_op jit(solution)/shard_map/ppermute | solution.py:310
  409.0 6.3 %collective-permute-done.24 = f32[256,512]{1,0:T(8,128)S(1)} collective-permute-done((f32[256,512]{1,0:T(8,128)S(1)}, f32[256,512]{1,0:T(8,128)S(1)}, u32[]{:S(2)}, u32[]{:S(2)}) %collective-permute-start.24) | collective-permute-done | bytes 524320 | tf_op jit(solution)/shard_map/ppermute | solution.py:310
  423.5 4.9 %place_whole.1.refs_3_ = f32[3,5,512,512]{3,2,1,0:T(8,128)} custom-call(f32[5,512,512]{2,1,0:T(8,128)} %get-tuple-element.178.refs_0_), custom_call_target="tpu_custom_call" | custom-call | tf_op jit(solution)/shard_map/place_whole/pallas_call | solution.py:281
  431.0 4.2 place.2.refs_3_
  437.3 5.3 %place.3 = f32[3,5,512,512]{3,2,1,0:T(8,128)} custom-call(s32[4]{0:T(128)S(1)} %pad_add_fusion.refs_0_, f32[1536,512]{1,0:T(8,128)} %get-tuple-element.180.refs_1_, f32[1536,512]{1,0:T(8,128)} %collective-permute-done.31.refs_2_, f32[3,5,512,512]{3,2,1,0:T(8,128)} %place.2.refs_3_), custom_call_target="tpu_custom_call", output_to_operand_aliasing={{}: (3, {})} | custom-call | tf_op jit(solution)/shard_map/place/pallas_call | solution.py:281
  (277 shorter events, 101.6 us)
Async XLA Ops:
  21.8 20.0 %all-to-all-start = ((f32[32,3,512]{2,1,0:T(4,128)}), f32[32,3,512]{2,1,0:T(4,128)S(1)}, u32[]{:S(2)}, u32[]{:S(2)}) async-start(f32[32,3,512]{2,1,0:T(4,128)} %get-tuple-element.90), calls=%async_computation | async-start | bytes 524288 | tf_op jit(solution)/shard_map/all_to_all | solution.py:305
  53.1 10.9 %all-to-all-start.1 = ((f32[32,2,512]{2,1,0:T(2,128)}), f32[32,2,512]{2,1,0:T(2,128)S(1)}, u32[]{:S(2)}, u32[]{:S(2)}) async-start(f32[32,2,512]{2,1,0:T(2,128)} %get-tuple-element.92), calls=%async_computation.1 | async-start | bytes 262144 | tf_op jit(solution)/shard_map/all_to_all | solution.py:305
  116.8 10.0 %all-to-all-start.4 = ((f32[32,4,80]{2,1,0:T(4,128)}), f32[32,4,80]{2,1,0:T(4,128)S(1)}, u32[]{:S(2)}, u32[]{:S(2)}) async-start(f32[32,4,80]{2,1,0:T(4,128)} %get-tuple-element.99), calls=%async_computation.4 | async-start | bytes 131072 | tf_op jit(solution)/shard_map/all_to_all | solution.py:305
  133.1 11.2 %all-to-all-start.5 = ((f32[32,2,512]{2,1,0:T(2,128)}), f32[32,2,512]{2,1,0:T(2,128)S(1)}, u32[]{:S(2)}, u32[]{:S(2)}) async-start(f32[32,2,512]{2,1,0:T(2,128)} %get-tuple-element.104), calls=%async_computation.5 | async-start | bytes 262144 | tf_op jit(solution)/shard_map/all_to_all | solution.py:305
  158.0 13.1 %all-to-all-start.6 = ((f32[32,2,512]{2,1,0:T(2,128)}), f32[32,2,512]{2,1,0:T(2,128)S(1)}, u32[]{:S(2)}, u32[]{:S(2)}) async-start(f32[32,2,512]{2,1,0:T(2,128)} %get-tuple-element.110), calls=%async_computation.6 | async-start | bytes 262144 | tf_op jit(solution)/shard_map/all_to_all | solution.py:305
  186.0 15.5 %all-to-all-start.7 = ((f32[32,2,512]{2,1,0:T(2,128)}), f32[32,2,512]{2,1,0:T(2,128)S(1)}, u32[]{:S(2)}, u32[]{:S(2)}) async-start(f32[32,2,512]{2,1,0:T(2,128)} %get-tuple-element.116), calls=%async_computation.7 | async-start | bytes 262144 | tf_op jit(solution)/shard_map/all_to_all | solution.py:305
  192.0 231.4 %all-reduce.4.cloned.1.call-start = ((), (), s32[]{:S(2)}) async-start(), calls=%async_computation.9 | async-start | bytes 12124160 | tf_op jit(solution)/shard_map/psum | solution.py:497
  201.5 20.9 %collective-permute-start.2 = (f32[1280,512]{1,0:T(8,128)}, f32[1280,512]{1,0:T(8,128)}, u32[]{:S(2)}, u32[]{:S(2)}) collective-permute-start(f32[1280,512]{1,0:T(8,128)} %bitcast.37), channel_id=1, source_target_pairs={{0,1},{1,0},{2,3},{3,2},{4,5},{5,4},{6,7},{7,6},{8,9},{9,8},{10,11... | collective-permute-start | bytes 7864328 | tf_op jit(solution)/shard_map/ppermute | solution.py:310
  216.4 24.7 %all-to-all-start.8 = ((f32[32,2,512]{2,1,0:T(2,128)}), f32[32,2,512]{2,1,0:T(2,128)S(1)}, u32[]{:S(2)}, u32[]{:S(2)}) async-start(f32[32,2,512]{2,1,0:T(2,128)} %get-tuple-element.123), calls=%async_computation.8 | async-start | bytes 262144 | tf_op jit(solution)/shard_map/all_to_all | solution.py:305
  226.8 20.7 %collective-permute-start.5 = (f32[192,512]{1,0:T(8,128)}, f32[192,512]{1,0:T(8,128)}, u32[]{:S(2)}, u32[]{:S(2)}) collective-permute-start(f32[192,512]{1,0:T(8,128)} %slice_select_fusion.5), channel_id=1, source_target_pairs={{0,8},{1,9},{2,10},{3,11},{4,12},{5,13},{6,14},{7,15},{8,0},{9,1},... | collective-permute-start | bytes 1179656 | tf_op jit(solution)/shard_map/ppermute | solution.py:310
  229.5 19.4 %collective-permute-start.4 = (f32[192,512]{1,0:T(8,128)}, f32[192,512]{1,0:T(8,128)}, u32[]{:S(2)}, u32[]{:S(2)}) collective-permute-start(f32[192,512]{1,0:T(8,128)} %slice_select_fusion.6), channel_id=1, source_target_pairs={{0,4},{1,5},{2,6},{3,7},{4,0},{5,1},{6,2},{7,3},{8,12},{9,13},{10,... | collective-permute-start | bytes 1179656 | tf_op jit(solution)/shard_map/ppermute | solution.py:310
  231.8 18.3 %collective-permute-start.3 = (f32[256,512]{1,0:T(8,128)}, f32[256,512]{1,0:T(8,128)S(1)}, u32[]{:S(2)}, u32[]{:S(2)}) collective-permute-start(f32[256,512]{1,0:T(8,128)} %slice_select_fusion.2), channel_id=1, source_target_pairs={{0,2},{1,3},{2,0},{3,1},{4,6},{5,7},{6,4},{7,5},{8,10},{9,11},{10,... | collective-permute-start | bytes 1572872 | tf_op jit(solution)/shard_map/ppermute | solution.py:310
  241.1 33.0 %collective-permute-start.6 = (f32[1280,512]{1,0:T(8,128)}, f32[1280,512]{1,0:T(8,128)S(1)}, u32[]{:S(2)}, u32[]{:S(2)}) collective-permute-start(f32[1280,512]{1,0:T(8,128)} %bitcast.36), channel_id=1, source_target_pairs={{0,1},{1,0},{2,3},{3,2},{4,5},{5,4},{6,7},{7,6},{8,9},{9,8},{10,11... | collective-permute-start | bytes 7864328 | tf_op jit(solution)/shard_map/ppermute | solution.py:310
  250.4 13.9 %collective-permute-start.12 = (f32[96,512]{1,0:T(8,128)S(1)}, f32[96,512]{1,0:T(8,128)S(1)}, u32[]{:S(2)}, u32[]{:S(2)}) collective-permute-start(f32[96,512]{1,0:T(8,128)S(1)} %slice_select_fusion.11), channel_id=1, source_target_pairs={{0,2},{1,3},{2,0},{3,1},{4,6},{5,7},{6,4},{7,5},{8,10},{9,11},{10,... | collective-permute-start | bytes 589832 | tf_op jit(solution)/shard_map/ppermute | solution.py:310
  252.2 12.1 %collective-permute-start.11 = (f32[96,512]{1,0:T(8,128)S(1)}, f32[96,512]{1,0:T(8,128)S(1)}, u32[]{:S(2)}, u32[]{:S(2)}) collective-permute-start(f32[96,512]{1,0:T(8,128)S(1)} %slice_select_fusion.12), channel_id=1, source_target_pairs={{0,8},{1,9},{2,10},{3,11},{4,12},{5,13},{6,14},{7,15},{8,0},{9,1},... | collective-permute-start | bytes 589832 | tf_op jit(solution)/shard_map/ppermute | solution.py:310
  253.6 10.8 %collective-permute-start.10 = (f32[128,512]{1,0:T(8,128)S(1)}, f32[128,512]{1,0:T(8,128)S(1)}, u32[]{:S(2)}, u32[]{:S(2)}) collective-permute-start(f32[128,512]{1,0:T(8,128)S(1)} %slice_select_fusion.10), channel_id=1, source_target_pairs={{0,4},{1,5},{2,6},{3,7},{4,0},{5,1},{6,2},{7,3},{8,12},{9,13},{10,... | collective-permute-start | bytes 786440 | tf_op jit(solution)/shard_map/ppermute | solution.py:310
  264.5 7.1 %collective-permute-start.34 = (f32[64,512]{1,0:T(8,128)S(1)}, f32[64,512]{1,0:T(8,128)S(1)}, u32[]{:S(2)}, u32[]{:S(2)}) collective-permute-start(f32[64,512]{1,0:T(8,128)S(1)} %slice_select_fusion.16), channel_id=1, source_target_pairs={{0,8},{1,9},{2,10},{3,11},{4,12},{5,13},{6,14},{7,15},{8,0},{9,1},... | collective-permute-start | bytes 393224 | tf_op jit(solution)/shard_map/ppermute | solution.py:310
  269.8 12.3 %collective-permute-start.13 = (f32[200,512]{1,0:T(8,128)S(1)}, f32[200,512]{1,0:T(8,128)S(1)}, u32[]{:S(2)}, u32[]{:S(2)}) collective-permute-start(f32[200,512]{1,0:T(8,128)S(1)} %bitcast.29), channel_id=1, source_target_pairs={{0,1},{1,0},{2,3},{3,2},{4,5},{5,4},{6,7},{7,6},{8,9},{9,8},{10,11... | collective-permute-start | bytes 1228808 | tf_op jit(solution)/shard_map/ppermute | solution.py:310
  271.6 10.4 %collective-permute-start.35 = (f32[80,512]{1,0:T(8,128)S(1)}, f32[80,512]{1,0:T(8,128)S(1)}, u32[]{:S(2)}, u32[]{:S(2)}) collective-permute-start(f32[80,512]{1,0:T(8,128)S(1)} %fusion.3), channel_id=1, source_target_pairs={{0,16},{1,17},{2,18},{3,19},{4,20},{5,21},{6,22},{7,23},{8,24},{9,... | collective-permute-start | bytes 491528 | tf_op jit(solution)/shard_map/ppermute | solution.py:310
  274.9 18.2 %collective-permute-start.17 = (f32[256,512]{1,0:T(8,128)S(1)}, f32[256,512]{1,0:T(8,128)S(1)}, u32[]{:S(2)}, u32[]{:S(2)}) collective-permute-start(f32[256,512]{1,0:T(8,128)S(1)} %get-tuple-element.187), channel_id=1, source_target_pairs={{0,2},{1,3},{2,0},{3,1},{4,6},{5,7},{6,4},{7,5},{8,10},{9,11},{10,... | collective-permute-start | bytes 1572872 | tf_op jit(solution)/shard_map/ppermute | solution.py:310
  275.9 17.3 %collective-permute-start.7 = (f32[256,512]{1,0:T(8,128)S(1)}, f32[256,512]{1,0:T(8,128)S(1)}, u32[]{:S(2)}, u32[]{:S(2)}) collective-permute-start(f32[256,512]{1,0:T(8,128)S(1)} %get-tuple-element.188), channel_id=1, source_target_pairs={{0,4},{1,5},{2,6},{3,7},{4,0},{5,1},{6,2},{7,3},{8,12},{9,13},{10,... | collective-permute-start | bytes 1572872 | tf_op jit(solution)/shard_map/ppermute | solution.py:310
  282.1 11.1 %collective-permute-start.36 = (f32[80,512]{1,0:T(8,128)S(1)}, f32[80,512]{1,0:T(8,128)S(1)}, u32[]{:S(2)}, u32[]{:S(2)}) collective-permute-start(f32[80,512]{1,0:T(8,128)S(1)} %select_add_fusion.12), channel_id=1, source_target_pairs={{0,16},{1,17},{2,18},{3,19},{4,20},{5,21},{6,22},{7,23},{8,24},{9,... | collective-permute-start | bytes 491528 | tf_op jit(solution)/shard_map/ppermute | solution.py:310
  293.7 6.7 %collective-permute-start.18 = (f32[128,512]{1,0:T(8,128)S(1)}, f32[128,512]{1,0:T(8,128)S(1)}, u32[]{:S(2)}, u32[]{:S(2)}) collective-permute-start(f32[128,512]{1,0:T(8,128)S(1)} %slice_select_fusion.7), channel_id=1, source_target_pairs={{0,4},{1,5},{2,6},{3,7},{4,0},{5,1},{6,2},{7,3},{8,12},{9,13},{10,... | collective-permute-start | bytes 786440 | tf_op jit(solution)/shard_map/ppermute | solution.py:310
  294.6 31.8 %collective-permute-start.14 = (f32[256,512]{1,0:T(8,128)S(1)}, f32[256,512]{1,0:T(8,128)S(1)}, u32[]{:S(2)}, u32[]{:S(2)}) collective-permute-start(f32[256,512]{1,0:T(8,128)S(1)} %get-tuple-element.185), channel_id=1, source_target_pairs={{0,8},{1,9},{2,10},{3,11},{4,12},{5,13},{6,14},{7,15},{8,0},{9,1},... | collective-permute-start | bytes 1572872 | tf_op jit(solution)/shard_map/ppermute | solution.py:310
  294.8 21.6 %collective-permute-start.8 = (f32[128,512]{1,0:T(8,128)S(1)}, f32[128,512]{1,0:T(8,128)S(1)}, u32[]{:S(2)}, u32[]{:S(2)}) collective-permute-start(f32[128,512]{1,0:T(8,128)S(1)} %slice_select_fusion.9), channel_id=1, source_target_pairs={{0,8},{1,9},{2,10},{3,11},{4,12},{5,13},{6,14},{7,15},{8,0},{9,1},... | collective-permute-start | bytes 786440 | tf_op jit(solution)/shard_map/ppermute | solution.py:310
  300.5 19.3 %collective-permute-start.19 = (f32[64,512]{1,0:T(8,128)S(1)}, f32[64,512]{1,0:T(8,128)S(1)}, u32[]{:S(2)}, u32[]{:S(2)}) collective-permute-start(f32[64,512]{1,0:T(8,128)S(1)} %slice_select_fusion.13), channel_id=1, source_target_pairs={{0,8},{1,9},{2,10},{3,11},{4,12},{5,13},{6,14},{7,15},{8,0},{9,1},... | collective-permute-start | bytes 393224 | tf_op jit(solution)/shard_map/ppermute | solution.py:310
  316.4 9.9 %collective-permute-start.9 = (f32[64,512]{1,0:T(8,128)S(1)}, f32[64,512]{1,0:T(8,128)S(1)}, u32[]{:S(2)}, u32[]{:S(2)}) collective-permute-start(f32[64,512]{1,0:T(8,128)S(1)} %slice_select_fusion.15), channel_id=1, source_target_pairs={{0,2},{1,3},{2,0},{3,1},{4,6},{5,7},{6,4},{7,5},{8,10},{9,11},{10,... | collective-permute-start | bytes 393224 | tf_op jit(solution)/shard_map/ppermute | solution.py:310
  330.8 9.1 %collective-permute-start.37 = (f32[64,512]{1,0:T(8,128)S(1)}, f32[64,512]{1,0:T(8,128)S(1)}, u32[]{:S(2)}, u32[]{:S(2)}) collective-permute-start(f32[64,512]{1,0:T(8,128)S(1)} %slice.291), channel_id=1, source_target_pairs={{0,8},{1,9},{2,10},{3,11},{4,12},{5,13},{6,14},{7,15},{8,0},{9,1},... | collective-permute-start | bytes 393224 | tf_op jit(solution)/shard_map/ppermute | solution.py:310
  331.0 8.5 %collective-permute-start.15 = (f32[128,512]{1,0:T(8,128)S(1)}, f32[128,512]{1,0:T(8,128)S(1)}, u32[]{:S(2)}, u32[]{:S(2)}) collective-permute-start(f32[128,512]{1,0:T(8,128)S(1)} %slice_select_fusion.8), channel_id=1, source_target_pairs={{0,2},{1,3},{2,0},{3,1},{4,6},{5,7},{6,4},{7,5},{8,10},{9,11},{10,... | collective-permute-start | bytes 786440 | tf_op jit(solution)/shard_map/ppermute | solution.py:310
  340.0 8.5 %collective-permute-start.42 = (f32[96,512]{1,0:T(8,128)S(1)}, f32[96,512]{1,0:T(8,128)S(1)}, u32[]{:S(2)}, u32[]{:S(2)}) collective-permute-start(f32[96,512]{1,0:T(8,128)S(1)} %pad_maximum_fusion.19), channel_id=1, source_target_pairs={{0,2},{1,3},{2,0},{3,1},{4,6},{5,7},{6,4},{7,5},{8,10},{9,11},{10,... | collective-permute-start | bytes 589832 | tf_op jit(solution)/shard_map/ppermute | solution.py:310
  340.2 11.1 %collective-permute-start.41 = (f32[96,512]{1,0:T(8,128)S(1)}, f32[96,512]{1,0:T(8,128)S(1)}, u32[]{:S(2)}, u32[]{:S(2)}) collective-permute-start(f32[96,512]{1,0:T(8,128)S(1)} %pad_maximum_fusion.18), channel_id=1, source_target_pairs={{0,8},{1,9},{2,10},{3,11},{4,12},{5,13},{6,14},{7,15},{8,0},{9,1},... | collective-permute-start | bytes 589832 | tf_op jit(solution)/shard_map/ppermute | solution.py:310
  342.1 32.5 %collective-permute-start.40 = (f32[128,512]{1,0:T(8,128)S(1)}, f32[128,512]{1,0:T(8,128)S(1)}, u32[]{:S(2)}, u32[]{:S(2)}) collective-permute-start(f32[128,512]{1,0:T(8,128)S(1)} %pad_maximum_fusion.15), channel_id=1, source_target_pairs={{0,4},{1,5},{2,6},{3,7},{4,0},{5,1},{6,2},{7,3},{8,12},{9,13},{10,... | collective-permute-start | bytes 786440 | tf_op jit(solution)/shard_map/ppermute | solution.py:310
  345.1 15.4 %collective-permute-start.20 = (f32[96,512]{1,0:T(8,128)S(1)}, f32[96,512]{1,0:T(8,128)S(1)}, u32[]{:S(2)}, u32[]{:S(2)}) collective-permute-start(f32[96,512]{1,0:T(8,128)S(1)} %fusion.2), channel_id=1, source_target_pairs={{0,16},{1,17},{2,18},{3,19},{4,20},{5,21},{6,22},{7,23},{8,24},{9,... | collective-permute-start | bytes 589832 | tf_op jit(solution)/shard_map/ppermute | solution.py:310
  360.6 12.7 %collective-permute-start.21 = (f32[96,512]{1,0:T(8,128)S(1)}, f32[96,512]{1,0:T(8,128)S(1)}, u32[]{:S(2)}, u32[]{:S(2)}) collective-permute-start(f32[96,512]{1,0:T(8,128)S(1)} %select_add_fusion.9), channel_id=1, source_target_pairs={{0,16},{1,17},{2,18},{3,19},{4,20},{5,21},{6,22},{7,23},{8,24},{9,... | collective-permute-start | bytes 589832 | tf_op jit(solution)/shard_map/ppermute | solution.py:310
  373.4 8.7 %collective-permute-start.22 = (f32[64,512]{1,0:T(8,128)S(1)}, f32[64,512]{1,0:T(8,128)S(1)}, u32[]{:S(2)}, u32[]{:S(2)}) collective-permute-start(f32[64,512]{1,0:T(8,128)S(1)} %slice.328), channel_id=1, source_target_pairs={{0,8},{1,9},{2,10},{3,11},{4,12},{5,13},{6,14},{7,15},{8,0},{9,1},... | collective-permute-start | bytes 393224 | tf_op jit(solution)/shard_map/ppermute | solution.py:310
  373.5 8.6 %collective-permute-start.28 = (f32[64,512]{1,0:T(8,128)S(1)}, f32[64,512]{1,0:T(8,128)S(1)}, u32[]{:S(2)}, u32[]{:S(2)}) collective-permute-start(f32[64,512]{1,0:T(8,128)S(1)} %slice.331), channel_id=1, source_target_pairs={{0,4},{1,5},{2,6},{3,7},{4,0},{5,1},{6,2},{7,3},{8,12},{9,13},{10,... | collective-permute-start | bytes 393224 | tf_op jit(solution)/shard_map/ppermute | solution.py:310
  374.6 22.1 %collective-permute-start.45 = (f32[192,512]{1,0:T(8,128)S(1)}, f32[192,512]{1,0:T(8,128)S(1)}, u32[]{:S(2)}, u32[]{:S(2)}) collective-permute-start(f32[192,512]{1,0:T(8,128)S(1)} %pad_maximum_fusion.10), channel_id=1, source_target_pairs={{0,8},{1,9},{2,10},{3,11},{4,12},{5,13},{6,14},{7,15},{8,0},{9,1},... | collective-permute-start | bytes 1179656 | tf_op jit(solution)/shard_map/ppermute | solution.py:310
  376.7 21.9 %collective-permute-start.44 = (f32[192,512]{1,0:T(8,128)S(1)}, f32[192,512]{1,0:T(8,128)S(1)}, u32[]{:S(2)}, u32[]{:S(2)}) collective-permute-start(f32[192,512]{1,0:T(8,128)S(1)} %pad_maximum_fusion.9), channel_id=1, source_target_pairs={{0,4},{1,5},{2,6},{3,7},{4,0},{5,1},{6,2},{7,3},{8,12},{9,13},{10,... | collective-permute-start | bytes 1179656 | tf_op jit(solution)/shard_map/ppermute | solution.py:310
  377.7 21.2 %collective-permute-start.43 = (f32[256,512]{1,0:T(8,128)S(1)}, f32[256,512]{1,0:T(8,128)S(1)}, u32[]{:S(2)}, u32[]{:S(2)}) collective-permute-start(f32[256,512]{1,0:T(8,128)S(1)} %pad_maximum_fusion.7), channel_id=1, source_target_pairs={{0,2},{1,3},{2,0},{3,1},{4,6},{5,7},{6,4},{7,5},{8,10},{9,11},{10,... | collective-permute-start | bytes 1572872 | tf_op jit(solution)/shard_map/ppermute | solution.py:310
  382.2 25.3 %collective-permute-start.29 = (f32[128,512]{1,0:T(8,128)S(1)}, f32[128,512]{1,0:T(8,128)S(1)}, u32[]{:S(2)}, u32[]{:S(2)}) collective-permute-start(f32[128,512]{1,0:T(8,128)S(1)} %pad_maximum_fusion.14), channel_id=1, source_target_pairs={{0,2},{1,3},{2,0},{3,1},{4,6},{5,7},{6,4},{7,5},{8,10},{9,11},{10,... | collective-permute-start | bytes 786440 | tf_op jit(solution)/shard_map/ppermute | solution.py:310
  382.9 15.9 %collective-permute-start.25 = (f32[64,512]{1,0:T(8,128)S(1)}, f32[64,512]{1,0:T(8,128)S(1)}, u32[]{:S(2)}, u32[]{:S(2)}) collective-permute-start(f32[64,512]{1,0:T(8,128)S(1)} %get-tuple-element.233), channel_id=1, source_target_pairs={{0,2},{1,3},{2,0},{3,1},{4,6},{5,7},{6,4},{7,5},{8,10},{9,11},{10,... | collective-permute-start | bytes 393224 | tf_op jit(solution)/shard_map/ppermute | solution.py:310
  396.7 9.2 %collective-permute-start.23 = (f32[128,512]{1,0:T(8,128)S(1)}, f32[128,512]{1,0:T(8,128)S(1)}, u32[]{:S(2)}, u32[]{:S(2)}) collective-permute-start(f32[128,512]{1,0:T(8,128)S(1)} %pad_maximum_fusion.12), channel_id=1, source_target_pairs={{0,4},{1,5},{2,6},{3,7},{4,0},{5,1},{6,2},{7,3},{8,12},{9,13},{10,... | collective-permute-start | bytes 786440 | tf_op jit(solution)/shard_map/ppermute | solution.py:310
  398.9 9.2 %collective-permute-start.26 = (f32[128,512]{1,0:T(8,128)S(1)}, f32[128,512]{1,0:T(8,128)S(1)}, u32[]{:S(2)}, u32[]{:S(2)}) collective-permute-start(f32[128,512]{1,0:T(8,128)S(1)} %pad_maximum_fusion.13), channel_id=1, source_target_pairs={{0,8},{1,9},{2,10},{3,11},{4,12},{5,13},{6,14},{7,15},{8,0},{9,1},... | collective-permute-start | bytes 786440 | tf_op jit(solution)/shard_map/ppermute | solution.py:310
  406.0 9.2 %collective-permute-start.24 = (f32[256,512]{1,0:T(8,128)S(1)}, f32[256,512]{1,0:T(8,128)S(1)}, u32[]{:S(2)}, u32[]{:S(2)}) collective-permute-start(f32[256,512]{1,0:T(8,128)S(1)} %pad_maximum_fusion.4), channel_id=1, source_target_pairs={{0,2},{1,3},{2,0},{3,1},{4,6},{5,7},{6,4},{7,5},{8,10},{9,11},{10,... | collective-permute-start | bytes 1572872 | tf_op jit(solution)/shard_map/ppermute | solution.py:310
  408.2 9.2 %collective-permute-start.27 = (f32[256,512]{1,0:T(8,128)S(1)}, f32[256,512]{1,0:T(8,128)S(1)}, u32[]{:S(2)}, u32[]{:S(2)}) collective-permute-start(f32[256,512]{1,0:T(8,128)S(1)} %pad_maximum_fusion.5), channel_id=1, source_target_pairs={{0,4},{1,5},{2,6},{3,7},{4,0},{5,1},{6,2},{7,3},{8,12},{9,13},{10,... | collective-permute-start | bytes 1572872 | tf_op jit(solution)/shard_map/ppermute | solution.py:310
  408.9 10.4 %collective-permute-start.30 = (f32[256,512]{1,0:T(8,128)S(1)}, f32[256,512]{1,0:T(8,128)S(1)}, u32[]{:S(2)}, u32[]{:S(2)}) collective-permute-start(f32[256,512]{1,0:T(8,128)S(1)} %pad_maximum_fusion.6), channel_id=1, source_target_pairs={{0,8},{1,9},{2,10},{3,11},{4,12},{5,13},{6,14},{7,15},{8,0},{9,1},... | collective-permute-start | bytes 1572872 | tf_op jit(solution)/shard_map/ppermute | solution.py:310
  421.2 13.9 %collective-permute-start.31 = (f32[1536,512]{1,0:T(8,128)}, f32[1536,512]{1,0:T(8,128)}, u32[]{:S(2)}, u32[]{:S(2)}) collective-permute-start(f32[1536,512]{1,0:T(8,128)} %get-tuple-element.180.refs_1_), channel_id=1, source_target_pairs={{0,1},{1,0},{2,3},{3,2},{4,5},{5,4},{6,7},{7,6},{8,9},{9,8},{10,11... | collective-permute-start | bytes 9437192 | tf_op jit(solution)/shard_map/ppermute | solution.py:310
  421.5 9.5 %collective-permute-start.46 = (f32[1280,512]{1,0:T(8,128)S(1)}, f32[1280,512]{1,0:T(8,128)}, u32[]{:S(2)}, u32[]{:S(2)}) collective-permute-start(f32[1280,512]{1,0:T(8,128)S(1)} %constant_dynamic-update-slice_fusion.1.refs_1_), channel_id=1, source_target_pairs={{0,1},{1,0},{2,3},{3,2},{4,5},{5,4},{6,7},{7,6},{8,9},{9,8},{10,11... | collective-permute-start | bytes 7864328 | tf_op jit(solution)/shard_map/ppermute | solution.py:310
  (51 other events, 480.8 us)
Sparse Core Ops, SparseCore 0:
  201.7 195.6 all-reduce.3

commit v5 on v4

--- a/solution.py
+++ b/solution.py
@@ -519,9 +519,11 @@
 
     while late.steps:
         late.advance()
-        if early.steps:
+        if early.steps and len(late.steps) <= len(early.steps) + 1:
             early.advance()
             early.state, _ = lax.optimization_barrier((early.state, late.state))
+    while early.steps:
+        early.advance()
     half = channels // 2
     small = (width, mels // 2, channels)
     mid_rows, small_rows = width * half, width * mels // 2

time: 458 us -> 455 us (level)
  waiting for transfers between devices: 148 us -> 139 us
  starting transfers between devices: 81.7 us -> 87.1 us
    ppermute x45, waiting for transfers between devices: 118 us -> 110 us  [swap(): return lax.ppermute(x, AXES, [(i, i ^ 1 << bit) for i in range(devices)])]
    ppermute x45, starting transfers between devices: 44.4 us -> 49.8 us  [swap(): return lax.ppermute(x, AXES, [(i, i ^ 1 << bit) for i in range(devices)])]
  transfers between devices with their start and end apart: 55 -> 55, of which waited for: 28 -> 27; matrix products, arithmetic and copies ran while one was open for 5% -> 5% of each run, Pallas kernels for 13% -> 13%
where the time goes in v5:
time: 455 us; the launch traced here: 448 us
  waiting for transfers between devices  139 us (31%)
  Pallas kernels  134 us (29%)
  starting transfers between devices  87.1 us (19%)
  local copies, waits for them, and re-layouts  29.9 us (7%)
  other arithmetic  21.6 us (5%)
  blocking collectives  20.4 us (4%)
  between operations  15.6 us (3%)
    pallas_call x18, Pallas kernels, call(): pl.pallas_call(kernel, name=name, out_shape=list(outs.values()), in_specs...  134 us
    ppermute x45, waiting for transfers between devices, swap(): return lax.ppermute(x, AXES, [(i, i ^ 1 << bit) for i in range(devices)])  110 us
    ppermute x45, starting transfers between devices, swap(): return lax.ppermute(x, AXES, [(i, i ^ 1 << bit) for i in range(devices)])  49.8 us
    all_to_all x7, starting transfers between devices, to_all(): return lax.all_to_all(copies, AXES, 0, 0)  32.6 us
    all_to_all x7, waiting for transfers between devices, to_all(): return lax.all_to_all(copies, AXES, 0, 0)  29.5 us
    unnamed x95, local copies, waits for them, and re-layouts  29 us
    all_to_all x2, blocking collectives, to_all(): return lax.all_to_all(copies, AXES, 0, 0)  20.4 us
  transfers between devices with their start and end apart: 55, of which 27 were waited for; matrix products, arithmetic and copies ran while one was open for 5% of the time, Pallas kernels for 13%

profile of v5, /device:TPU:0, one launch (start us, length us, event | category | flops | bytes accessed | tf_op | source)
XLA Modules:
  0.0 447.6 jit_solution(3072553904414216834)
XLA Ops:
  10.7 3.0 collective-permute-start
  15.7 4.3 forward_first.1
  21.8 9.5 %all-to-all-start = ((f32[32,3,512]{2,1,0:T(4,128)}), f32[32,3,512]{2,1,0:T(4,128)S(1)}, u32[]{:S(2)}, u32[]{:S(2)}) async-start(f32[32,3,512]{2,1,0:T(4,128)} %get-tuple-element.91), calls=%async_computation | async-start | bytes 524288 | tf_op jit(solution)/shard_map/all_to_all | solution.py:305
  31.3 10.5 %all-to-all-done.refs_2_ = f32[32,3,512]{2,1,0:T(4,128)S(1)} async-done(((f32[32,3,512]{2,1,0:T(4,128)}), f32[32,3,512]{2,1,0:T(4,128)S(1)}, u32[]{:S(2)}, u32[]{:S(2)}) %all-to-all-start) | async-done | bytes 196640 | tf_op jit(solution)/shard_map/all_to_all | solution.py:305
  41.8 10.2 %forward.4 = (f32[608,512]{1,0:T(8,128)S(1)}, f32[32,2,512]{2,1,0:T(2,128)}, f32[608,512]{1,0:T(8,128)S(1)}, f32[3,512]{1,0:T(4,128)S(1)}) custom-call(s32[4]{0:T(128)S(1)} %pad_add_fusion.refs_0_, f32[608,512]{1,0:T(8,128)} %copy-done.11, f32[32,3,512]{2,1,0:T(4,128)S(1)} %all-to-all-done.refs_2_, f32[1,512]{1,0:T(1,128)S(1)} %get-tuple-element.259.refs_3_.refs_5_, ...), custom_call_target="tpu_custom_call" | custom-call | flops 4781506560 | bytes 19802128 | tf_op jit(solution)/shard_map/forward/pallas_call | solution.py:281
  53.1 2.7 all-to-all-start.1
  55.9 8.2 %all-to-all-done.1.refs_2_ = f32[32,2,512]{2,1,0:T(2,128)S(1)} async-done(((f32[32,2,512]{2,1,0:T(2,128)}), f32[32,2,512]{2,1,0:T(2,128)S(1)}, u32[]{:S(2)}, u32[]{:S(2)}) %all-to-all-start.1) | async-done | bytes 131104 | tf_op jit(solution)/shard_map/all_to_all | solution.py:305
  65.4 8.8 %forward.5 = (f32[608,512]{1,0:T(8,128)S(1)}, f32[32,2,512]{2,1,0:T(2,128)S(1)}, f32[608,512]{1,0:T(8,128)S(1)}, f32[3,512]{1,0:T(4,128)S(1)}) custom-call(s32[4]{0:T(128)S(1)} %pad_add_fusion.refs_0_, f32[608,512]{1,0:T(8,128)S(1)} %copy-done.16, f32[32,2,512]{2,1,0:T(2,128)S(1)} %all-to-all-done.1.refs_2_, ...), custom_call_target="tpu_custom_call" | custom-call | flops 4781506560 | bytes 19738640 | tf_op jit(solution)/shard_map/forward/pallas_call | solution.py:281
  75.2 10.1 %all_to_all.45.refs_2_ = f32[32,2,512]{2,1,0:T(2,128)S(1)} all-to-all(f32[32,2,512]{2,1,0:T(2,128)S(1)} %get-tuple-element.96), channel_id=1, replica_groups=mesh['dp'=8,'tm'=4] {'dp','tm'}, dimensions={0} | all-to-all | bytes 262144 | tf_op jit(solution)/shard_map/all_to_all | solution.py:305
  85.3 8.8 %forward.6 = (f32[608,512]{1,0:T(8,128)S(1)}, f32[32,2,512]{2,1,0:T(2,128)S(1)}, f32[608,512]{1,0:T(8,128)S(1)}, f32[3,512]{1,0:T(4,128)S(1)}) custom-call(s32[4]{0:T(128)S(1)} %pad_add_fusion.refs_0_, f32[608,512]{1,0:T(8,128)S(1)} %get-tuple-element.95.refs_1_.refs_8_.refs_2_, f32[32,2,512]{2,1,0:T(2,128)S(1)} %all_to_all.45.refs_2_, ...), custom_call_target="tpu_custom_call" | custom-call | flops 4781506560 | bytes 19738640 | tf_op jit(solution)/shard_map/forward/pallas_call | solution.py:281
  96.2 10.3 %all_to_all.46.refs_2_ = f32[32,2,512]{2,1,0:T(2,128)S(1)} all-to-all(f32[32,2,512]{2,1,0:T(2,128)S(1)} %get-tuple-element.98), channel_id=1, replica_groups=mesh['dp'=8,'tm'=4] {'dp','tm'}, dimensions={0} | all-to-all | bytes 262144 | tf_op jit(solution)/shard_map/all_to_all | solution.py:305
  106.5 9.2 %forward.7 = (f32[608,80]{1,0:T(8,128)S(1)}, f32[32,4,80]{2,1,0:T(4,128)}, f32[608,512]{1,0:T(8,128)S(1)}, f32[3,512]{1,0:T(4,128)S(1)}) custom-call(s32[4]{0:T(128)S(1)} %pad_add_fusion.refs_0_, f32[608,512]{1,0:T(8,128)} %copy-done.7, f32[32,2,512]{2,1,0:T(2,128)S(1)} %all_to_all.46.refs_2_, f32[1,512]{1,0:T(1,128)S(1)} %get-tuple-element.261.refs_3_.refs_5_, ...), custom_call_target="tpu_custom_call" | custom-call | flops 747110400 | bytes 3883024 | tf_op jit(solution)/shard_map/forward/pallas_call | solution.py:281
  119.4 7.4 %all-to-all-done.4.refs_1_ = f32[32,4,80]{2,1,0:T(4,128)S(1)} async-done(((f32[32,4,80]{2,1,0:T(4,128)}), f32[32,4,80]{2,1,0:T(4,128)S(1)}, u32[]{:S(2)}, u32[]{:S(2)}) %all-to-all-start.4) | async-done | bytes 40992 | tf_op jit(solution)/shard_map/all_to_all | solution.py:305
  126.8 5.2 %backward.5 = (f32[608,80]{1,0:T(8,128)S(1)}, f32[2,80]{1,0:T(2,128)S(1)}, f32[2,256,80]{2,1,0:T(8,128)S(1)}, f32[608,512]{1,0:T(8,128)S(1)}, f32[32,2,512]{2,1,0:T(2,128)}) custom-call(s32[4]{0:T(128)S(1)} %pad_add_fusion.refs_0_, f32[32,4,80]{2,1,0:T(4,128)S(1)} %all-to-all-done.4.refs_1_, f32[608,80]{1,0:T(8,128)S(1)} %get-tuple-element.101.refs_2_, ...), custom_call_target="tpu_custom_call" | custom-call | flops 5976883200 | bytes 5651728 | tf_op jit(solution)/shard_map/backward/pallas_call | solution.py:281
  133.1 3.0 all-to-all-start.5
  137.5 3.5 weight_gradient.5
  141.0 3.4 all-to-all-done.5.refs_1_
  144.4 11.5 %backward.6 = (f32[608,512]{1,0:T(8,128)S(1)}, f32[2,512]{1,0:T(2,128)S(1)}, f32[608,512]{1,0:T(8,128)S(1)}, f32[32,2,512]{2,1,0:T(2,128)}) custom-call(s32[4]{0:T(128)S(1)} %pad_add_fusion.refs_0_, f32[32,2,512]{2,1,0:T(2,128)S(1)} %all-to-all-done.5.refs_1_, f32[608,512]{1,0:T(8,128)S(1)} %copy-done.8, f32[608,512]{1,0:T(8,128)} %copy-done.26, ...), custom_call_target="tpu_custom_call" | custom-call | flops 38252052480 | bytes 23480336 | tf_op jit(solution)/shard_map/backward/pallas_call | solution.py:281
  158.0 2.8 all-to-all-start.6
  163.3 7.7 %weight_gradient.6 = f32[5,512,512]{2,1,0:T(8,128)} custom-call(s32[4]{0:T(128)S(1)} %pad_add_fusion.refs_0_, f32[608,512]{1,0:T(8,128)S(1)} %copy-done.23, f32[608,512]{1,0:T(8,128)S(1)} %copy-done.35), custom_call_target="tpu_custom_call" | custom-call | flops 38252052480 | bytes 7733264 | tf_op jit(solution)/shard_map/weight_gradient/pallas_call | solution.py:281
  172.4 11.5 %backward.7 = (f32[608,512]{1,0:T(8,128)S(1)}, f32[2,512]{1,0:T(2,128)S(1)}, f32[608,512]{1,0:T(8,128)S(1)}, f32[32,2,512]{2,1,0:T(2,128)}) custom-call(s32[4]{0:T(128)S(1)} %pad_add_fusion.refs_0_, f32[32,2,512]{2,1,0:T(2,128)S(1)} %all-to-all-done.6.refs_1_, f32[608,512]{1,0:T(8,128)S(1)} %copy-done.21, f32[608,512]{1,0:T(8,128)} %copy-done.31, ...), custom_call_target="tpu_custom_call" | custom-call | flops 38252052480 | bytes 23480336 | tf_op jit(solution)/shard_map/backward/pallas_call | solution.py:281
  186.0 6.0 %all-to-all-start.7 = ((f32[32,2,512]{2,1,0:T(2,128)}), f32[32,2,512]{2,1,0:T(2,128)S(1)}, u32[]{:S(2)}, u32[]{:S(2)}) async-start(f32[32,2,512]{2,1,0:T(2,128)} %get-tuple-element.117), calls=%async_computation.7 | async-start | bytes 262144 | tf_op jit(solution)/shard_map/all_to_all | solution.py:305
  193.8 7.7 %weight_gradient.7 = (f32[5,256,512]{2,1,0:T(8,128)}, f32[5,256,512]{2,1,0:T(8,128)}) custom-call(s32[4]{0:T(128)S(1)} %pad_add_fusion.refs_0_, f32[608,512]{1,0:T(8,128)S(1)} %copy-done.19, f32[608,512]{1,0:T(8,128)S(1)} %copy-done.33), custom_call_target="tpu_custom_call" | custom-call | flops 38252052480 | bytes 7733264 | tf_op jit(solution)/shard_map/weight_gradient/pallas_call | solution.py:281
  202.8 11.5 %backward.8 = (f32[608,512]{1,0:T(8,128)S(1)}, f32[2,512]{1,0:T(2,128)S(1)}, f32[608,512]{1,0:T(8,128)S(1)}, f32[32,2,512]{2,1,0:T(2,128)}) custom-call(s32[4]{0:T(128)S(1)} %pad_add_fusion.refs_0_, f32[32,2,512]{2,1,0:T(2,128)S(1)} %all-to-all-done.7.refs_1_, f32[608,512]{1,0:T(8,128)S(1)} %copy-done.17, f32[608,512]{1,0:T(8,128)} %copy-done.28, ...), custom_call_target="tpu_custom_call" | custom-call | flops 38252052480 | bytes 23480336 | tf_op jit(solution)/shard_map/backward/pallas_call | solution.py:281
  216.4 6.0 %all-to-all-start.8 = ((f32[32,2,512]{2,1,0:T(2,128)}), f32[32,2,512]{2,1,0:T(2,128)S(1)}, u32[]{:S(2)}, u32[]{:S(2)}) async-start(f32[32,2,512]{2,1,0:T(2,128)} %get-tuple-element.124), calls=%async_computation.8 | async-start | bytes 262144 | tf_op jit(solution)/shard_map/all_to_all | solution.py:305
  222.4 3.3 add.55
  233.3 7.8 %weight_gradient.8 = (f32[5,256,512]{2,1,0:T(8,128)}, f32[5,256,512]{2,1,0:T(8,128)}) custom-call(s32[4]{0:T(128)S(1)} %pad_add_fusion.refs_0_, f32[608,512]{1,0:T(8,128)S(1)} %copy-done.14, f32[608,512]{1,0:T(8,128)S(1)} %copy-done.30), custom_call_target="tpu_custom_call" | custom-call | flops 38252052480 | bytes 7733264 | tf_op jit(solution)/shard_map/weight_gradient/pallas_call | solution.py:281
  241.2 6.3 %collective-permute-done.5 = f32[192,512]{1,0:T(8,128)} collective-permute-done((f32[192,512]{1,0:T(8,128)}, f32[192,512]{1,0:T(8,128)}, u32[]{:S(2)}, u32[]{:S(2)}) %collective-permute-start.5) | collective-permute-done | bytes 393248 | tf_op jit(solution)/shard_map/ppermute | solution.py:310
  255.1 9.1 %backward.9 = (f32[608,512]{1,0:T(8,128)S(1)}, f32[2,512]{1,0:T(2,128)S(1)}, f32[2,256,80]{2,1,0:T(8,128)S(1)}) custom-call(s32[4]{0:T(128)S(1)} %pad_add_fusion.refs_0_, f32[32,2,512]{2,1,0:T(2,128)S(1)} %all-to-all-done.8.refs_1_, f32[608,512]{1,0:T(8,128)S(1)} %copy-done.12, f32[608,512]{1,0:T(8,128)} %copy-done.27, f32[3,512]{1,0:T(4,128)S(1)} %copy-done.1, ...), custom_call_target="tpu_custom_call" | custom-call | flops 5976883200 | bytes 5025808 | tf_op jit(solution)/shard_map/backward/pallas_call | solution.py:281
  267.1 2.6 weight_gradient.9
  276.6 9.9 %collective-permute-done.17 = f32[256,512]{1,0:T(8,128)S(1)} collective-permute-done((f32[256,512]{1,0:T(8,128)S(1)}, f32[256,512]{1,0:T(8,128)S(1)}, u32[]{:S(2)}, u32[]{:S(2)}) %collective-permute-start.17) | collective-permute-done | bytes 524320 | tf_op jit(solution)/shard_map/ppermute | solution.py:310
  292.1 5.1 %collective-permute-done.18 = f32[128,512]{1,0:T(8,128)S(1)} collective-permute-done((f32[128,512]{1,0:T(8,128)S(1)}, f32[128,512]{1,0:T(8,128)S(1)}, u32[]{:S(2)}, u32[]{:S(2)}) %collective-permute-start.18) | collective-permute-done | bytes 262176 | tf_op jit(solution)/shard_map/ppermute | solution.py:310
  299.3 13.9 %collective-permute-done.14 = f32[256,512]{1,0:T(8,128)S(1)} collective-permute-done((f32[256,512]{1,0:T(8,128)S(1)}, f32[256,512]{1,0:T(8,128)S(1)}, u32[]{:S(2)}, u32[]{:S(2)}) %collective-permute-start.14) | collective-permute-done | bytes 524320 | tf_op jit(solution)/shard_map/ppermute | solution.py:310
  315.6 4.2 collective-permute-done.15
  325.3 11.8 %collective-permute-done.36 = f32[80,512]{1,0:T(8,128)S(1)} collective-permute-done((f32[80,512]{1,0:T(8,128)S(1)}, f32[80,512]{1,0:T(8,128)S(1)}, u32[]{:S(2)}, u32[]{:S(2)}) %collective-permute-start.36) | collective-permute-done | bytes 163872 | tf_op jit(solution)/shard_map/ppermute | solution.py:310
  340.0 2.9 collective-permute-start.37
  343.0 10.1 %collective-permute-done.20 = f32[96,512]{1,0:T(8,128)S(1)} collective-permute-done((f32[96,512]{1,0:T(8,128)S(1)}, f32[96,512]{1,0:T(8,128)S(1)}, u32[]{:S(2)}, u32[]{:S(2)}) %collective-permute-start.20) | collective-permute-done | bytes 196640 | tf_op jit(solution)/shard_map/ppermute | solution.py:310
  358.6 7.6 %collective-permute-done.21 = f32[96,512]{1,0:T(8,128)S(1)} collective-permute-done((f32[96,512]{1,0:T(8,128)S(1)}, f32[96,512]{1,0:T(8,128)S(1)}, u32[]{:S(2)}, u32[]{:S(2)}) %collective-permute-start.21) | collective-permute-done | bytes 196640 | tf_op jit(solution)/shard_map/ppermute | solution.py:310
  372.8 3.6 collective-permute-start.44
  378.7 12.4 %collective-permute-done.25 = f32[64,512]{1,0:T(8,128)S(1)} collective-permute-done((f32[64,512]{1,0:T(8,128)S(1)}, f32[64,512]{1,0:T(8,128)S(1)}, u32[]{:S(2)}, u32[]{:S(2)}) %collective-permute-start.25) | collective-permute-done | bytes 131104 | tf_op jit(solution)/shard_map/ppermute | solution.py:310
  391.1 4.2 collective-permute-done.29
  395.6 4.7 %collective-permute-done.23 = f32[128,512]{1,0:T(8,128)S(1)} collective-permute-done((f32[128,512]{1,0:T(8,128)S(1)}, f32[128,512]{1,0:T(8,128)S(1)}, u32[]{:S(2)}, u32[]{:S(2)}) %collective-permute-start.23) | collective-permute-done | bytes 262176 | tf_op jit(solution)/shard_map/ppermute | solution.py:310
  400.7 4.4 collective-permute-done.26
  405.9 3.7 collective-permute-done.24
  411.4 3.1 collective-permute-done.27
  420.5 4.9 %place_whole.1.refs_3_ = f32[3,5,512,512]{3,2,1,0:T(8,128)} custom-call(f32[5,512,512]{2,1,0:T(8,128)} %get-tuple-element.180.refs_0_), custom_call_target="tpu_custom_call" | custom-call | tf_op jit(solution)/shard_map/place_whole/pallas_call | solution.py:281
  428.0 4.2 place.2.refs_3_
  434.3 5.3 %place.3 = f32[3,5,512,512]{3,2,1,0:T(8,128)} custom-call(s32[4]{0:T(128)S(1)} %pad_add_fusion.refs_0_, f32[1536,512]{1,0:T(8,128)} %get-tuple-element.182.refs_1_, f32[1536,512]{1,0:T(8,128)} %collective-permute-done.31.refs_2_, f32[3,5,512,512]{3,2,1,0:T(8,128)} %place.2.refs_3_), custom_call_target="tpu_custom_call", output_to_operand_aliasing={{}: (3, {})} | custom-call | tf_op jit(solution)/shard_map/place/pallas_call | solution.py:281
  (277 shorter events, 104.2 us)
Async XLA Ops:
  21.8 20.0 %all-to-all-start = ((f32[32,3,512]{2,1,0:T(4,128)}), f32[32,3,512]{2,1,0:T(4,128)S(1)}, u32[]{:S(2)}, u32[]{:S(2)}) async-start(f32[32,3,512]{2,1,0:T(4,128)} %get-tuple-element.91), calls=%async_computation | async-start | bytes 524288 | tf_op jit(solution)/shard_map/all_to_all | solution.py:305
  53.1 10.9 %all-to-all-start.1 = ((f32[32,2,512]{2,1,0:T(2,128)}), f32[32,2,512]{2,1,0:T(2,128)S(1)}, u32[]{:S(2)}, u32[]{:S(2)}) async-start(f32[32,2,512]{2,1,0:T(2,128)} %get-tuple-element.93), calls=%async_computation.1 | async-start | bytes 262144 | tf_op jit(solution)/shard_map/all_to_all | solution.py:305
  116.8 10.0 %all-to-all-start.4 = ((f32[32,4,80]{2,1,0:T(4,128)}), f32[32,4,80]{2,1,0:T(4,128)S(1)}, u32[]{:S(2)}, u32[]{:S(2)}) async-start(f32[32,4,80]{2,1,0:T(4,128)} %get-tuple-element.100), calls=%async_computation.4 | async-start | bytes 131072 | tf_op jit(solution)/shard_map/all_to_all | solution.py:305
  133.1 11.2 %all-to-all-start.5 = ((f32[32,2,512]{2,1,0:T(2,128)}), f32[32,2,512]{2,1,0:T(2,128)S(1)}, u32[]{:S(2)}, u32[]{:S(2)}) async-start(f32[32,2,512]{2,1,0:T(2,128)} %get-tuple-element.105), calls=%async_computation.5 | async-start | bytes 262144 | tf_op jit(solution)/shard_map/all_to_all | solution.py:305
  158.0 13.1 %all-to-all-start.6 = ((f32[32,2,512]{2,1,0:T(2,128)}), f32[32,2,512]{2,1,0:T(2,128)S(1)}, u32[]{:S(2)}, u32[]{:S(2)}) async-start(f32[32,2,512]{2,1,0:T(2,128)} %get-tuple-element.111), calls=%async_computation.6 | async-start | bytes 262144 | tf_op jit(solution)/shard_map/all_to_all | solution.py:305
  186.0 15.5 %all-to-all-start.7 = ((f32[32,2,512]{2,1,0:T(2,128)}), f32[32,2,512]{2,1,0:T(2,128)S(1)}, u32[]{:S(2)}, u32[]{:S(2)}) async-start(f32[32,2,512]{2,1,0:T(2,128)} %get-tuple-element.117), calls=%async_computation.7 | async-start | bytes 262144 | tf_op jit(solution)/shard_map/all_to_all | solution.py:305
  192.0 228.5 %all-reduce.4.cloned.1.call-start = ((), (), s32[]{:S(2)}) async-start(), calls=%async_computation.9 | async-start | bytes 12124160 | tf_op jit(solution)/shard_map/psum | solution.py:497
  201.5 20.9 %collective-permute-start.2 = (f32[1280,512]{1,0:T(8,128)}, f32[1280,512]{1,0:T(8,128)}, u32[]{:S(2)}, u32[]{:S(2)}) collective-permute-start(f32[1280,512]{1,0:T(8,128)} %bitcast.37), channel_id=1, source_target_pairs={{0,1},{1,0},{2,3},{3,2},{4,5},{5,4},{6,7},{7,6},{8,9},{9,8},{10,11... | collective-permute-start | bytes 7864328 | tf_op jit(solution)/shard_map/ppermute | solution.py:310
  216.4 24.7 %all-to-all-start.8 = ((f32[32,2,512]{2,1,0:T(2,128)}), f32[32,2,512]{2,1,0:T(2,128)S(1)}, u32[]{:S(2)}, u32[]{:S(2)}) async-start(f32[32,2,512]{2,1,0:T(2,128)} %get-tuple-element.124), calls=%async_computation.8 | async-start | bytes 262144 | tf_op jit(solution)/shard_map/all_to_all | solution.py:305
  226.7 20.7 %collective-permute-start.5 = (f32[192,512]{1,0:T(8,128)}, f32[192,512]{1,0:T(8,128)}, u32[]{:S(2)}, u32[]{:S(2)}) collective-permute-start(f32[192,512]{1,0:T(8,128)} %slice_select_fusion.5), channel_id=1, source_target_pairs={{0,8},{1,9},{2,10},{3,11},{4,12},{5,13},{6,14},{7,15},{8,0},{9,1},... | collective-permute-start | bytes 1179656 | tf_op jit(solution)/shard_map/ppermute | solution.py:310
  229.4 19.4 %collective-permute-start.4 = (f32[192,512]{1,0:T(8,128)}, f32[192,512]{1,0:T(8,128)}, u32[]{:S(2)}, u32[]{:S(2)}) collective-permute-start(f32[192,512]{1,0:T(8,128)} %slice_select_fusion.6), channel_id=1, source_target_pairs={{0,4},{1,5},{2,6},{3,7},{4,0},{5,1},{6,2},{7,3},{8,12},{9,13},{10,... | collective-permute-start | bytes 1179656 | tf_op jit(solution)/shard_map/ppermute | solution.py:310
  231.8 18.3 %collective-permute-start.3 = (f32[256,512]{1,0:T(8,128)}, f32[256,512]{1,0:T(8,128)S(1)}, u32[]{:S(2)}, u32[]{:S(2)}) collective-permute-start(f32[256,512]{1,0:T(8,128)} %slice_select_fusion.2), channel_id=1, source_target_pairs={{0,2},{1,3},{2,0},{3,1},{4,6},{5,7},{6,4},{7,5},{8,10},{9,11},{10,... | collective-permute-start | bytes 1572872 | tf_op jit(solution)/shard_map/ppermute | solution.py:310
  241.1 29.5 %collective-permute-start.6 = (f32[1280,512]{1,0:T(8,128)}, f32[1280,512]{1,0:T(8,128)S(1)}, u32[]{:S(2)}, u32[]{:S(2)}) collective-permute-start(f32[1280,512]{1,0:T(8,128)} %bitcast.36), channel_id=1, source_target_pairs={{0,1},{1,0},{2,3},{3,2},{4,5},{5,4},{6,7},{7,6},{8,9},{9,8},{10,11... | collective-permute-start | bytes 7864328 | tf_op jit(solution)/shard_map/ppermute | solution.py:310
  250.3 13.9 %collective-permute-start.12 = (f32[96,512]{1,0:T(8,128)S(1)}, f32[96,512]{1,0:T(8,128)S(1)}, u32[]{:S(2)}, u32[]{:S(2)}) collective-permute-start(f32[96,512]{1,0:T(8,128)S(1)} %slice_select_fusion.11), channel_id=1, source_target_pairs={{0,2},{1,3},{2,0},{3,1},{4,6},{5,7},{6,4},{7,5},{8,10},{9,11},{10,... | collective-permute-start | bytes 589832 | tf_op jit(solution)/shard_map/ppermute | solution.py:310
  252.2 12.1 %collective-permute-start.11 = (f32[96,512]{1,0:T(8,128)S(1)}, f32[96,512]{1,0:T(8,128)S(1)}, u32[]{:S(2)}, u32[]{:S(2)}) collective-permute-start(f32[96,512]{1,0:T(8,128)S(1)} %slice_select_fusion.12), channel_id=1, source_target_pairs={{0,8},{1,9},{2,10},{3,11},{4,12},{5,13},{6,14},{7,15},{8,0},{9,1},... | collective-permute-start | bytes 589832 | tf_op jit(solution)/shard_map/ppermute | solution.py:310
  253.6 10.8 %collective-permute-start.10 = (f32[128,512]{1,0:T(8,128)S(1)}, f32[128,512]{1,0:T(8,128)S(1)}, u32[]{:S(2)}, u32[]{:S(2)}) collective-permute-start(f32[128,512]{1,0:T(8,128)S(1)} %slice_select_fusion.10), channel_id=1, source_target_pairs={{0,4},{1,5},{2,6},{3,7},{4,0},{5,1},{6,2},{7,3},{8,12},{9,13},{10,... | collective-permute-start | bytes 786440 | tf_op jit(solution)/shard_map/ppermute | solution.py:310
  264.4 10.3 %collective-permute-start.34 = (f32[64,512]{1,0:T(8,128)S(1)}, f32[64,512]{1,0:T(8,128)S(1)}, u32[]{:S(2)}, u32[]{:S(2)}) collective-permute-start(f32[64,512]{1,0:T(8,128)S(1)} %slice_select_fusion.16), channel_id=1, source_target_pairs={{0,8},{1,9},{2,10},{3,11},{4,12},{5,13},{6,14},{7,15},{8,0},{9,1},... | collective-permute-start | bytes 393224 | tf_op jit(solution)/shard_map/ppermute | solution.py:310
  269.8 6.8 %collective-permute-start.13 = (f32[200,512]{1,0:T(8,128)S(1)}, f32[200,512]{1,0:T(8,128)S(1)}, u32[]{:S(2)}, u32[]{:S(2)}) collective-permute-start(f32[200,512]{1,0:T(8,128)S(1)} %bitcast.29), channel_id=1, source_target_pairs={{0,1},{1,0},{2,3},{3,2},{4,5},{5,4},{6,7},{7,6},{8,9},{9,8},{10,11... | collective-permute-start | bytes 1228808 | tf_op jit(solution)/shard_map/ppermute | solution.py:310
  271.4 15.1 %collective-permute-start.17 = (f32[256,512]{1,0:T(8,128)S(1)}, f32[256,512]{1,0:T(8,128)S(1)}, u32[]{:S(2)}, u32[]{:S(2)}) collective-permute-start(f32[256,512]{1,0:T(8,128)S(1)} %get-tuple-element.189), channel_id=1, source_target_pairs={{0,2},{1,3},{2,0},{3,1},{4,6},{5,7},{6,4},{7,5},{8,10},{9,11},{10,... | collective-permute-start | bytes 1572872 | tf_op jit(solution)/shard_map/ppermute | solution.py:310
  273.0 16.0 %collective-permute-start.7 = (f32[256,512]{1,0:T(8,128)S(1)}, f32[256,512]{1,0:T(8,128)S(1)}, u32[]{:S(2)}, u32[]{:S(2)}) collective-permute-start(f32[256,512]{1,0:T(8,128)S(1)} %get-tuple-element.190), channel_id=1, source_target_pairs={{0,4},{1,5},{2,6},{3,7},{4,0},{5,1},{6,2},{7,3},{8,12},{9,13},{10,... | collective-permute-start | bytes 1572872 | tf_op jit(solution)/shard_map/ppermute | solution.py:310
  274.8 15.2 %collective-permute-start.35 = (f32[80,512]{1,0:T(8,128)S(1)}, f32[80,512]{1,0:T(8,128)S(1)}, u32[]{:S(2)}, u32[]{:S(2)}) collective-permute-start(f32[80,512]{1,0:T(8,128)S(1)} %fusion.3), channel_id=1, source_target_pairs={{0,16},{1,17},{2,18},{3,19},{4,20},{5,21},{6,22},{7,23},{8,24},{9,... | collective-permute-start | bytes 491528 | tf_op jit(solution)/shard_map/ppermute | solution.py:310
  289.6 7.6 %collective-permute-start.18 = (f32[128,512]{1,0:T(8,128)S(1)}, f32[128,512]{1,0:T(8,128)S(1)}, u32[]{:S(2)}, u32[]{:S(2)}) collective-permute-start(f32[128,512]{1,0:T(8,128)S(1)} %slice_select_fusion.7), channel_id=1, source_target_pairs={{0,4},{1,5},{2,6},{3,7},{4,0},{5,1},{6,2},{7,3},{8,12},{9,13},{10,... | collective-permute-start | bytes 786440 | tf_op jit(solution)/shard_map/ppermute | solution.py:310
  290.0 9.2 %collective-permute-start.8 = (f32[128,512]{1,0:T(8,128)S(1)}, f32[128,512]{1,0:T(8,128)S(1)}, u32[]{:S(2)}, u32[]{:S(2)}) collective-permute-start(f32[128,512]{1,0:T(8,128)S(1)} %slice_select_fusion.9), channel_id=1, source_target_pairs={{0,8},{1,9},{2,10},{3,11},{4,12},{5,13},{6,14},{7,15},{8,0},{9,1},... | collective-permute-start | bytes 786440 | tf_op jit(solution)/shard_map/ppermute | solution.py:310
  291.4 21.8 %collective-permute-start.14 = (f32[256,512]{1,0:T(8,128)S(1)}, f32[256,512]{1,0:T(8,128)S(1)}, u32[]{:S(2)}, u32[]{:S(2)}) collective-permute-start(f32[256,512]{1,0:T(8,128)S(1)} %get-tuple-element.187), channel_id=1, source_target_pairs={{0,8},{1,9},{2,10},{3,11},{4,12},{5,13},{6,14},{7,15},{8,0},{9,1},... | collective-permute-start | bytes 1572872 | tf_op jit(solution)/shard_map/ppermute | solution.py:310
  297.3 18.3 %collective-permute-start.19 = (f32[64,512]{1,0:T(8,128)S(1)}, f32[64,512]{1,0:T(8,128)S(1)}, u32[]{:S(2)}, u32[]{:S(2)}) collective-permute-start(f32[64,512]{1,0:T(8,128)S(1)} %slice_select_fusion.13), channel_id=1, source_target_pairs={{0,8},{1,9},{2,10},{3,11},{4,12},{5,13},{6,14},{7,15},{8,0},{9,1},... | collective-permute-start | bytes 393224 | tf_op jit(solution)/shard_map/ppermute | solution.py:310
  313.4 6.4 %collective-permute-start.15 = (f32[128,512]{1,0:T(8,128)S(1)}, f32[128,512]{1,0:T(8,128)S(1)}, u32[]{:S(2)}, u32[]{:S(2)}) collective-permute-start(f32[128,512]{1,0:T(8,128)S(1)} %slice_select_fusion.8), channel_id=1, source_target_pairs={{0,2},{1,3},{2,0},{3,1},{4,6},{5,7},{6,4},{7,5},{8,10},{9,11},{10,... | collective-permute-start | bytes 786440 | tf_op jit(solution)/shard_map/ppermute | solution.py:310
  313.9 9.7 %collective-permute-start.9 = (f32[64,512]{1,0:T(8,128)S(1)}, f32[64,512]{1,0:T(8,128)S(1)}, u32[]{:S(2)}, u32[]{:S(2)}) collective-permute-start(f32[64,512]{1,0:T(8,128)S(1)} %slice_select_fusion.15), channel_id=1, source_target_pairs={{0,2},{1,3},{2,0},{3,1},{4,6},{5,7},{6,4},{7,5},{8,10},{9,11},{10,... | collective-permute-start | bytes 393224 | tf_op jit(solution)/shard_map/ppermute | solution.py:310
  323.7 13.5 %collective-permute-start.36 = (f32[80,512]{1,0:T(8,128)S(1)}, f32[80,512]{1,0:T(8,128)S(1)}, u32[]{:S(2)}, u32[]{:S(2)}) collective-permute-start(f32[80,512]{1,0:T(8,128)S(1)} %select_add_fusion.12), channel_id=1, source_target_pairs={{0,16},{1,17},{2,18},{3,19},{4,20},{5,21},{6,22},{7,23},{8,24},{9,... | collective-permute-start | bytes 491528 | tf_op jit(solution)/shard_map/ppermute | solution.py:310
  339.9 13.2 %collective-permute-start.20 = (f32[96,512]{1,0:T(8,128)S(1)}, f32[96,512]{1,0:T(8,128)S(1)}, u32[]{:S(2)}, u32[]{:S(2)}) collective-permute-start(f32[96,512]{1,0:T(8,128)S(1)} %fusion.2), channel_id=1, source_target_pairs={{0,16},{1,17},{2,18},{3,19},{4,20},{5,21},{6,22},{7,23},{8,24},{9,... | collective-permute-start | bytes 589832 | tf_op jit(solution)/shard_map/ppermute | solution.py:310
  340.0 13.2 %collective-permute-start.37 = (f32[64,512]{1,0:T(8,128)S(1)}, f32[64,512]{1,0:T(8,128)S(1)}, u32[]{:S(2)}, u32[]{:S(2)}) collective-permute-start(f32[64,512]{1,0:T(8,128)S(1)} %slice.289), channel_id=1, source_target_pairs={{0,8},{1,9},{2,10},{3,11},{4,12},{5,13},{6,14},{7,15},{8,0},{9,1},... | collective-permute-start | bytes 393224 | tf_op jit(solution)/shard_map/ppermute | solution.py:310
  353.1 13.0 %collective-permute-start.21 = (f32[96,512]{1,0:T(8,128)S(1)}, f32[96,512]{1,0:T(8,128)S(1)}, u32[]{:S(2)}, u32[]{:S(2)}) collective-permute-start(f32[96,512]{1,0:T(8,128)S(1)} %select_add_fusion.9), channel_id=1, source_target_pairs={{0,16},{1,17},{2,18},{3,19},{4,20},{5,21},{6,22},{7,23},{8,24},{9,... | collective-permute-start | bytes 589832 | tf_op jit(solution)/shard_map/ppermute | solution.py:310
  353.3 15.5 %collective-permute-start.42 = (f32[96,512]{1,0:T(8,128)S(1)}, f32[96,512]{1,0:T(8,128)S(1)}, u32[]{:S(2)}, u32[]{:S(2)}) collective-permute-start(f32[96,512]{1,0:T(8,128)S(1)} %pad_maximum_fusion.19), channel_id=1, source_target_pairs={{0,2},{1,3},{2,0},{3,1},{4,6},{5,7},{6,4},{7,5},{8,10},{9,11},{10,... | collective-permute-start | bytes 589832 | tf_op jit(solution)/shard_map/ppermute | solution.py:310
  355.3 14.8 %collective-permute-start.41 = (f32[96,512]{1,0:T(8,128)S(1)}, f32[96,512]{1,0:T(8,128)S(1)}, u32[]{:S(2)}, u32[]{:S(2)}) collective-permute-start(f32[96,512]{1,0:T(8,128)S(1)} %pad_maximum_fusion.18), channel_id=1, source_target_pairs={{0,8},{1,9},{2,10},{3,11},{4,12},{5,13},{6,14},{7,15},{8,0},{9,1},... | collective-permute-start | bytes 589832 | tf_op jit(solution)/shard_map/ppermute | solution.py:310
  357.8 12.4 %collective-permute-start.40 = (f32[128,512]{1,0:T(8,128)S(1)}, f32[128,512]{1,0:T(8,128)S(1)}, u32[]{:S(2)}, u32[]{:S(2)}) collective-permute-start(f32[128,512]{1,0:T(8,128)S(1)} %pad_maximum_fusion.15), channel_id=1, source_target_pairs={{0,4},{1,5},{2,6},{3,7},{4,0},{5,1},{6,2},{7,3},{8,12},{9,13},{10,... | collective-permute-start | bytes 786440 | tf_op jit(solution)/shard_map/ppermute | solution.py:310
  366.2 10.2 %collective-permute-start.22 = (f32[64,512]{1,0:T(8,128)S(1)}, f32[64,512]{1,0:T(8,128)S(1)}, u32[]{:S(2)}, u32[]{:S(2)}) collective-permute-start(f32[64,512]{1,0:T(8,128)S(1)} %slice.326), channel_id=1, source_target_pairs={{0,8},{1,9},{2,10},{3,11},{4,12},{5,13},{6,14},{7,15},{8,0},{9,1},... | collective-permute-start | bytes 393224 | tf_op jit(solution)/shard_map/ppermute | solution.py:310
  366.3 10.1 %collective-permute-start.28 = (f32[64,512]{1,0:T(8,128)S(1)}, f32[64,512]{1,0:T(8,128)S(1)}, u32[]{:S(2)}, u32[]{:S(2)}) collective-permute-start(f32[64,512]{1,0:T(8,128)S(1)} %slice.329), channel_id=1, source_target_pairs={{0,4},{1,5},{2,6},{3,7},{4,0},{5,1},{6,2},{7,3},{8,12},{9,13},{10,... | collective-permute-start | bytes 393224 | tf_op jit(solution)/shard_map/ppermute | solution.py:310
  370.3 30.1 %collective-permute-start.45 = (f32[192,512]{1,0:T(8,128)S(1)}, f32[192,512]{1,0:T(8,128)S(1)}, u32[]{:S(2)}, u32[]{:S(2)}) collective-permute-start(f32[192,512]{1,0:T(8,128)S(1)} %pad_maximum_fusion.10), channel_id=1, source_target_pairs={{0,8},{1,9},{2,10},{3,11},{4,12},{5,13},{6,14},{7,15},{8,0},{9,1},... | collective-permute-start | bytes 1179656 | tf_op jit(solution)/shard_map/ppermute | solution.py:310
  372.8 27.7 %collective-permute-start.44 = (f32[192,512]{1,0:T(8,128)S(1)}, f32[192,512]{1,0:T(8,128)S(1)}, u32[]{:S(2)}, u32[]{:S(2)}) collective-permute-start(f32[192,512]{1,0:T(8,128)S(1)} %pad_maximum_fusion.9), channel_id=1, source_target_pairs={{0,4},{1,5},{2,6},{3,7},{4,0},{5,1},{6,2},{7,3},{8,12},{9,13},{10,... | collective-permute-start | bytes 1179656 | tf_op jit(solution)/shard_map/ppermute | solution.py:310
  376.4 29.4 %collective-permute-start.43 = (f32[256,512]{1,0:T(8,128)S(1)}, f32[256,512]{1,0:T(8,128)S(1)}, u32[]{:S(2)}, u32[]{:S(2)}) collective-permute-start(f32[256,512]{1,0:T(8,128)S(1)} %pad_maximum_fusion.7), channel_id=1, source_target_pairs={{0,2},{1,3},{2,0},{3,1},{4,6},{5,7},{6,4},{7,5},{8,10},{9,11},{10,... | collective-permute-start | bytes 1572872 | tf_op jit(solution)/shard_map/ppermute | solution.py:310
  376.4 14.6 %collective-permute-start.25 = (f32[64,512]{1,0:T(8,128)S(1)}, f32[64,512]{1,0:T(8,128)S(1)}, u32[]{:S(2)}, u32[]{:S(2)}) collective-permute-start(f32[64,512]{1,0:T(8,128)S(1)} %get-tuple-element.235), channel_id=1, source_target_pairs={{0,2},{1,3},{2,0},{3,1},{4,6},{5,7},{6,4},{7,5},{8,10},{9,11},{10,... | collective-permute-start | bytes 393224 | tf_op jit(solution)/shard_map/ppermute | solution.py:310
  378.6 16.8 %collective-permute-start.29 = (f32[128,512]{1,0:T(8,128)S(1)}, f32[128,512]{1,0:T(8,128)S(1)}, u32[]{:S(2)}, u32[]{:S(2)}) collective-permute-start(f32[128,512]{1,0:T(8,128)S(1)} %pad_maximum_fusion.14), channel_id=1, source_target_pairs={{0,2},{1,3},{2,0},{3,1},{4,6},{5,7},{6,4},{7,5},{8,10},{9,11},{10,... | collective-permute-start | bytes 786440 | tf_op jit(solution)/shard_map/ppermute | solution.py:310
  391.1 9.2 %collective-permute-start.23 = (f32[128,512]{1,0:T(8,128)S(1)}, f32[128,512]{1,0:T(8,128)S(1)}, u32[]{:S(2)}, u32[]{:S(2)}) collective-permute-start(f32[128,512]{1,0:T(8,128)S(1)} %pad_maximum_fusion.12), channel_id=1, source_target_pairs={{0,4},{1,5},{2,6},{3,7},{4,0},{5,1},{6,2},{7,3},{8,12},{9,13},{10,... | collective-permute-start | bytes 786440 | tf_op jit(solution)/shard_map/ppermute | solution.py:310
  395.4 9.8 %collective-permute-start.26 = (f32[128,512]{1,0:T(8,128)S(1)}, f32[128,512]{1,0:T(8,128)S(1)}, u32[]{:S(2)}, u32[]{:S(2)}) collective-permute-start(f32[128,512]{1,0:T(8,128)S(1)} %pad_maximum_fusion.13), channel_id=1, source_target_pairs={{0,8},{1,9},{2,10},{3,11},{4,12},{5,13},{6,14},{7,15},{8,0},{9,1},... | collective-permute-start | bytes 786440 | tf_op jit(solution)/shard_map/ppermute | solution.py:310
  400.3 16.0 %collective-permute-start.30 = (f32[256,512]{1,0:T(8,128)S(1)}, f32[256,512]{1,0:T(8,128)S(1)}, u32[]{:S(2)}, u32[]{:S(2)}) collective-permute-start(f32[256,512]{1,0:T(8,128)S(1)} %pad_maximum_fusion.6), channel_id=1, source_target_pairs={{0,8},{1,9},{2,10},{3,11},{4,12},{5,13},{6,14},{7,15},{8,0},{9,1},... | collective-permute-start | bytes 1572872 | tf_op jit(solution)/shard_map/ppermute | solution.py:310
  400.4 9.2 %collective-permute-start.24 = (f32[256,512]{1,0:T(8,128)S(1)}, f32[256,512]{1,0:T(8,128)S(1)}, u32[]{:S(2)}, u32[]{:S(2)}) collective-permute-start(f32[256,512]{1,0:T(8,128)S(1)} %pad_maximum_fusion.4), channel_id=1, source_target_pairs={{0,2},{1,3},{2,0},{3,1},{4,6},{5,7},{6,4},{7,5},{8,10},{9,11},{10,... | collective-permute-start | bytes 1572872 | tf_op jit(solution)/shard_map/ppermute | solution.py:310
  405.2 9.2 %collective-permute-start.27 = (f32[256,512]{1,0:T(8,128)S(1)}, f32[256,512]{1,0:T(8,128)S(1)}, u32[]{:S(2)}, u32[]{:S(2)}) collective-permute-start(f32[256,512]{1,0:T(8,128)S(1)} %pad_maximum_fusion.5), channel_id=1, source_target_pairs={{0,4},{1,5},{2,6},{3,7},{4,0},{5,1},{6,2},{7,3},{8,12},{9,13},{10,... | collective-permute-start | bytes 1572872 | tf_op jit(solution)/shard_map/ppermute | solution.py:310
  418.3 13.9 %collective-permute-start.31 = (f32[1536,512]{1,0:T(8,128)}, f32[1536,512]{1,0:T(8,128)}, u32[]{:S(2)}, u32[]{:S(2)}) collective-permute-start(f32[1536,512]{1,0:T(8,128)} %get-tuple-element.182.refs_1_), channel_id=1, source_target_pairs={{0,1},{1,0},{2,3},{3,2},{4,5},{5,4},{6,7},{7,6},{8,9},{9,8},{10,11... | collective-permute-start | bytes 9437192 | tf_op jit(solution)/shard_map/ppermute | solution.py:310
  418.5 9.5 %collective-permute-start.46 = (f32[1280,512]{1,0:T(8,128)S(1)}, f32[1280,512]{1,0:T(8,128)}, u32[]{:S(2)}, u32[]{:S(2)}) collective-permute-start(f32[1280,512]{1,0:T(8,128)S(1)} %constant_dynamic-update-slice_fusion.1.refs_1_), channel_id=1, source_target_pairs={{0,1},{1,0},{2,3},{3,2},{4,5},{5,4},{6,7},{7,6},{8,9},{9,8},{10,11... | collective-permute-start | bytes 7864328 | tf_op jit(solution)/shard_map/ppermute | solution.py:310
  (51 other events, 478.1 us)
Sparse Core Ops, SparseCore 0:
  201.7 199.6 all-reduce.3
